TPU v7x, 32 devices: a whole 2x2x4 slice. The times are simulated.
32 devices in a mesh: group: 2 (over x), chan: 8 (over z, y), tm: 2 (over core).
Axes of the slice: x: 2, y: 2, z: 4, core: 2. Of those that a mesh axis runs over, the one named last changes fastest.
Arguments:
- signal: float32 [1664, 16384], P(('group', 'chan'), 'tm'), parts along dimension 0, may hold values from -56 to 56
- valid_flags: int32 [1664, 16], P(('group', 'chan'), 'tm'), parts along dimension 0, may hold values 0 or 1
Outputs:
- correlations: bfloat16 [2, 104, 1664, 512], P(None, 'tm', ('group', 'chan')), parts along dimension 2
There are 2 independent parts, one for each index of `group`. A program takes and returns all parts, laid end to end along the dimension named above; each array names one. Nothing has to cross between parts.
All inputs are finite; a program needn't handle non-finite values. No bound on the sum of `valid_flags` on one device may be relied on, other than what follows from the above.
Results may differ from a plain program's by a relative error of at most 0.009.
Values may be sent and summed in bfloat16 or wider, within the bound.
No kernel may reach another device: no remote copies, remote signals or barrier semaphores. Data moves between devices by JAX's collectives and lax.ppermute only.
A program may use at most 192 MiB of HBM per device.

v0:
```python
import functools

import jax
import jax.numpy as jnp
import numpy as np
from jax import lax
from jax.experimental import pallas as pl
from jax.experimental.pallas import tpu as pltpu
from jax.sharding import PartitionSpec as P

WINDOW = 1024
LAGS = 512
ROUNDS = 2

epsilon = 1e-06

BINS = WINDOW // 2
HALF = BINS // 2
LANES = 128
GROUP = 8
OCTETS = BINS // GROUP
STEPS = OCTETS // 4
ROWS_PER_CHUNK = (20, 20, 12)

f32 = jnp.float32
bf16 = jnp.bfloat16


def frequency_order():
    order = np.zeros((OCTETS, GROUP), np.int64)
    for m in range(STEPS):
        for j in range(4):
            base = 16 * m + 8 * (j % 2) + np.arange(GROUP)
            order[4 * m + j] = base if j < 2 else np.where(base == 0, HALF, BINS - base)
    return order


def forward_rows():
    order = frequency_order()
    sample = np.arange(WINDOW)
    phases = 2.0 * np.pi / WINDOW * (order[:, :, None] * sample[None, None, :] % WINDOW)
    rows = np.stack([np.cos(phases), -np.sin(phases)], axis=1)
    return jnp.asarray(rows.reshape(WINDOW, WINDOW).astype(np.float32)).astype(bf16)


def lag_rows(windows):
    frequency = np.arange(HALF)
    weight = np.where(frequency == 0, 1.0, 2.0) / (WINDOW * float(WINDOW * windows) ** 0.5)
    tables = []
    for parity in range(2):
        shift = np.arange(parity, LAGS, 2)[:, None] - LAGS // 2
        phases = 2.0 * np.pi / WINDOW * (frequency[None, :] * shift % WINDOW)
        real = weight * np.cos(phases)
        imag = -weight * np.sin(phases)
        middle = 2.0 * np.pi / WINDOW * (HALF * shift[:, 0] % WINDOW)
        imag[:, 0] = weight[1] * (np.cos(middle) if parity == 0 else -np.sin(middle))
        tables.append(np.concatenate([real, imag], axis=1))
    return jnp.asarray(np.stack(tables).astype(np.float32)).astype(bf16)


def taper_row():
    return (0.5 - 0.5 * np.cos(2.0 * np.pi * np.arange(WINDOW) / WINDOW)).astype(np.float32)[None]


def spectra_kernel(chunks, half, me_ref, signal_ref, flags_ref, table_ref, taper_ref, *refs):
    outs, (tap, rows32, live) = refs[:-3], refs[-3:]
    piece_refs, own_ref = outs[:-1], outs[-1]
    row_count = signal_ref.shape[0]
    spans = signal_ref.shape[1] // WINDOW
    taper = taper_ref[...]
    tap[...] = jnp.zeros_like(tap)
    live[...] = jnp.zeros_like(live)
    live[:, :row_count] = flags_ref[...].astype(f32)
    for w in range(spans):
        x = signal_ref[:, w * WINDOW : (w + 1) * WINDOW]
        mean_square = jnp.mean(x * x, axis=1, keepdims=True)
        scale = lax.rsqrt(mean_square + epsilon)
        tap[pl.ds(w * LANES, row_count), :] = (x * scale * taper).astype(bf16)
    for g in range(4):
        result = lax.dot_general(
            table_ref[g * 256 : (g + 1) * 256, :],
            tap[...],
            (((1,), (1,)), ((), ())),
            preferred_element_type=f32,
        )
        for o in range(16):
            position = g * 16 + o
            tiles = [
                [
                    result[o * 16 + s * 8 : o * 16 + s * 8 + 8, w * LANES : (w + 1) * LANES]
                    * live[w : w + 1, :]
                    for w in range(spans)
                ]
                for s in range(2)
            ]
            real, imag = tiles
            plain = jnp.concatenate([p for w in range(spans) for p in (real[w], imag[w])], axis=0)
            turned = jnp.concatenate([p for w in range(spans) for p in (imag[w], -real[w])], axis=0)
            own_ref[position, :, :LANES] = plain.astype(bf16)
            own_ref[position, :, LANES:] = turned.astype(bf16)
            flipped = jnp.transpose(plain)
            for c in range(0, row_count, 8):
                rows32[pl.ds(c * OCTETS + position, 8, stride=OCTETS), :] = flipped[c : c + 8]
    me = me_ref[0]
    start = 0
    for k, rows in enumerate(chunks):
        for side in range(2):
            first = (me * half if side == 0 else (1 - me) * half) + start
            block = rows32[pl.ds(pl.multiple_of(first * OCTETS, OCTETS), rows * OCTETS), :]
            piece_refs[2 * k + side][...] = block.astype(bf16).reshape(rows, OCTETS, LANES)
        start += rows


def spectra(me, signal, valid_flags, table, taper, chunks, half):
    row_count = signal.shape[0]
    spans = signal.shape[1] // WINDOW
    pieces = [
        jax.ShapeDtypeStruct((rows, OCTETS, LANES), bf16)
        for rows in chunks
        for _ in range(2)
    ]
    own = jax.ShapeDtypeStruct((OCTETS, LANES, 2 * LANES), bf16)
    vmem = pl.BlockSpec(memory_space=pltpu.VMEM)
    return pl.pallas_call(
        functools.partial(spectra_kernel, chunks, half),
        out_shape=pieces + [own],
        in_specs=[pl.BlockSpec(memory_space=pltpu.SMEM)] + [vmem] * 4,
        out_specs=[vmem] * (len(pieces) + 1),
        scratch_shapes=[
            pltpu.VMEM((spans * LANES, WINDOW), bf16),
            pltpu.VMEM((row_count * OCTETS, LANES), f32),
            pltpu.VMEM((spans, LANES), f32),
        ],
        compiler_params=pltpu.CompilerParams(vmem_limit_bytes=60 << 20),
        cost_estimate=pl.CostEstimate(flops=2 * WINDOW**3, bytes_accessed=12 << 20, transcendentals=0),
        name="spectra",
    )(me, signal, valid_flags, table, taper)


def cross_kernel(parts, row_count, has_prior, odd_ref, *refs):
    source_count = sum(2 * alternatives for _, _, _, alternatives in parts)
    near_ref, far_ref, lag_ref = refs[:3]
    sources = refs[3 : 3 + source_count]
    rest = refs[3 + source_count + (1 if has_prior else 0) :]
    out_ref, packed, rows32, cross, mixed, result, in_sem, out_sem = rest
    total = sum(part[2] for part in parts)
    pairs = total // 2

    def load(part_index, side):
        cursor, row = 0, 0
        for index, (_, _, rows, alternatives) in enumerate(parts):
            if index == part_index:
                return [
                    pltpu.make_async_copy(
                        sources[cursor + 2 * a + side],
                        packed.at[pl.ds(row, rows), side],
                        in_sem.at[index, side],
                    )
                    for a in range(alternatives)
                ]
            cursor += 2 * alternatives
            row += rows

    for index, part in enumerate(parts):
        for side in range(2):
            copies = load(index, side)
            if len(copies) == 1:
                copies[0].start()
            else:
                odd = odd_ref[0]
                pl.when(odd == 0)(copies[0].start)
                pl.when(odd != 0)(copies[1].start)
    row = 0
    for index, part in enumerate(parts):
        for side in range(2):
            load(index, side)[0].wait()
        rows32[pl.ds(row, part[2])] = packed[pl.ds(row, part[2])].astype(f32)
        row += part[2]

    lane = lax.broadcasted_iota(jnp.int32, (GROUP, LANES), 1)
    sub = lax.broadcasted_iota(jnp.int32, (GROUP, LANES), 0)
    keep = lax.rem(lane, GROUP) == sub
    zero = jnp.zeros((GROUP, LANES), f32)
    top = sub == 0

    def step(m, first):
        products = []
        for j in range(4):
            position = m * 4 + j
            blocks = []
            for d in range(total):
                halves = [
                    jnp.where(
                        keep,
                        jnp.broadcast_to(rows32[d, side, pl.ds(position, 1), :], (GROUP, LANES)),
                        zero,
                    )
                    for side in range(2)
                ]
                blocks.append(jnp.concatenate(halves, axis=1))
            left = jnp.concatenate(blocks, axis=0).astype(bf16)
            weight = jnp.concatenate([near_ref[position], far_ref[position]], axis=0)
            products.append(jnp.dot(left, weight, preferred_element_type=f32))
        base = pl.multiple_of(m * 16, 16)
        for d in range(total):
            a0, a1, b0, b1 = [p[d * GROUP : (d + 1) * GROUP] for p in products]
            s0, s1, t0, t1 = a0 + b0, a1 + b1, a0 - b0, a1 - b1
            even_real, odd_real = s0[:, :LANES], t0[:, :LANES]
            even_imag, odd_imag = t0[:, LANES:], s0[:, LANES:]
            if first:
                even_real = jnp.where(top, a0[:, :LANES], even_real)
                odd_real = jnp.where(top, a0[:, :LANES], odd_real)
                even_imag = jnp.where(top, b0[:, :LANES], even_imag)
                odd_imag = jnp.where(top, b0[:, LANES:], odd_imag)
            p, lanes = d // 2, pl.ds((d % 2) * LANES, LANES)
            for parity, offset, low, high in (
                (0, 0, even_real, s1[:, :LANES]),
                (0, HALF, even_imag, t1[:, LANES:]),
                (1, 0, odd_real, t1[:, :LANES]),
                (1, HALF, odd_imag, s1[:, LANES:]),
            ):
                cross[parity, p, pl.ds(base + offset, 16), lanes] = jnp.concatenate(
                    [low, high], axis=0
                ).astype(bf16)

    step(0, True)
    lax.fori_loop(1, STEPS, lambda m, c: (step(m, False), c)[1], 0)

    targets = [(part[0], part[1] + i) for part in parts for i in range(part[2])]
    out_copies = []
    for p in range(pairs):
        for parity in range(2):
            lagged = jnp.dot(lag_ref[parity], cross[parity, p], preferred_element_type=f32)
            for d in range(2):
                mixed[p % 2, d, pl.ds(parity, LAGS // 2, stride=2), :] = lagged[:, d * LANES : (d + 1) * LANES]
        for d in range(2):
            result[2 * p + d] = jnp.transpose(mixed[p % 2, d].astype(bf16))[:row_count]
            target = targets[2 * p + d]
            copy = pltpu.make_async_copy(
                result.at[2 * p + d], out_ref.at[target[0], target[1]], out_sem.at[2 * p + d]
            )
            copy.start()
            out_copies.append(copy)
    for copy in out_copies:
        copy.wait()


def cross_part(odd, near, far, lag_table, parts, sources, prior, local_rows, row_count):
    total = sum(part[2] for part in parts)
    any_space = pl.BlockSpec(memory_space=pl.ANY)
    operands = [odd, near, far, lag_table] + sources
    specs = [pl.BlockSpec(memory_space=pltpu.SMEM)] + [pl.BlockSpec(memory_space=pltpu.VMEM)] * 3
    specs += [pl.BlockSpec(memory_space=pltpu.MemorySpace.HBM)] * len(sources)
    aliases = {}
    if prior is not None:
        aliases = {len(operands): 0}
        operands.append(prior)
        specs.append(any_space)
    return pl.pallas_call(
        functools.partial(cross_kernel, tuple(parts), row_count, prior is not None),
        out_shape=jax.ShapeDtypeStruct((ROUNDS, local_rows, row_count, LAGS), bf16),
        in_specs=specs,
        out_specs=any_space,
        scratch_shapes=[
            pltpu.VMEM((total, 2, OCTETS, LANES), bf16),
            pltpu.VMEM((total, 2, OCTETS, LANES), f32),
            pltpu.VMEM((2, total // 2, 2 * HALF, 2 * LANES), bf16),
            pltpu.VMEM((2, 2, LAGS, LANES), f32),
            pltpu.VMEM((total, row_count, LAGS), bf16),
            pltpu.SemaphoreType.DMA((len(parts), 2)),
            pltpu.SemaphoreType.DMA((total,)),
        ],
        input_output_aliases=aliases,
        compiler_params=pltpu.CompilerParams(vmem_limit_bytes=40 << 20),
        cost_estimate=pl.CostEstimate(
            flops=total * 600_000_000 // 4, bytes_accessed=12 << 20, transcendentals=0
        ),
        name="cross",
    )(*operands)


def chunk_rows(local_rows):
    if sum(ROWS_PER_CHUNK) == local_rows:
        return ROWS_PER_CHUNK
    return (local_rows,)


def local(signal, valid_flags):
    row_count = signal.shape[0]
    span_windows = signal.shape[1] // WINDOW
    owner_count = lax.axis_size("tm")
    blocks = lax.axis_size("chan")
    local_rows = row_count // owner_count
    chunks = chunk_rows(local_rows)
    me = lax.axis_index("tm").astype(jnp.int32)
    odd = lax.rem(lax.axis_index("chan"), 2).astype(jnp.int32)

    *pieces, near = spectra(
        me[None], signal, valid_flags.T, forward_rows(), taper_row(), chunks, local_rows
    )

    def back(hops, side):
        return [
            (b * owner_count + t, (b - hops) % blocks * owner_count + (t + side) % owner_count)
            for b in range(blocks)
            for t in range(owner_count)
        ]

    axes = ("chan", "tm")
    two_away = [lax.ppermute(x, axes, back(2, i % 2)) for i, x in enumerate(pieces)]
    one_away = [
        lax.ppermute(x, axes, [q for q in back(1, i % 2) if q[0] // owner_count % 2 == 1])
        for i, x in enumerate(pieces)
    ]
    far = lax.ppermute(near, "tm", [(0, 1), (1, 0)])
    onward = [(b, b + 1) for b in range(0, blocks, 2)]
    relayed = [lax.ppermute(x, "chan", onward) for x in two_away]

    lag_table = lag_rows(span_windows * owner_count)
    out = None
    starts = np.cumsum([0] + list(chunks))
    for k in range(len(chunks) + 1):
        parts, sources = [], []
        if k < len(chunks):
            parts.append((1, int(starts[k]), chunks[k], 1))
            sources += two_away[2 * k : 2 * k + 2]
        if k > 0:
            parts.append((0, int(starts[k - 1]), chunks[k - 1], 2))
            sources += one_away[2 * k - 2 : 2 * k] + relayed[2 * k - 2 : 2 * k]
        out = cross_part(
            odd[None], near, far, lag_table, parts, sources, out, local_rows, row_count
        )
    return out


def solution(mesh):
    return jax.shard_map(
        local,
        mesh=mesh,
        in_specs=(P(("group", "chan"), "tm"), P(("group", "chan"), "tm")),
        out_specs=P(None, "tm", ("group", "chan"), None),
        check_vma=False,
    )
```

profile of v0, /device:TPU:0, one launch (start us, length us, event | category | flops | bytes accessed | tf_op | source)
XLA Modules:
  0.0 112.1 jit_solution(10708542533313454385)
XLA Ops:
  0.0 9.9 %spectra.1 = (bf16[20,64,128]{2,1,0:T(8,128)(2,1)}, bf16[20,64,128]{2,1,0:T(8,128)(2,1)}, bf16[20,64,128]{2,1,0:T(8,128)(2,1)}, bf16[20,64,128]{2,1,0:T(8,128)(2...) custom-call(s32[1]{0:T(128)} %bitcast.1.me_ref, ...), custom_call_target="tpu_custom_call" | custom-call | flops 2147483648 | bytes 12582912 | tf_op jit(solution)/shard_map/spectra/pallas_call | solution.py:124
  9.9 0.5 collective-permute-start
  10.4 4.6 %collective-permute-start.15 = (bf16[20,64,128]{2,1,0:T(8,128)(2,1)}, bf16[20,64,128]{2,1,0:T(8,128)(2,1)S(1)}, u32[]{:S(2)}, u32[]{:S(2)}) collective-permute-start(bf16[20,64,128]{2,1,0:T(8,128)(2,1)} %get-tuple-element.17), channel_id=1, source_target_pairs={{0,12},{1,13},{2,14},{3,15},{4,0},{5,1},{6,2},{7,3},{8,4},{9,5},{1... | collective-permute-start | bytes 983048 | tf_op jit(solution)/shard_map/ppermute | solution.py:310
  15.0 0.3 collective-permute-start.17
  15.3 0.3 collective-permute-start.11
  15.6 0.1 collective-permute-start.3
  15.8 25.4 %collective-permute-done.3.refs_3_ = bf16[12,64,128]{2,1,0:T(8,128)(2,1)S(1)} collective-permute-done((bf16[12,64,128]{2,1,0:T(8,128)(2,1)}, bf16[12,64,128]{2,1,0:T(8,128)(2,1)S(1)}, u32[]{:S(2)}, u32[]{:S(2)}) %collective-permute-start.3) | collective-permute-done | bytes 196640 | tf_op jit(solution)/shard_map/ppermute | solution.py:310
  41.2 4.2 %collective-permute-start.9 = (bf16[20,64,128]{2,1,0:T(8,128)(2,1)}, bf16[20,64,128]{2,1,0:T(8,128)(2,1)S(1)}, u32[]{:S(2)}, u32[]{:S(2)}) collective-permute-start(bf16[20,64,128]{2,1,0:T(8,128)(2,1)} %get-tuple-element.15), channel_id=1, source_target_pairs={{0,12},{1,13},{2,14},{3,15},{4,0},{5,1},{6,2},{7,3},{8,4},{9,5},{1... | collective-permute-start | bytes 983048 | tf_op jit(solution)/shard_map/ppermute | solution.py:310
  45.4 0.0 collective-permute-done.15.refs_3_
  45.4 1.3 %collective-permute-start.13 = (bf16[20,64,128]{2,1,0:T(8,128)(2,1)}, bf16[20,64,128]{2,1,0:T(8,128)(2,1)S(1)}, u32[]{:S(2)}, u32[]{:S(2)}) collective-permute-start(bf16[20,64,128]{2,1,0:T(8,128)(2,1)} %get-tuple-element.17), channel_id=1, source_target_pairs={{2,0},{3,1},{6,4},{7,5},{10,8},{11,9},{14,12},{15,13},{18,16},{19,... | collective-permute-start | bytes 983048 | tf_op jit(solution)/shard_map/ppermute | solution.py:312
  46.7 0.0 collective-permute-done.17.refs_4_
  46.7 1.3 %collective-permute-start.14 = (bf16[20,64,128]{2,1,0:T(8,128)(2,1)}, bf16[20,64,128]{2,1,0:T(8,128)(2,1)S(1)}, u32[]{:S(2)}, u32[]{:S(2)}) collective-permute-start(bf16[20,64,128]{2,1,0:T(8,128)(2,1)} %get-tuple-element.18), channel_id=1, source_target_pairs={{2,1},{3,0},{6,5},{7,4},{10,9},{11,8},{14,13},{15,12},{18,17},{19,... | collective-permute-start | bytes 983048 | tf_op jit(solution)/shard_map/ppermute | solution.py:312
  48.0 0.0 collective-permute-done.11.refs_4_
  48.0 4.6 %collective-permute-start.16 = (bf16[20,64,128]{2,1,0:T(8,128)(2,1)S(1)}, bf16[20,64,128]{2,1,0:T(8,128)(2,1)S(1)}, u32[]{:S(2)}, u32[]{:S(2)}) collective-permute-start(bf16[20,64,128]{2,1,0:T(8,128)(2,1)S(1)} %collective-permute-done.15.refs_3_), channel_id=1, source_target_pairs={{0,2},{4,6},{8,10},{12,14},{1,3},{5,7},{9,11},{13,15},{16,18},{20,... | collective-permute-start | bytes 983048 | tf_op jit(solution)/shard_map/ppermute | solution.py:317
  52.6 0.0 collective-permute-done.refs_1_
  52.6 1.9 %copy-done.1 = bf16[64,128,256]{2,1,0:T(8,128)(2,1)} copy-done((bf16[64,128,256]{2,1,0:T(8,128)(2,1)}, bf16[64,128,256]{2,1,0:T(8,128)(2,1)S(1)}, u32[]{:S(2)}) %copy-start.1) | copy-done | bytes 4194328
  54.6 1.3 %collective-permute-start.18 = (bf16[20,64,128]{2,1,0:T(8,128)(2,1)S(1)}, bf16[20,64,128]{2,1,0:T(8,128)(2,1)S(1)}, u32[]{:S(2)}, u32[]{:S(2)}) collective-permute-start(bf16[20,64,128]{2,1,0:T(8,128)(2,1)S(1)} %collective-permute-done.17.refs_4_), channel_id=1, source_target_pairs={{0,2},{4,6},{8,10},{12,14},{1,3},{5,7},{9,11},{13,15},{16,18},{20,... | collective-permute-start | bytes 983048 | tf_op jit(solution)/shard_map/ppermute | solution.py:317
  55.9 0.0 copy-start
  55.9 2.2 %copy-done = bf16[64,128,256]{2,1,0:T(8,128)(2,1)S(1)} copy-done((bf16[64,128,256]{2,1,0:T(8,128)(2,1)S(1)}, bf16[64,128,256]{2,1,0:T(8,128)(2,1)}, u32[]{:S(2)}) %copy-start) | copy-done | bytes 4194328
  58.1 2.2 %copy-done.2 = bf16[64,128,256]{2,1,0:T(8,128)(2,1)S(1)} copy-done((bf16[64,128,256]{2,1,0:T(8,128)(2,1)S(1)}, bf16[64,128,256]{2,1,0:T(8,128)(2,1)}, u32[]{:S(2)}) %copy-start.2) | copy-done | bytes 4194328
  60.3 1.0 copy-done.3
  61.3 7.2 %cross.4.refs_9_ = bf16[2,52,104,512]{3,2,1,0:T(8,128)(2,1)} custom-call(s32[1]{0:T(128)} %bitcast.odd_ref, bf16[64,128,256]{2,1,0:T(8,128)(2,1)S(1)} %copy-done, bf16[64,128,256]{2,1,0:T(8,128)(2,1)S(1)} %copy-done.2, bf16[2,256,512]{2,1,0:T(8,128)(2,1)S(1)} %copy-done.3, bf16[20,64,128]{2,1,0:T(8,128)(2,1)S(1)} %collective-permute-done.15.refs_3_, ...), custom_call_target="tpu_custom_call" | custom-call | flops 3000000000 | bytes 12582912 | tf_op jit(solution)/shard_map/cross/pallas_call | solution.py:259
  68.5 0.0 collective-permute-done.9.refs_3_
  68.5 1.3 %collective-permute-start.7 = (bf16[20,64,128]{2,1,0:T(8,128)(2,1)S(1)}, bf16[20,64,128]{2,1,0:T(8,128)(2,1)S(1)}, u32[]{:S(2)}, u32[]{:S(2)}) collective-permute-start(bf16[20,64,128]{2,1,0:T(8,128)(2,1)S(1)} %copy-done.5), channel_id=1, source_target_pairs={{2,0},{3,1},{6,4},{7,5},{10,8},{11,9},{14,12},{15,13},{18,16},{19,... | collective-permute-start | bytes 983048 | tf_op jit(solution)/shard_map/ppermute | solution.py:312
  69.8 0.0 collective-permute-done.13.refs_5_
  69.8 1.3 %collective-permute-start.8 = (bf16[20,64,128]{2,1,0:T(8,128)(2,1)S(1)}, bf16[20,64,128]{2,1,0:T(8,128)(2,1)S(1)}, u32[]{:S(2)}, u32[]{:S(2)}) collective-permute-start(bf16[20,64,128]{2,1,0:T(8,128)(2,1)S(1)} %copy-done.4), channel_id=1, source_target_pairs={{2,1},{3,0},{6,5},{7,4},{10,9},{11,8},{14,13},{15,12},{18,17},{19,... | collective-permute-start | bytes 983048 | tf_op jit(solution)/shard_map/ppermute | solution.py:312
  71.1 0.0 collective-permute-done.14.refs_6_
  71.2 0.1 collective-permute-start.5
  71.2 0.0 collective-permute-done.16.refs_7_
  71.2 4.6 %collective-permute-start.10 = (bf16[20,64,128]{2,1,0:T(8,128)(2,1)S(1)}, bf16[20,64,128]{2,1,0:T(8,128)(2,1)S(1)}, u32[]{:S(2)}, u32[]{:S(2)}) collective-permute-start(bf16[20,64,128]{2,1,0:T(8,128)(2,1)S(1)} %collective-permute-done.9.refs_3_), channel_id=1, source_target_pairs={{0,2},{4,6},{8,10},{12,14},{1,3},{5,7},{9,11},{13,15},{16,18},{20,... | collective-permute-start | bytes 983048 | tf_op jit(solution)/shard_map/ppermute | solution.py:317
  75.9 0.0 collective-permute-done.18.refs_8_
  75.9 1.3 %collective-permute-start.12 = (bf16[20,64,128]{2,1,0:T(8,128)(2,1)S(1)}, bf16[20,64,128]{2,1,0:T(8,128)(2,1)S(1)}, u32[]{:S(2)}, u32[]{:S(2)}) collective-permute-start(bf16[20,64,128]{2,1,0:T(8,128)(2,1)S(1)} %collective-permute-done.11.refs_4_), channel_id=1, source_target_pairs={{0,2},{4,6},{8,10},{12,14},{1,3},{5,7},{9,11},{13,15},{16,18},{20,... | collective-permute-start | bytes 983048 | tf_op jit(solution)/shard_map/ppermute | solution.py:317
  77.2 10.9 %cross.5.refs_9_ = bf16[2,52,104,512]{3,2,1,0:T(8,128)(2,1)} custom-call(s32[1]{0:T(128)} %bitcast.odd_ref, bf16[64,128,256]{2,1,0:T(8,128)(2,1)S(1)} %copy-done, bf16[64,128,256]{2,1,0:T(8,128)(2,1)S(1)} %copy-done.2, bf16[2,256,512]{2,1,0:T(8,128)(2,1)S(1)} %copy-done.3, ...), custom_call_target="tpu_custom_call", output_to_operand_aliasing={{}: (10, {})} | custom-call | flops 6000000000 | bytes 12582912 | tf_op jit(solution)/shard_map/cross/pallas_call | solution.py:259
  88.1 0.0 collective-permute-done.5.refs_4_
  88.1 1.3 %collective-permute-start.1 = (bf16[12,64,128]{2,1,0:T(8,128)(2,1)S(1)}, bf16[12,64,128]{2,1,0:T(8,128)(2,1)S(1)}, u32[]{:S(2)}, u32[]{:S(2)}) collective-permute-start(bf16[12,64,128]{2,1,0:T(8,128)(2,1)S(1)} %copy-done.7), channel_id=1, source_target_pairs={{2,0},{3,1},{6,4},{7,5},{10,8},{11,9},{14,12},{15,13},{18,16},{19,... | collective-permute-start | bytes 589832 | tf_op jit(solution)/shard_map/ppermute | solution.py:312
  89.4 0.0 collective-permute-done.7.refs_5_
  89.4 1.3 %collective-permute-start.2 = (bf16[12,64,128]{2,1,0:T(8,128)(2,1)S(1)}, bf16[12,64,128]{2,1,0:T(8,128)(2,1)S(1)}, u32[]{:S(2)}, u32[]{:S(2)}) collective-permute-start(bf16[12,64,128]{2,1,0:T(8,128)(2,1)S(1)} %copy-done.6), channel_id=1, source_target_pairs={{2,1},{3,0},{6,5},{7,4},{10,9},{11,8},{14,13},{15,12},{18,17},{19,... | collective-permute-start | bytes 589832 | tf_op jit(solution)/shard_map/ppermute | solution.py:312
  90.7 0.0 collective-permute-done.8.refs_6_
  90.7 4.6 %collective-permute-start.4 = (bf16[12,64,128]{2,1,0:T(8,128)(2,1)S(1)}, bf16[12,64,128]{2,1,0:T(8,128)(2,1)S(1)}, u32[]{:S(2)}, u32[]{:S(2)}) collective-permute-start(bf16[12,64,128]{2,1,0:T(8,128)(2,1)S(1)} %collective-permute-done.3.refs_3_), channel_id=1, source_target_pairs={{0,2},{4,6},{8,10},{12,14},{1,3},{5,7},{9,11},{13,15},{16,18},{20,... | collective-permute-start | bytes 589832 | tf_op jit(solution)/shard_map/ppermute | solution.py:317
  95.3 0.0 collective-permute-done.10.refs_7_
  95.3 1.3 %collective-permute-start.6 = (bf16[12,64,128]{2,1,0:T(8,128)(2,1)S(1)}, bf16[12,64,128]{2,1,0:T(8,128)(2,1)S(1)}, u32[]{:S(2)}, u32[]{:S(2)}) collective-permute-start(bf16[12,64,128]{2,1,0:T(8,128)(2,1)S(1)} %collective-permute-done.5.refs_4_), channel_id=1, source_target_pairs={{0,2},{4,6},{8,10},{12,14},{1,3},{5,7},{9,11},{13,15},{16,18},{20,... | collective-permute-start | bytes 589832 | tf_op jit(solution)/shard_map/ppermute | solution.py:317
  96.6 0.0 collective-permute-done.12.refs_8_
  96.6 9.3 %cross.6.refs_7_ = bf16[2,52,104,512]{3,2,1,0:T(8,128)(2,1)} custom-call(s32[1]{0:T(128)} %bitcast.odd_ref, bf16[64,128,256]{2,1,0:T(8,128)(2,1)S(1)} %copy-done, bf16[64,128,256]{2,1,0:T(8,128)(2,1)S(1)} %copy-done.2, bf16[2,256,512]{2,1,0:T(8,128)(2,1)S(1)} %copy-done.3, ...), custom_call_target="tpu_custom_call", output_to_operand_aliasing={{}: (10, {})} | custom-call | flops 4800000000 | bytes 12582912 | tf_op jit(solution)/shard_map/cross/pallas_call | solution.py:259
  105.9 0.0 collective-permute-done.1.refs_3_
  106.0 0.0 collective-permute-done.2.refs_4_
  106.0 0.0 collective-permute-done.4.refs_5_
  106.0 0.0 collective-permute-done.6.refs_6_
  106.0 5.9 %cross.7 = bf16[2,52,104,512]{3,2,1,0:T(8,128)(2,1)} custom-call(s32[1]{0:T(128)} %bitcast.odd_ref, bf16[64,128,256]{2,1,0:T(8,128)(2,1)S(1)} %copy-done, bf16[64,128,256]{2,1,0:T(8,128)(2,1)S(1)} %copy-done.2, bf16[2,256,512]{2,1,0:T(8,128)(2,1)S(1)} %copy-done.3, ...), custom_call_target="tpu_custom_call", output_to_operand_aliasing={{}: (8, {})} | custom-call | flops 1800000000 | bytes 12582912 | tf_op jit(solution)/shard_map/cross/pallas_call | solution.py:259
  (11 shorter events, 0.0 us)
Async XLA Ops:
  9.9 42.7 %collective-permute-start = (bf16[64,128,256]{2,1,0:T(8,128)(2,1)}, bf16[64,128,256]{2,1,0:T(8,128)(2,1)S(1)}, u32[]{:S(2)}, u32[]{:S(2)}) collective-permute-start(bf16[64,128,256]{2,1,0:T(8,128)(2,1)} %get-tuple-element.12.refs_0_), channel_id=1, source_target_pairs={{0,1},{1,0},{2,3},{3,2},{4,5},{5,4},{6,7},{7,6},{8,9},{9,8},{10,11... | collective-permute-start | bytes 12582920 | tf_op jit(solution)/shard_map/ppermute | solution.py:315
  10.4 35.0 %collective-permute-start.15 = (bf16[20,64,128]{2,1,0:T(8,128)(2,1)}, bf16[20,64,128]{2,1,0:T(8,128)(2,1)S(1)}, u32[]{:S(2)}, u32[]{:S(2)}) collective-permute-start(bf16[20,64,128]{2,1,0:T(8,128)(2,1)} %get-tuple-element.17), channel_id=1, source_target_pairs={{0,12},{1,13},{2,14},{3,15},{4,0},{5,1},{6,2},{7,3},{8,4},{9,5},{1... | collective-permute-start | bytes 983048 | tf_op jit(solution)/shard_map/ppermute | solution.py:310
  15.0 31.7 %collective-permute-start.17 = (bf16[20,64,128]{2,1,0:T(8,128)(2,1)}, bf16[20,64,128]{2,1,0:T(8,128)(2,1)S(1)}, u32[]{:S(2)}, u32[]{:S(2)}) collective-permute-start(bf16[20,64,128]{2,1,0:T(8,128)(2,1)} %get-tuple-element.18), channel_id=1, source_target_pairs={{0,13},{1,12},{2,15},{3,14},{4,1},{5,0},{6,3},{7,2},{8,5},{9,4},{1... | collective-permute-start | bytes 983048 | tf_op jit(solution)/shard_map/ppermute | solution.py:310
  15.3 32.7 %collective-permute-start.11 = (bf16[20,64,128]{2,1,0:T(8,128)(2,1)}, bf16[20,64,128]{2,1,0:T(8,128)(2,1)S(1)}, u32[]{:S(2)}, u32[]{:S(2)}) collective-permute-start(bf16[20,64,128]{2,1,0:T(8,128)(2,1)} %get-tuple-element.16), channel_id=1, source_target_pairs={{0,13},{1,12},{2,15},{3,14},{4,1},{5,0},{6,3},{7,2},{8,5},{9,4},{1... | collective-permute-start | bytes 983048 | tf_op jit(solution)/shard_map/ppermute | solution.py:310
  15.6 25.6 %collective-permute-start.3 = (bf16[12,64,128]{2,1,0:T(8,128)(2,1)}, bf16[12,64,128]{2,1,0:T(8,128)(2,1)S(1)}, u32[]{:S(2)}, u32[]{:S(2)}) collective-permute-start(bf16[12,64,128]{2,1,0:T(8,128)(2,1)} %get-tuple-element.13), channel_id=1, source_target_pairs={{0,12},{1,13},{2,14},{3,15},{4,0},{5,1},{6,2},{7,3},{8,4},{9,5},{1... | collective-permute-start | bytes 589832 | tf_op jit(solution)/shard_map/ppermute | solution.py:310
  41.2 27.3 %collective-permute-start.9 = (bf16[20,64,128]{2,1,0:T(8,128)(2,1)}, bf16[20,64,128]{2,1,0:T(8,128)(2,1)S(1)}, u32[]{:S(2)}, u32[]{:S(2)}) collective-permute-start(bf16[20,64,128]{2,1,0:T(8,128)(2,1)} %get-tuple-element.15), channel_id=1, source_target_pairs={{0,12},{1,13},{2,14},{3,15},{4,0},{5,1},{6,2},{7,3},{8,4},{9,5},{1... | collective-permute-start | bytes 983048 | tf_op jit(solution)/shard_map/ppermute | solution.py:310
  45.4 24.4 %collective-permute-start.13 = (bf16[20,64,128]{2,1,0:T(8,128)(2,1)}, bf16[20,64,128]{2,1,0:T(8,128)(2,1)S(1)}, u32[]{:S(2)}, u32[]{:S(2)}) collective-permute-start(bf16[20,64,128]{2,1,0:T(8,128)(2,1)} %get-tuple-element.17), channel_id=1, source_target_pairs={{2,0},{3,1},{6,4},{7,5},{10,8},{11,9},{14,12},{15,13},{18,16},{19,... | collective-permute-start | bytes 983048 | tf_op jit(solution)/shard_map/ppermute | solution.py:312
  46.7 24.4 %collective-permute-start.14 = (bf16[20,64,128]{2,1,0:T(8,128)(2,1)}, bf16[20,64,128]{2,1,0:T(8,128)(2,1)S(1)}, u32[]{:S(2)}, u32[]{:S(2)}) collective-permute-start(bf16[20,64,128]{2,1,0:T(8,128)(2,1)} %get-tuple-element.18), channel_id=1, source_target_pairs={{2,1},{3,0},{6,5},{7,4},{10,9},{11,8},{14,13},{15,12},{18,17},{19,... | collective-permute-start | bytes 983048 | tf_op jit(solution)/shard_map/ppermute | solution.py:312
  48.0 23.2 %collective-permute-start.16 = (bf16[20,64,128]{2,1,0:T(8,128)(2,1)S(1)}, bf16[20,64,128]{2,1,0:T(8,128)(2,1)S(1)}, u32[]{:S(2)}, u32[]{:S(2)}) collective-permute-start(bf16[20,64,128]{2,1,0:T(8,128)(2,1)S(1)} %collective-permute-done.15.refs_3_), channel_id=1, source_target_pairs={{0,2},{4,6},{8,10},{12,14},{1,3},{5,7},{9,11},{13,15},{16,18},{20,... | collective-permute-start | bytes 983048 | tf_op jit(solution)/shard_map/ppermute | solution.py:317
  52.6 2.0 %copy-start.1 = (bf16[64,128,256]{2,1,0:T(8,128)(2,1)}, bf16[64,128,256]{2,1,0:T(8,128)(2,1)S(1)}, u32[]{:S(2)}) copy-start(bf16[64,128,256]{2,1,0:T(8,128)(2,1)S(1)} %collective-permute-done.refs_1_) | copy-start | bytes 12582916
  54.6 21.3 %collective-permute-start.18 = (bf16[20,64,128]{2,1,0:T(8,128)(2,1)S(1)}, bf16[20,64,128]{2,1,0:T(8,128)(2,1)S(1)}, u32[]{:S(2)}, u32[]{:S(2)}) collective-permute-start(bf16[20,64,128]{2,1,0:T(8,128)(2,1)S(1)} %collective-permute-done.17.refs_4_), channel_id=1, source_target_pairs={{0,2},{4,6},{8,10},{12,14},{1,3},{5,7},{9,11},{13,15},{16,18},{20,... | collective-permute-start | bytes 983048 | tf_op jit(solution)/shard_map/ppermute | solution.py:317
  55.9 2.2 %copy-start = (bf16[64,128,256]{2,1,0:T(8,128)(2,1)S(1)}, bf16[64,128,256]{2,1,0:T(8,128)(2,1)}, u32[]{:S(2)}) copy-start(bf16[64,128,256]{2,1,0:T(8,128)(2,1)} %get-tuple-element.12.refs_0_) | copy-start | bytes 12582916
  58.1 2.2 %copy-start.2 = (bf16[64,128,256]{2,1,0:T(8,128)(2,1)S(1)}, bf16[64,128,256]{2,1,0:T(8,128)(2,1)}, u32[]{:S(2)}) copy-start(bf16[64,128,256]{2,1,0:T(8,128)(2,1)} %copy-done.1) | copy-start | bytes 12582916
  60.3 1.0 copy-start.3
  61.3 7.2 %copy-start.5 = (bf16[20,64,128]{2,1,0:T(8,128)(2,1)S(1)}, bf16[20,64,128]{2,1,0:T(8,128)(2,1)}, u32[]{:S(2)}) copy-start(bf16[20,64,128]{2,1,0:T(8,128)(2,1)} %get-tuple-element.15) | copy-start | bytes 983044
  61.3 8.5 %copy-start.4 = (bf16[20,64,128]{2,1,0:T(8,128)(2,1)S(1)}, bf16[20,64,128]{2,1,0:T(8,128)(2,1)}, u32[]{:S(2)}) copy-start(bf16[20,64,128]{2,1,0:T(8,128)(2,1)} %get-tuple-element.16) | copy-start | bytes 983044
  61.3 9.8 %copy-start.6 = (bf16[12,64,128]{2,1,0:T(8,128)(2,1)S(1)}, bf16[12,64,128]{2,1,0:T(8,128)(2,1)}, u32[]{:S(2)}) copy-start(bf16[12,64,128]{2,1,0:T(8,128)(2,1)} %get-tuple-element.14) | copy-start | bytes 589828
  68.5 20.9 %collective-permute-start.7 = (bf16[20,64,128]{2,1,0:T(8,128)(2,1)S(1)}, bf16[20,64,128]{2,1,0:T(8,128)(2,1)S(1)}, u32[]{:S(2)}, u32[]{:S(2)}) collective-permute-start(bf16[20,64,128]{2,1,0:T(8,128)(2,1)S(1)} %copy-done.5), channel_id=1, source_target_pairs={{2,0},{3,1},{6,4},{7,5},{10,8},{11,9},{14,12},{15,13},{18,16},{19,... | collective-permute-start | bytes 983048 | tf_op jit(solution)/shard_map/ppermute | solution.py:312
  69.8 20.9 %collective-permute-start.8 = (bf16[20,64,128]{2,1,0:T(8,128)(2,1)S(1)}, bf16[20,64,128]{2,1,0:T(8,128)(2,1)S(1)}, u32[]{:S(2)}, u32[]{:S(2)}) collective-permute-start(bf16[20,64,128]{2,1,0:T(8,128)(2,1)S(1)} %copy-done.4), channel_id=1, source_target_pairs={{2,1},{3,0},{6,5},{7,4},{10,9},{11,8},{14,13},{15,12},{18,17},{19,... | collective-permute-start | bytes 983048 | tf_op jit(solution)/shard_map/ppermute | solution.py:312
  71.2 16.9 %copy-start.7 = (bf16[12,64,128]{2,1,0:T(8,128)(2,1)S(1)}, bf16[12,64,128]{2,1,0:T(8,128)(2,1)}, u32[]{:S(2)}) copy-start(bf16[12,64,128]{2,1,0:T(8,128)(2,1)} %get-tuple-element.13) | copy-start | bytes 589828
  71.2 16.9 %collective-permute-start.5 = (bf16[12,64,128]{2,1,0:T(8,128)(2,1)S(1)}, bf16[12,64,128]{2,1,0:T(8,128)(2,1)S(1)}, u32[]{:S(2)}, u32[]{:S(2)}) collective-permute-start(bf16[12,64,128]{2,1,0:T(8,128)(2,1)S(1)} %copy-done.6), channel_id=1, source_target_pairs={{0,13},{1,12},{2,15},{3,14},{4,1},{5,0},{6,3},{7,2},{8,5},{9,4},{1... | collective-permute-start | bytes 589832 | tf_op jit(solution)/shard_map/ppermute | solution.py:310
  71.2 24.1 %collective-permute-start.10 = (bf16[20,64,128]{2,1,0:T(8,128)(2,1)S(1)}, bf16[20,64,128]{2,1,0:T(8,128)(2,1)S(1)}, u32[]{:S(2)}, u32[]{:S(2)}) collective-permute-start(bf16[20,64,128]{2,1,0:T(8,128)(2,1)S(1)} %collective-permute-done.9.refs_3_), channel_id=1, source_target_pairs={{0,2},{4,6},{8,10},{12,14},{1,3},{5,7},{9,11},{13,15},{16,18},{20,... | collective-permute-start | bytes 983048 | tf_op jit(solution)/shard_map/ppermute | solution.py:317
  75.9 20.8 %collective-permute-start.12 = (bf16[20,64,128]{2,1,0:T(8,128)(2,1)S(1)}, bf16[20,64,128]{2,1,0:T(8,128)(2,1)S(1)}, u32[]{:S(2)}, u32[]{:S(2)}) collective-permute-start(bf16[20,64,128]{2,1,0:T(8,128)(2,1)S(1)} %collective-permute-done.11.refs_4_), channel_id=1, source_target_pairs={{0,2},{4,6},{8,10},{12,14},{1,3},{5,7},{9,11},{13,15},{16,18},{20,... | collective-permute-start | bytes 983048 | tf_op jit(solution)/shard_map/ppermute | solution.py:317
  88.1 17.9 %collective-permute-start.1 = (bf16[12,64,128]{2,1,0:T(8,128)(2,1)S(1)}, bf16[12,64,128]{2,1,0:T(8,128)(2,1)S(1)}, u32[]{:S(2)}, u32[]{:S(2)}) collective-permute-start(bf16[12,64,128]{2,1,0:T(8,128)(2,1)S(1)} %copy-done.7), channel_id=1, source_target_pairs={{2,0},{3,1},{6,4},{7,5},{10,8},{11,9},{14,12},{15,13},{18,16},{19,... | collective-permute-start | bytes 589832 | tf_op jit(solution)/shard_map/ppermute | solution.py:312
  89.4 16.6 %collective-permute-start.2 = (bf16[12,64,128]{2,1,0:T(8,128)(2,1)S(1)}, bf16[12,64,128]{2,1,0:T(8,128)(2,1)S(1)}, u32[]{:S(2)}, u32[]{:S(2)}) collective-permute-start(bf16[12,64,128]{2,1,0:T(8,128)(2,1)S(1)} %copy-done.6), channel_id=1, source_target_pairs={{2,1},{3,0},{6,5},{7,4},{10,9},{11,8},{14,13},{15,12},{18,17},{19,... | collective-permute-start | bytes 589832 | tf_op jit(solution)/shard_map/ppermute | solution.py:312
  90.7 15.3 %collective-permute-start.4 = (bf16[12,64,128]{2,1,0:T(8,128)(2,1)S(1)}, bf16[12,64,128]{2,1,0:T(8,128)(2,1)S(1)}, u32[]{:S(2)}, u32[]{:S(2)}) collective-permute-start(bf16[12,64,128]{2,1,0:T(8,128)(2,1)S(1)} %collective-permute-done.3.refs_3_), channel_id=1, source_target_pairs={{0,2},{4,6},{8,10},{12,14},{1,3},{5,7},{9,11},{13,15},{16,18},{20,... | collective-permute-start | bytes 589832 | tf_op jit(solution)/shard_map/ppermute | solution.py:317
  95.3 10.7 %collective-permute-start.6 = (bf16[12,64,128]{2,1,0:T(8,128)(2,1)S(1)}, bf16[12,64,128]{2,1,0:T(8,128)(2,1)S(1)}, u32[]{:S(2)}, u32[]{:S(2)}) collective-permute-start(bf16[12,64,128]{2,1,0:T(8,128)(2,1)S(1)} %collective-permute-done.5.refs_4_), channel_id=1, source_target_pairs={{0,2},{4,6},{8,10},{12,14},{1,3},{5,7},{9,11},{13,15},{16,18},{20,... | collective-permute-start | bytes 589832 | tf_op jit(solution)/shard_map/ppermute | solution.py:317
where the time goes:
time: 113 us; the launch traced here: 112 us
  Pallas kernels  43.2 us (38%)
  starting transfers between devices  35.5 us (31%)
  waiting for transfers between devices  25.5 us (23%)
  local copies, waits for them, and re-layouts  7.37 us (7%)
    pallas_call x4, Pallas kernels, cross_part(): pl.pallas_call(functools.partial(cross_kernel, tuple(parts), row_count, p...  33.3 us
    ppermute x6, waiting for transfers between devices, local(): lax.ppermute(x, axes, back(2, i % 2))  25.4 us
    ppermute x6, starting transfers between devices, local(): relayed = [lax.ppermute(x, 'chan', onward) for x in two_away]  17.7 us
    pallas_call x1, Pallas kernels, spectra(): pl.pallas_call(functools.partial(spectra_kernel, chunks, half), out_shape...  9.92 us
    ppermute x6, starting transfers between devices, local(): lax.ppermute(x, axes, back(2, i % 2))  9.6 us
    ppermute x6, starting transfers between devices, local(): lax.ppermute(x, axes, [q for q in back(1, i % 2) if q[0] // owner_count %...  7.74 us
    unnamed x16, local copies, waits for them, and re-layouts  7.37 us
  transfers between devices with their start and end apart: 19, of which 1 were waited for; matrix products, arithmetic and copies ran while one was open for 0% of the time, Pallas kernels for 24%

commit v1 on v0

--- a/solution.py
+++ b/solution.py
@@ -64,7 +64,7 @@
 
 def spectra_kernel(chunks, half, me_ref, signal_ref, flags_ref, table_ref, taper_ref, *refs):
     outs, (tap, rows32, live) = refs[:-3], refs[-3:]
-    piece_refs, own_ref = outs[:-1], outs[-1]
+    piece_refs, give_ref, own_ref = outs[:-2], outs[-2], outs[-1]
     row_count = signal_ref.shape[0]
     spans = signal_ref.shape[1] // WINDOW
     taper = taper_ref[...]
@@ -109,6 +109,8 @@
             block = rows32[pl.ds(pl.multiple_of(first * OCTETS, OCTETS), rows * OCTETS), :]
             piece_refs[2 * k + side][...] = block.astype(bf16).reshape(rows, OCTETS, LANES)
         start += rows
+    block = rows32[pl.ds(pl.multiple_of((1 - me) * half * OCTETS, OCTETS), half * OCTETS), :]
+    give_ref[...] = block.astype(bf16).reshape(half, OCTETS, LANES)
 
 
 def spectra(me, signal, valid_flags, table, taper, chunks, half):
@@ -118,7 +120,7 @@
         jax.ShapeDtypeStruct((rows, OCTETS, LANES), bf16)
         for rows in chunks
         for _ in range(2)
-    ]
+    ] + [jax.ShapeDtypeStruct((half, OCTETS, LANES), bf16)]
     own = jax.ShapeDtypeStruct((OCTETS, LANES, 2 * LANES), bf16)
     vmem = pl.BlockSpec(memory_space=pltpu.VMEM)
     return pl.pallas_call(
@@ -137,8 +139,45 @@
     )(me, signal, valid_flags, table, taper)
 
 
-def cross_kernel(parts, row_count, has_prior, odd_ref, *refs):
-    source_count = sum(2 * alternatives for _, _, _, alternatives in parts)
+def payload_kernel(first, rows, odd_ref, keep, taken, near_side, far_side, out_ref, hold, in_sem, out_sem):
+    odd = odd_ref[0]
+    span = pl.ds(first, rows)
+    own = [pltpu.make_async_copy(keep, hold.at[0], in_sem.at[0]),
+           pltpu.make_async_copy(taken.at[span], hold.at[1], in_sem.at[1])]
+    come = [pltpu.make_async_copy(near_side, hold.at[0], in_sem.at[0]),
+            pltpu.make_async_copy(far_side, hold.at[1], in_sem.at[1])]
+    for i in range(2):
+        pl.when(odd != 0)(own[i].start)
+        pl.when(odd == 0)(come[i].start)
+    leave = [pltpu.make_async_copy(hold.at[i], out_ref.at[i], out_sem.at[i]) for i in range(2)]
+    for i in range(2):
+        come[i].wait()
+        leave[i].start()
+    for i in range(2):
+        leave[i].wait()
+
+
+def payload(odd, keep, taken, near_side, far_side, first):
+    hbm = pl.BlockSpec(memory_space=pltpu.MemorySpace.HBM)
+    shape = (2,) + keep.shape
+    return pl.pallas_call(
+        functools.partial(payload_kernel, first, keep.shape[0]),
+        out_shape=jax.ShapeDtypeStruct(shape, bf16),
+        in_specs=[pl.BlockSpec(memory_space=pltpu.SMEM)] + [hbm] * 4,
+        out_specs=hbm,
+        scratch_shapes=[
+            pltpu.VMEM(shape, bf16),
+            pltpu.SemaphoreType.DMA((2,)),
+            pltpu.SemaphoreType.DMA((2,)),
+        ],
+        compiler_params=pltpu.CompilerParams(vmem_limit_bytes=4 << 20),
+        cost_estimate=pl.CostEstimate(flops=0, bytes_accessed=2 << 20, transcendentals=0),
+        name="payload",
+    )(odd, keep, taken, near_side, far_side)
+
+
+def cross_kernel(parts, row_count, has_prior, *refs):
+    source_count = sum(part[3] for part in parts)
     near_ref, far_ref, lag_ref = refs[:3]
     sources = refs[3 : 3 + source_count]
     rest = refs[3 + source_count + (1 if has_prior else 0) :]
@@ -146,36 +185,20 @@
     total = sum(part[2] for part in parts)
     pairs = total // 2
 
-    def load(part_index, side):
-        cursor, row = 0, 0
-        for index, (_, _, rows, alternatives) in enumerate(parts):
-            if index == part_index:
-                return [
-                    pltpu.make_async_copy(
-                        sources[cursor + 2 * a + side],
-                        packed.at[pl.ds(row, rows), side],
-                        in_sem.at[index, side],
-                    )
-                    for a in range(alternatives)
-                ]
-            cursor += 2 * alternatives
-            row += rows
-
-    for index, part in enumerate(parts):
+    loads, cursor, row = [], 0, 0
+    for index, (_, _, rows, arrays) in enumerate(parts):
         for side in range(2):
-            copies = load(index, side)
-            if len(copies) == 1:
-                copies[0].start()
-            else:
-                odd = odd_ref[0]
-                pl.when(odd == 0)(copies[0].start)
-                pl.when(odd != 0)(copies[1].start)
-    row = 0
-    for index, part in enumerate(parts):
-        for side in range(2):
-            load(index, side)[0].wait()
-        rows32[pl.ds(row, part[2])] = packed[pl.ds(row, part[2])].astype(f32)
-        row += part[2]
+            source = sources[cursor].at[side] if arrays == 1 else sources[cursor + side]
+            copy = pltpu.make_async_copy(
+                source, packed.at[side, pl.ds(row, rows)], in_sem.at[index, side]
+            )
+            copy.start()
+            loads.append((copy, side, row, rows))
+        cursor += arrays
+        row += rows
+    for copy, side, row, rows in loads:
+        copy.wait()
+        rows32[side, pl.ds(row, rows)] = packed[side, pl.ds(row, rows)].astype(f32)
 
     lane = lax.broadcasted_iota(jnp.int32, (GROUP, LANES), 1)
     sub = lax.broadcasted_iota(jnp.int32, (GROUP, LANES), 0)
@@ -192,7 +215,7 @@
                 halves = [
                     jnp.where(
                         keep,
-                        jnp.broadcast_to(rows32[d, side, pl.ds(position, 1), :], (GROUP, LANES)),
+                        jnp.broadcast_to(rows32[side, d, pl.ds(position, 1), :], (GROUP, LANES)),
                         zero,
                     )
                     for side in range(2)
@@ -245,11 +268,11 @@
         copy.wait()
 
 
-def cross_part(odd, near, far, lag_table, parts, sources, prior, local_rows, row_count):
+def cross_part(near, far, lag_table, parts, sources, prior, local_rows, row_count):
     total = sum(part[2] for part in parts)
     any_space = pl.BlockSpec(memory_space=pl.ANY)
-    operands = [odd, near, far, lag_table] + sources
-    specs = [pl.BlockSpec(memory_space=pltpu.SMEM)] + [pl.BlockSpec(memory_space=pltpu.VMEM)] * 3
+    operands = [near, far, lag_table] + sources
+    specs = [pl.BlockSpec(memory_space=pltpu.VMEM)] * 3
     specs += [pl.BlockSpec(memory_space=pltpu.MemorySpace.HBM)] * len(sources)
     aliases = {}
     if prior is not None:
@@ -262,8 +285,8 @@
         in_specs=specs,
         out_specs=any_space,
         scratch_shapes=[
-            pltpu.VMEM((total, 2, OCTETS, LANES), bf16),
-            pltpu.VMEM((total, 2, OCTETS, LANES), f32),
+            pltpu.VMEM((2, total, OCTETS, LANES), bf16),
+            pltpu.VMEM((2, total, OCTETS, LANES), f32),
             pltpu.VMEM((2, total // 2, 2 * HALF, 2 * LANES), bf16),
             pltpu.VMEM((2, 2, LAGS, LANES), f32),
             pltpu.VMEM((total, row_count, LAGS), bf16),
@@ -271,7 +294,7 @@
             pltpu.SemaphoreType.DMA((total,)),
         ],
         input_output_aliases=aliases,
-        compiler_params=pltpu.CompilerParams(vmem_limit_bytes=40 << 20),
+        compiler_params=pltpu.CompilerParams(vmem_limit_bytes=32 << 20),
         cost_estimate=pl.CostEstimate(
             flops=total * 600_000_000 // 4, bytes_accessed=12 << 20, transcendentals=0
         ),
@@ -295,7 +318,7 @@
     me = lax.axis_index("tm").astype(jnp.int32)
     odd = lax.rem(lax.axis_index("chan"), 2).astype(jnp.int32)
 
-    *pieces, near = spectra(
+    *pieces, give, near = spectra(
         me[None], signal, valid_flags.T, forward_rows(), taper_row(), chunks, local_rows
     )
 
@@ -308,28 +331,27 @@
 
     axes = ("chan", "tm")
     two_away = [lax.ppermute(x, axes, back(2, i % 2)) for i, x in enumerate(pieces)]
-    one_away = [
-        lax.ppermute(x, axes, [q for q in back(1, i % 2) if q[0] // owner_count % 2 == 1])
-        for i, x in enumerate(pieces)
-    ]
-    far = lax.ppermute(near, "tm", [(0, 1), (1, 0)])
-    onward = [(b, b + 1) for b in range(0, blocks, 2)]
-    relayed = [lax.ppermute(x, "chan", onward) for x in two_away]
+    other = [(t, 1 - t) for t in range(owner_count)]
+    taken = lax.ppermute(give, "tm", other)
+    far = lax.ppermute(near, "tm", other)
+    swap = [(b, b - 1 if b % 2 else b + 1) for b in range(blocks)]
 
     lag_table = lag_rows(span_windows * owner_count)
     out = None
     starts = np.cumsum([0] + list(chunks))
+    one_away = []
     for k in range(len(chunks) + 1):
         parts, sources = [], []
         if k < len(chunks):
-            parts.append((1, int(starts[k]), chunks[k], 1))
-            sources += two_away[2 * k : 2 * k + 2]
+            sent = two_away[2 * k : 2 * k + 2]
+            load = payload(odd[None], pieces[2 * k], taken, *sent, int(starts[k]))
+            one_away.append(lax.ppermute(load, "chan", swap))
+            parts.append((1, int(starts[k]), chunks[k], 2))
+            sources += sent
         if k > 0:
-            parts.append((0, int(starts[k - 1]), chunks[k - 1], 2))
-            sources += one_away[2 * k - 2 : 2 * k] + relayed[2 * k - 2 : 2 * k]
-        out = cross_part(
-            odd[None], near, far, lag_table, parts, sources, out, local_rows, row_count
-        )
+            parts.append((0, int(starts[k - 1]), chunks[k - 1], 1))
+            sources.append(one_away[k - 1])
+        out = cross_part(near, far, lag_table, parts, sources, out, local_rows, row_count)
     return out
 
 

time: 113 us -> 108 us (0.956)
  starting transfers between devices: 35.5 us -> 14.5 us
  Pallas kernels: 43.2 us -> 55.6 us
  waiting for transfers between devices: 25.5 us -> 32.2 us
  local copies, waits for them, and re-layouts: 7.37 us -> 5.06 us
    ppermute x13 -> x5, starting transfers between devices: 25.9 us -> 4.3 us  [the longest x3 3.74 us: local(): one_away.append(lax.ppermute(load, 'chan', swap))]
    pallas_call x4, Pallas kernels: 33.3 us -> 43.3 us  [cross_part(): pl.pallas_call(functools.partial(cross_kernel, tuple(parts), row_count, p...]
    ppermute x6, waiting for transfers between devices: 25.4 us -> 32.2 us  [local(): lax.ppermute(x, axes, back(2, i % 2))]
    unnamed x16 -> x10, local copies, waits for them, and re-layouts: 7.37 us -> 5.06 us
    pallas_call x0 -> x3, Pallas kernels: none -> 2.1 us  [payload(): pl.pallas_call(functools.partial(payload_kernel, first, keep.shape[0]), o...]
  transfers between devices with their start and end apart: 19 -> 11, of which waited for: 1 -> 3; matrix products, arithmetic and copies ran while one was open for 0% -> 0% of each run, Pallas kernels for 24% -> 34%
where the time goes in v1:
time: 108 us
  Pallas kernels  55.6 us (51%)
  waiting for transfers between devices  32.2 us (30%)
  starting transfers between devices  14.5 us (13%)
  local copies, waits for them, and re-layouts  5.06 us (5%)
    pallas_call x4, Pallas kernels, cross_part(): pl.pallas_call(functools.partial(cross_kernel, tuple(parts), row_count, p...  43.3 us
    ppermute x6, waiting for transfers between devices, local(): lax.ppermute(x, axes, back(2, i % 2))  32.2 us
    pallas_call x1, Pallas kernels, spectra(): pl.pallas_call(functools.partial(spectra_kernel, chunks, half), out_shape...  10.3 us
    ppermute x6, starting transfers between devices, local(): lax.ppermute(x, axes, back(2, i % 2))  10.2 us
    unnamed x10, local copies, waits for them, and re-layouts  5.06 us
    ppermute x3, starting transfers between devices, local(): one_away.append(lax.ppermute(load, 'chan', swap))  3.74 us
  transfers between devices with their start and end apart: 11, of which 3 were waited for; matrix products, arithmetic and copies ran while one was open for 0% of the time, Pallas kernels for 34%

profile of v1, /device:TPU:0, one launch (start us, length us, event | category | flops | bytes accessed | tf_op | source)
XLA Modules:
  0.0 107.7 jit_solution(7799035063225063073)
XLA Ops:
  0.0 0.0 copy-start.1
  0.0 10.3 %spectra.1 = (bf16[20,64,128]{2,1,0:T(8,128)(2,1)}, bf16[20,64,128]{2,1,0:T(8,128)(2,1)}, bf16[20,64,128]{2,1,0:T(8,128)(2,1)}, bf16[20,64,128]{2,1,0:T(8,128)(2...) custom-call(s32[1]{0:T(128)} %bitcast.me_ref, ...), custom_call_target="tpu_custom_call" | custom-call | flops 2147483648 | bytes 12582912 | tf_op jit(solution)/shard_map/spectra/pallas_call | solution.py:126
  10.3 0.5 collective-permute-start
  10.8 0.1 collective-permute-start.1
  10.8 4.7 %collective-permute-start.9 = (bf16[20,64,128]{2,1,0:T(8,128)(2,1)}, bf16[20,64,128]{2,1,0:T(8,128)(2,1)S(1)}, u32[]{:S(2)}, u32[]{:S(2)}) collective-permute-start(bf16[20,64,128]{2,1,0:T(8,128)(2,1)} %get-tuple-element.20), channel_id=1, source_target_pairs={{0,13},{1,12},{2,15},{3,14},{4,1},{5,0},{6,3},{7,2},{8,5},{9,4},{1... | collective-permute-start | bytes 983048 | tf_op jit(solution)/shard_map/ppermute | solution.py:333
  15.6 0.4 collective-permute-start.8
  16.0 0.2 collective-permute-start.3
  16.2 7.8 %collective-permute-done.9.far_side.refs_4_ = bf16[20,64,128]{2,1,0:T(8,128)(2,1)S(1)} collective-permute-done((bf16[20,64,128]{2,1,0:T(8,128)(2,1)}, bf16[20,64,128]{2,1,0:T(8,128)(2,1)S(1)}, u32[]{:S(2)}, u32[]{:S(2)}) %collective-permute-start.9) | collective-permute-done | bytes 327712 | tf_op jit(solution)/shard_map/ppermute | solution.py:333
  24.0 7.0 %collective-permute-done.8.near_side.refs_3_ = bf16[20,64,128]{2,1,0:T(8,128)(2,1)S(1)} collective-permute-done((bf16[20,64,128]{2,1,0:T(8,128)(2,1)}, bf16[20,64,128]{2,1,0:T(8,128)(2,1)S(1)}, u32[]{:S(2)}, u32[]{:S(2)}) %collective-permute-start.8) | collective-permute-done | bytes 327712 | tf_op jit(solution)/shard_map/ppermute | solution.py:333
  31.0 0.0 collective-permute-done.1.taken
  31.0 0.0 copy-start.3
  31.0 1.0 copy-done.3
  32.0 0.4 payload.5
  32.4 1.6 %collective-permute-start.10 = (bf16[2,20,64,128]{3,2,1,0:T(8,128)(2,1)S(1)}, bf16[2,20,64,128]{3,2,1,0:T(8,128)(2,1)S(1)}, u32[]{:S(2)}, u32[]{:S(2)}) collective-permute-start(bf16[2,20,64,128]{3,2,1,0:T(8,128)(2,1)S(1)} %payload.5), channel_id=1, source_target_pairs={{0,2},{2,0},{4,6},{6,4},{8,10},{10,8},{12,14},{14,12},{1,3},{3,1},... | collective-permute-start | bytes 1966088 | tf_op jit(solution)/shard_map/ppermute | solution.py:348
  34.0 3.1 %collective-permute-start.6 = (bf16[20,64,128]{2,1,0:T(8,128)(2,1)}, bf16[20,64,128]{2,1,0:T(8,128)(2,1)S(1)}, u32[]{:S(2)}, u32[]{:S(2)}) collective-permute-start(bf16[20,64,128]{2,1,0:T(8,128)(2,1)} %get-tuple-element.18), channel_id=1, source_target_pairs={{0,13},{1,12},{2,15},{3,14},{4,1},{5,0},{6,3},{7,2},{8,5},{9,4},{1... | collective-permute-start | bytes 983048 | tf_op jit(solution)/shard_map/ppermute | solution.py:333
  37.1 1.1 collective-permute-start.5
  38.2 0.0 collective-permute-done.3.far_side.refs_4_
  38.2 0.7 collective-permute-start.2
  38.9 17.4 %collective-permute-done.2.near_side.refs_3_ = bf16[12,64,128]{2,1,0:T(8,128)(2,1)S(1)} collective-permute-done((bf16[12,64,128]{2,1,0:T(8,128)(2,1)}, bf16[12,64,128]{2,1,0:T(8,128)(2,1)S(1)}, u32[]{:S(2)}, u32[]{:S(2)}) %collective-permute-start.2) | collective-permute-done | bytes 196640 | tf_op jit(solution)/shard_map/ppermute | solution.py:333
  56.3 0.0 copy-start.4
  56.3 0.9 copy-done.4
  57.2 1.0 payload.3
  58.3 0.6 collective-permute-start.4
  58.9 0.0 collective-permute-done.6.far_side.refs_4_
  58.9 0.0 collective-permute-done.5.near_side.refs_3_
  58.9 0.0 copy-start.2
  58.9 1.0 copy-done.2
  59.8 0.6 payload.4
  60.5 1.6 %collective-permute-start.7 = (bf16[2,20,64,128]{3,2,1,0:T(8,128)(2,1)S(1)}, bf16[2,20,64,128]{3,2,1,0:T(8,128)(2,1)S(1)}, u32[]{:S(2)}, u32[]{:S(2)}) collective-permute-start(bf16[2,20,64,128]{3,2,1,0:T(8,128)(2,1)S(1)} %payload.4), channel_id=1, source_target_pairs={{0,2},{2,0},{4,6},{6,4},{8,10},{10,8},{12,14},{14,12},{1,3},{3,1},... | collective-permute-start | bytes 1966088 | tf_op jit(solution)/shard_map/ppermute | solution.py:348
  62.1 0.0 collective-permute-done.refs_1_
  62.1 0.0 copy-done.1
  62.1 0.0 copy-start
  62.1 2.2 %copy-done = bf16[64,128,256]{2,1,0:T(8,128)(2,1)S(1)} copy-done((bf16[64,128,256]{2,1,0:T(8,128)(2,1)S(1)}, bf16[64,128,256]{2,1,0:T(8,128)(2,1)}, u32[]{:S(2)}) %copy-start) | copy-done | bytes 4194328
  64.3 9.5 %cross.4.refs_6_ = bf16[2,52,104,512]{3,2,1,0:T(8,128)(2,1)} custom-call(bf16[64,128,256]{2,1,0:T(8,128)(2,1)S(1)} %copy-done, bf16[64,128,256]{2,1,0:T(8,128)(2,1)} %collective-permute-done.refs_1_, bf16[2,256,512]{2,1,0:T(8,128)(2,1)S(1)} %copy-done.1, bf16[20,64,128]{2,1,0:T(8,128)(2,1)S(1)} %collective-permute-done.8.near_side.refs_3_, ...), custom_call_target="tpu_custom_call" | custom-call | flops 3000000000 | bytes 12582912 | tf_op jit(solution)/shard_map/cross/pallas_call | solution.py:282
  73.8 0.0 collective-permute-done.10.refs_5_
  73.8 13.2 %cross.5.refs_6_ = bf16[2,52,104,512]{3,2,1,0:T(8,128)(2,1)} custom-call(bf16[64,128,256]{2,1,0:T(8,128)(2,1)S(1)} %copy-done, bf16[64,128,256]{2,1,0:T(8,128)(2,1)} %collective-permute-done.refs_1_, bf16[2,256,512]{2,1,0:T(8,128)(2,1)S(1)} %copy-done.1, ...), custom_call_target="tpu_custom_call", output_to_operand_aliasing={{}: (6, {})} | custom-call | flops 6000000000 | bytes 12582912 | tf_op jit(solution)/shard_map/cross/pallas_call | solution.py:282
  87.0 0.0 collective-permute-done.7.refs_5_
  87.0 12.0 %cross.6.refs_4_ = bf16[2,52,104,512]{3,2,1,0:T(8,128)(2,1)} custom-call(bf16[64,128,256]{2,1,0:T(8,128)(2,1)S(1)} %copy-done, bf16[64,128,256]{2,1,0:T(8,128)(2,1)} %collective-permute-done.refs_1_, bf16[2,256,512]{2,1,0:T(8,128)(2,1)S(1)} %copy-done.1, ...), custom_call_target="tpu_custom_call", output_to_operand_aliasing={{}: (6, {})} | custom-call | flops 4800000000 | bytes 12582912 | tf_op jit(solution)/shard_map/cross/pallas_call | solution.py:282
  99.0 0.0 collective-permute-done.4.refs_3_
  99.1 8.5 %cross.7 = bf16[2,52,104,512]{3,2,1,0:T(8,128)(2,1)} custom-call(bf16[64,128,256]{2,1,0:T(8,128)(2,1)S(1)} %copy-done, bf16[64,128,256]{2,1,0:T(8,128)(2,1)} %collective-permute-done.refs_1_, bf16[2,256,512]{2,1,0:T(8,128)(2,1)S(1)} %copy-done.1, bf16[2,12,64,128]{3,2,1,0:T(8,128)(2,1)S(1)} %collective-permute-done.4.refs_3_, ...), custom_call_target="tpu_custom_call", output_to_operand_aliasing={{}: (4, {})} | custom-call | flops 1800000000 | bytes 12582912 | tf_op jit(solution)/shard_map/cross/pallas_call | solution.py:282
Async XLA Ops:
  0.0 62.1 %copy-start.1 = (bf16[2,256,512]{2,1,0:T(8,128)(2,1)S(1)}, bf16[2,256,512]{2,1,0:T(8,128)(2,1)}, u32[]{:S(2)}) copy-start(bf16[2,256,512]{2,1,0:T(8,128)(2,1)} %constant.25.refs_2_) | copy-start | bytes 1572868
  10.3 51.8 %collective-permute-start = (bf16[64,128,256]{2,1,0:T(8,128)(2,1)}, bf16[64,128,256]{2,1,0:T(8,128)(2,1)}, u32[]{:S(2)}, u32[]{:S(2)}) collective-permute-start(bf16[64,128,256]{2,1,0:T(8,128)(2,1)} %get-tuple-element.13.refs_0_), channel_id=1, source_target_pairs={{0,1},{1,0},{2,3},{3,2},{4,5},{5,4},{6,7},{7,6},{8,9},{9,8},{10,11... | collective-permute-start | bytes 12582920 | tf_op jit(solution)/shard_map/ppermute | solution.py:336
  10.8 20.2 %collective-permute-start.1 = (bf16[52,64,128]{2,1,0:T(8,128)(2,1)}, bf16[52,64,128]{2,1,0:T(8,128)(2,1)S(1)}, u32[]{:S(2)}, u32[]{:S(2)}) collective-permute-start(bf16[52,64,128]{2,1,0:T(8,128)(2,1)} %get-tuple-element.15), channel_id=1, source_target_pairs={{0,1},{1,0},{2,3},{3,2},{4,5},{5,4},{6,7},{7,6},{8,9},{9,8},{10,11... | collective-permute-start | bytes 2555912 | tf_op jit(solution)/shard_map/ppermute | solution.py:335
  10.8 13.1 %collective-permute-start.9 = (bf16[20,64,128]{2,1,0:T(8,128)(2,1)}, bf16[20,64,128]{2,1,0:T(8,128)(2,1)S(1)}, u32[]{:S(2)}, u32[]{:S(2)}) collective-permute-start(bf16[20,64,128]{2,1,0:T(8,128)(2,1)} %get-tuple-element.20), channel_id=1, source_target_pairs={{0,13},{1,12},{2,15},{3,14},{4,1},{5,0},{6,3},{7,2},{8,5},{9,4},{1... | collective-permute-start | bytes 983048 | tf_op jit(solution)/shard_map/ppermute | solution.py:333
  15.6 15.4 %collective-permute-start.8 = (bf16[20,64,128]{2,1,0:T(8,128)(2,1)}, bf16[20,64,128]{2,1,0:T(8,128)(2,1)S(1)}, u32[]{:S(2)}, u32[]{:S(2)}) collective-permute-start(bf16[20,64,128]{2,1,0:T(8,128)(2,1)} %get-tuple-element.19.keep), channel_id=1, source_target_pairs={{0,12},{1,13},{2,14},{3,15},{4,0},{5,1},{6,2},{7,3},{8,4},{9,5},{1... | collective-permute-start | bytes 983048 | tf_op jit(solution)/shard_map/ppermute | solution.py:333
  16.0 22.2 %collective-permute-start.3 = (bf16[12,64,128]{2,1,0:T(8,128)(2,1)}, bf16[12,64,128]{2,1,0:T(8,128)(2,1)S(1)}, u32[]{:S(2)}, u32[]{:S(2)}) collective-permute-start(bf16[12,64,128]{2,1,0:T(8,128)(2,1)} %get-tuple-element.16), channel_id=1, source_target_pairs={{0,13},{1,12},{2,15},{3,14},{4,1},{5,0},{6,3},{7,2},{8,5},{9,4},{1... | collective-permute-start | bytes 589832 | tf_op jit(solution)/shard_map/ppermute | solution.py:333
  31.0 1.0 copy-start.3
  32.4 41.4 %collective-permute-start.10 = (bf16[2,20,64,128]{3,2,1,0:T(8,128)(2,1)S(1)}, bf16[2,20,64,128]{3,2,1,0:T(8,128)(2,1)S(1)}, u32[]{:S(2)}, u32[]{:S(2)}) collective-permute-start(bf16[2,20,64,128]{3,2,1,0:T(8,128)(2,1)S(1)} %payload.5), channel_id=1, source_target_pairs={{0,2},{2,0},{4,6},{6,4},{8,10},{10,8},{12,14},{14,12},{1,3},{3,1},... | collective-permute-start | bytes 1966088 | tf_op jit(solution)/shard_map/ppermute | solution.py:348
  34.0 24.8 %collective-permute-start.6 = (bf16[20,64,128]{2,1,0:T(8,128)(2,1)}, bf16[20,64,128]{2,1,0:T(8,128)(2,1)S(1)}, u32[]{:S(2)}, u32[]{:S(2)}) collective-permute-start(bf16[20,64,128]{2,1,0:T(8,128)(2,1)} %get-tuple-element.18), channel_id=1, source_target_pairs={{0,13},{1,12},{2,15},{3,14},{4,1},{5,0},{6,3},{7,2},{8,5},{9,4},{1... | collective-permute-start | bytes 983048 | tf_op jit(solution)/shard_map/ppermute | solution.py:333
  37.1 21.7 %collective-permute-start.5 = (bf16[20,64,128]{2,1,0:T(8,128)(2,1)}, bf16[20,64,128]{2,1,0:T(8,128)(2,1)S(1)}, u32[]{:S(2)}, u32[]{:S(2)}) collective-permute-start(bf16[20,64,128]{2,1,0:T(8,128)(2,1)} %get-tuple-element.17.keep), channel_id=1, source_target_pairs={{0,12},{1,13},{2,14},{3,15},{4,0},{5,1},{6,2},{7,3},{8,4},{9,5},{1... | collective-permute-start | bytes 983048 | tf_op jit(solution)/shard_map/ppermute | solution.py:333
  38.2 18.1 %collective-permute-start.2 = (bf16[12,64,128]{2,1,0:T(8,128)(2,1)}, bf16[12,64,128]{2,1,0:T(8,128)(2,1)S(1)}, u32[]{:S(2)}, u32[]{:S(2)}) collective-permute-start(bf16[12,64,128]{2,1,0:T(8,128)(2,1)} %get-tuple-element.14.keep), channel_id=1, source_target_pairs={{0,12},{1,13},{2,14},{3,15},{4,0},{5,1},{6,2},{7,3},{8,4},{9,5},{1... | collective-permute-start | bytes 589832 | tf_op jit(solution)/shard_map/ppermute | solution.py:333
  56.3 0.9 copy-start.4
  58.3 40.8 %collective-permute-start.4 = (bf16[2,12,64,128]{3,2,1,0:T(8,128)(2,1)S(1)}, bf16[2,12,64,128]{3,2,1,0:T(8,128)(2,1)S(1)}, u32[]{:S(2)}, u32[]{:S(2)}) collective-permute-start(bf16[2,12,64,128]{3,2,1,0:T(8,128)(2,1)S(1)} %payload.3), channel_id=1, source_target_pairs={{0,2},{2,0},{4,6},{6,4},{8,10},{10,8},{12,14},{14,12},{1,3},{3,1},... | collective-permute-start | bytes 1179656 | tf_op jit(solution)/shard_map/ppermute | solution.py:348
  58.9 1.0 copy-start.2
  60.5 26.5 %collective-permute-start.7 = (bf16[2,20,64,128]{3,2,1,0:T(8,128)(2,1)S(1)}, bf16[2,20,64,128]{3,2,1,0:T(8,128)(2,1)S(1)}, u32[]{:S(2)}, u32[]{:S(2)}) collective-permute-start(bf16[2,20,64,128]{3,2,1,0:T(8,128)(2,1)S(1)} %payload.4), channel_id=1, source_target_pairs={{0,2},{2,0},{4,6},{6,4},{8,10},{10,8},{12,14},{14,12},{1,3},{3,1},... | collective-permute-start | bytes 1966088 | tf_op jit(solution)/shard_map/ppermute | solution.py:348
  62.1 2.2 %copy-start = (bf16[64,128,256]{2,1,0:T(8,128)(2,1)S(1)}, bf16[64,128,256]{2,1,0:T(8,128)(2,1)}, u32[]{:S(2)}) copy-start(bf16[64,128,256]{2,1,0:T(8,128)(2,1)} %get-tuple-element.13.refs_0_) | copy-start | bytes 12582916

commit v2 on v1

--- a/solution.py
+++ b/solution.py
@@ -20,7 +20,7 @@
 GROUP = 8
 OCTETS = BINS // GROUP
 STEPS = OCTETS // 4
-ROWS_PER_CHUNK = (20, 20, 12)
+ROWS_PER_CHUNK = (14, 14, 12, 12)
 
 f32 = jnp.float32
 bf16 = jnp.bfloat16
@@ -62,81 +62,216 @@
     return (0.5 - 0.5 * np.cos(2.0 * np.pi * np.arange(WINDOW) / WINDOW)).astype(np.float32)[None]
 
 
-def spectra_kernel(chunks, half, me_ref, signal_ref, flags_ref, table_ref, taper_ref, *refs):
-    outs, (tap, rows32, live) = refs[:-3], refs[-3:]
-    piece_refs, give_ref, own_ref = outs[:-2], outs[-2], outs[-1]
-    row_count = signal_ref.shape[0]
-    spans = signal_ref.shape[1] // WINDOW
+def window_order(spans):
+    return [w for start in range(2) for w in range(start, spans, 2)]
+
+
+def table_copies(table_hbm, table, sem):
+    return [
+        pltpu.make_async_copy(
+            table_hbm.at[pl.ds(g * 256, 256)], table.at[pl.ds(g * 256, 256)], sem.at[g]
+        )
+        for g in range(4)
+    ]
+
+
+def taper_rows(x, taper):
+    mean_square = jnp.mean(x * x, axis=1, keepdims=True)
+    return (x * lax.rsqrt(mean_square + epsilon) * taper).astype(bf16)
+
+
+def transform(table, tap, g):
+    return lax.dot_general(
+        table[g * 256 : (g + 1) * 256, :],
+        tap[...],
+        (((1,), (1,)), ((), ())),
+        preferred_element_type=f32,
+    )
+
+
+def first_kernel(
+    rows, half, bounds, me_ref, signal_hbm, live_ref, table_hbm, taper_ref,
+    same_ref, cross_ref, signal, tap, table, rows32, in_sem, table_sem,
+):
+    spans = signal.shape[1] // WINDOW
+    width = LANES // 2
+    loads, held = [], 0
+    for h, (low, high) in enumerate(bounds):
+        copy = pltpu.make_async_copy(
+            signal_hbm.at[pl.ds(low, high - low)], signal.at[pl.ds(held, high - low)], in_sem.at[h]
+        )
+        copy.start()
+        loads.append(copy)
+        held += high - low
+    tables = table_copies(table_hbm, table, table_sem)
+    for copy in tables:
+        copy.start()
+    taper = taper_ref[...]
+    tap[...] = jnp.zeros_like(tap)
+    for copy in loads:
+        copy.wait()
+    for w in range(spans):
+        x = signal[:, w * WINDOW : (w + 1) * WINDOW]
+        tap[pl.ds(w * width, held), :] = taper_rows(x, taper)
+    for g in range(4):
+        tables[g].wait()
+        result = transform(table, tap, g)
+        for o in range(16):
+            position = g * 16 + o
+            plain = jnp.concatenate(
+                [
+                    result[o * 16 : o * 16 + 16, v * LANES : (v + 1) * LANES] * live_ref[v : v + 1, :]
+                    for v in range(spans // 2)
+                ],
+                axis=0,
+            )
+            flipped = jnp.transpose(plain)
+            for c in range(0, held, 8):
+                rows32[pl.ds(c * OCTETS + position, 8, stride=OCTETS), :] = jnp.concatenate(
+                    [flipped[c : c + 8], flipped[width + c : width + c + 8]], axis=1
+                )
+    me = me_ref[0]
+    places = (-bounds[0][0], bounds[0][1] - bounds[0][0] + half - bounds[1][0])
+    for side, out in enumerate((same_ref, cross_ref)):
+        place = jnp.where(me == side, places[0], places[1])
+        block = rows32[pl.ds(pl.multiple_of(place * OCTETS, OCTETS), rows * OCTETS), :]
+        out[...] = block.astype(bf16).reshape(rows, OCTETS, LANES)
+
+
+def first_flags(flags, rows, half):
+    width = LANES // 2
+    parts = [flags[:, h * half // 8 * 8 : -(-(h * half + rows) // 8) * 8] for h in range(2)]
+    held = jnp.concatenate(parts, axis=1)
+    held = jnp.pad(held, ((0, 0), (0, width - held.shape[1])))
+    return held.reshape(flags.shape[0] // 2, LANES)
+
+
+def first_spectra(me, signal, live, table, taper, rows, half):
+    spans = signal.shape[1] // WINDOW
+    bounds = []
+    for h in range(2):
+        bounds.append((h * half // 8 * 8, -(-(h * half + rows) // 8) * 8))
+    held = sum(high - low for low, high in bounds)
+    assert held <= LANES // 2
+    vmem = pl.BlockSpec(memory_space=pltpu.VMEM)
+    hbm = pl.BlockSpec(memory_space=pltpu.MemorySpace.HBM)
+    return pl.pallas_call(
+        functools.partial(first_kernel, rows, half, tuple(bounds)),
+        out_shape=[jax.ShapeDtypeStruct((rows, OCTETS, LANES), bf16)] * 2,
+        in_specs=[pl.BlockSpec(memory_space=pltpu.SMEM), hbm, vmem, hbm, vmem],
+        out_specs=[vmem] * 2,
+        scratch_shapes=[
+            pltpu.VMEM((held, spans * WINDOW), f32),
+            pltpu.VMEM((spans * LANES // 2, WINDOW), bf16),
+            pltpu.VMEM((WINDOW, WINDOW), bf16),
+            pltpu.VMEM((held * OCTETS, LANES), f32),
+            pltpu.SemaphoreType.DMA((2,)),
+            pltpu.SemaphoreType.DMA((4,)),
+        ],
+        compiler_params=pltpu.CompilerParams(vmem_limit_bytes=32 << 20),
+        cost_estimate=pl.CostEstimate(flops=WINDOW**3, bytes_accessed=6 << 20, transcendentals=0),
+        name="first",
+    )(me, signal, live, table, taper)
+
+
+def spectra_kernel(
+    chunks, half, me_ref, signal_hbm, flags_ref, table_hbm, taper_ref, *refs
+):
+    count = 2 * len(chunks) - 2
+    pieces, (give_hbm, own_hbm) = refs[:count], refs[count : count + 2]
+    signal, tap, table, rows32, live, own, give, in_sem, table_sem, own_sem, give_sem = refs[count + 2 :]
+    row_count = signal.shape[0]
+    spans = signal.shape[1] // WINDOW
+    loads = []
+    for w in range(spans):
+        part = pl.ds(w * WINDOW, WINDOW)
+        copy = pltpu.make_async_copy(signal_hbm.at[:, part], signal.at[:, part], in_sem.at[w])
+        copy.start()
+        loads.append(copy)
+    tables = table_copies(table_hbm, table, table_sem)
+    for copy in tables:
+        copy.start()
     taper = taper_ref[...]
     tap[...] = jnp.zeros_like(tap)
     live[...] = jnp.zeros_like(live)
     live[:, :row_count] = flags_ref[...].astype(f32)
     for w in range(spans):
-        x = signal_ref[:, w * WINDOW : (w + 1) * WINDOW]
-        mean_square = jnp.mean(x * x, axis=1, keepdims=True)
-        scale = lax.rsqrt(mean_square + epsilon)
-        tap[pl.ds(w * LANES, row_count), :] = (x * scale * taper).astype(bf16)
+        loads[w].wait()
+        x = signal[:, w * WINDOW : (w + 1) * WINDOW]
+        tap[pl.ds(w * LANES, row_count), :] = taper_rows(x, taper)
+    order = window_order(spans)
+    leaving = []
     for g in range(4):
-        result = lax.dot_general(
-            table_ref[g * 256 : (g + 1) * 256, :],
-            tap[...],
-            (((1,), (1,)), ((), ())),
-            preferred_element_type=f32,
-        )
+        tables[g].wait()
+        result = transform(table, tap, g)
         for o in range(16):
             position = g * 16 + o
-            tiles = [
+            real, imag = [
                 [
                     result[o * 16 + s * 8 : o * 16 + s * 8 + 8, w * LANES : (w + 1) * LANES]
                     * live[w : w + 1, :]
-                    for w in range(spans)
+                    for w in order
                 ]
                 for s in range(2)
             ]
-            real, imag = tiles
-            plain = jnp.concatenate([p for w in range(spans) for p in (real[w], imag[w])], axis=0)
-            turned = jnp.concatenate([p for w in range(spans) for p in (imag[w], -real[w])], axis=0)
-            own_ref[position, :, :LANES] = plain.astype(bf16)
-            own_ref[position, :, LANES:] = turned.astype(bf16)
+            plain = jnp.concatenate([p for pair in zip(real, imag) for p in pair], axis=0)
+            turned = jnp.concatenate([p for r, i in zip(real, imag) for p in (i, -r)], axis=0)
+            own[position, :, :LANES] = plain.astype(bf16)
+            own[position, :, LANES:] = turned.astype(bf16)
             flipped = jnp.transpose(plain)
             for c in range(0, row_count, 8):
                 rows32[pl.ds(c * OCTETS + position, 8, stride=OCTETS), :] = flipped[c : c + 8]
+        part = pl.ds(g * 16, 16)
+        leaving.append(pltpu.make_async_copy(own.at[part], own_hbm.at[part], own_sem.at[g]))
+        leaving[-1].start()
     me = me_ref[0]
-    start = 0
-    for k, rows in enumerate(chunks):
+
+    def block(side, start, rows):
+        first = (me * half if side == 0 else (1 - me) * half) + start
+        value = rows32[pl.ds(pl.multiple_of(first * OCTETS, OCTETS), rows * OCTETS), :]
+        return value.astype(bf16).reshape(rows, OCTETS, LANES)
+
+    give[...] = block(1, 0, half)
+    leaving.append(pltpu.make_async_copy(give, give_hbm, give_sem))
+    leaving[-1].start()
+    start = chunks[0]
+    for k, rows in enumerate(chunks[1:]):
         for side in range(2):
-            first = (me * half if side == 0 else (1 - me) * half) + start
-            block = rows32[pl.ds(pl.multiple_of(first * OCTETS, OCTETS), rows * OCTETS), :]
-            piece_refs[2 * k + side][...] = block.astype(bf16).reshape(rows, OCTETS, LANES)
+            pieces[2 * k + side][...] = block(side, start, rows)
         start += rows
-    block = rows32[pl.ds(pl.multiple_of((1 - me) * half * OCTETS, OCTETS), half * OCTETS), :]
-    give_ref[...] = block.astype(bf16).reshape(half, OCTETS, LANES)
-
-
-def spectra(me, signal, valid_flags, table, taper, chunks, half):
+    for copy in leaving:
+        copy.wait()
+
+
+def spectra(me, signal, flags, table, taper, chunks, half):
     row_count = signal.shape[0]
     spans = signal.shape[1] // WINDOW
-    pieces = [
-        jax.ShapeDtypeStruct((rows, OCTETS, LANES), bf16)
-        for rows in chunks
-        for _ in range(2)
-    ] + [jax.ShapeDtypeStruct((half, OCTETS, LANES), bf16)]
-    own = jax.ShapeDtypeStruct((OCTETS, LANES, 2 * LANES), bf16)
+    shapes = [(rows, OCTETS, LANES) for rows in chunks[1:] for _ in range(2)]
+    give, own = (half, OCTETS, LANES), (OCTETS, LANES, 2 * LANES)
     vmem = pl.BlockSpec(memory_space=pltpu.VMEM)
+    hbm = pl.BlockSpec(memory_space=pltpu.MemorySpace.HBM)
     return pl.pallas_call(
         functools.partial(spectra_kernel, chunks, half),
-        out_shape=pieces + [own],
-        in_specs=[pl.BlockSpec(memory_space=pltpu.SMEM)] + [vmem] * 4,
-        out_specs=[vmem] * (len(pieces) + 1),
+        out_shape=[jax.ShapeDtypeStruct(shape, bf16) for shape in shapes + [give, own]],
+        in_specs=[pl.BlockSpec(memory_space=pltpu.SMEM), hbm, vmem, hbm, vmem],
+        out_specs=[vmem] * len(shapes) + [hbm] * 2,
         scratch_shapes=[
+            pltpu.VMEM((row_count, spans * WINDOW), f32),
             pltpu.VMEM((spans * LANES, WINDOW), bf16),
+            pltpu.VMEM((WINDOW, WINDOW), bf16),
             pltpu.VMEM((row_count * OCTETS, LANES), f32),
             pltpu.VMEM((spans, LANES), f32),
+            pltpu.VMEM(own, bf16),
+            pltpu.VMEM(give, bf16),
+            pltpu.SemaphoreType.DMA((spans,)),
+            pltpu.SemaphoreType.DMA((4,)),
+            pltpu.SemaphoreType.DMA((4,)),
+            pltpu.SemaphoreType.DMA,
         ],
-        compiler_params=pltpu.CompilerParams(vmem_limit_bytes=60 << 20),
+        compiler_params=pltpu.CompilerParams(vmem_limit_bytes=40 << 20),
         cost_estimate=pl.CostEstimate(flops=2 * WINDOW**3, bytes_accessed=12 << 20, transcendentals=0),
         name="spectra",
-    )(me, signal, valid_flags, table, taper)
+    )(me, signal, flags, table, taper)
 
 
 def payload_kernel(first, rows, odd_ref, keep, taken, near_side, far_side, out_ref, hold, in_sem, out_sem):
@@ -178,10 +313,11 @@
 
 def cross_kernel(parts, row_count, has_prior, *refs):
     source_count = sum(part[3] for part in parts)
-    near_ref, far_ref, lag_ref = refs[:3]
+    near_ref, far_hbm, lag_hbm = refs[:3]
     sources = refs[3 : 3 + source_count]
     rest = refs[3 + source_count + (1 if has_prior else 0) :]
-    out_ref, packed, rows32, cross, mixed, result, in_sem, out_sem = rest
+    out_ref, far_ref, lag_ref, packed, rows32, cross, mixed, result = rest[:8]
+    in_sem, far_sem, lag_sem, out_sem = rest[8:]
     total = sum(part[2] for part in parts)
     pairs = total // 2
 
@@ -196,6 +332,15 @@
             loads.append((copy, side, row, rows))
         cursor += arrays
         row += rows
+
+    def far_copy(m):
+        part = pl.ds(m * 4, 4)
+        return pltpu.make_async_copy(far_hbm.at[part], far_ref.at[part], far_sem.at[m])
+
+    for m in range(STEPS):
+        far_copy(m).start()
+    lag_copy = pltpu.make_async_copy(lag_hbm, lag_ref, lag_sem)
+    lag_copy.start()
     for copy, side, row, rows in loads:
         copy.wait()
         rows32[side, pl.ds(row, rows)] = packed[side, pl.ds(row, rows)].astype(f32)
@@ -207,6 +352,7 @@
     top = sub == 0
 
     def step(m, first):
+        far_copy(m).wait()
         products = []
         for j in range(4):
             position = m * 4 + j
@@ -249,6 +395,7 @@
     step(0, True)
     lax.fori_loop(1, STEPS, lambda m, c: (step(m, False), c)[1], 0)
 
+    lag_copy.wait()
     targets = [(part[0], part[1] + i) for part in parts for i in range(part[2])]
     out_copies = []
     for p in range(pairs):
@@ -272,8 +419,8 @@
     total = sum(part[2] for part in parts)
     any_space = pl.BlockSpec(memory_space=pl.ANY)
     operands = [near, far, lag_table] + sources
-    specs = [pl.BlockSpec(memory_space=pltpu.VMEM)] * 3
-    specs += [pl.BlockSpec(memory_space=pltpu.MemorySpace.HBM)] * len(sources)
+    specs = [pl.BlockSpec(memory_space=pltpu.VMEM)]
+    specs += [pl.BlockSpec(memory_space=pltpu.MemorySpace.HBM)] * (len(sources) + 2)
     aliases = {}
     if prior is not None:
         aliases = {len(operands): 0}
@@ -285,12 +432,16 @@
         in_specs=specs,
         out_specs=any_space,
         scratch_shapes=[
+            pltpu.VMEM(far.shape, bf16),
+            pltpu.VMEM(lag_table.shape, bf16),
             pltpu.VMEM((2, total, OCTETS, LANES), bf16),
             pltpu.VMEM((2, total, OCTETS, LANES), f32),
             pltpu.VMEM((2, total // 2, 2 * HALF, 2 * LANES), bf16),
             pltpu.VMEM((2, 2, LAGS, LANES), f32),
             pltpu.VMEM((total, row_count, LAGS), bf16),
             pltpu.SemaphoreType.DMA((len(parts), 2)),
+            pltpu.SemaphoreType.DMA((STEPS,)),
+            pltpu.SemaphoreType.DMA,
             pltpu.SemaphoreType.DMA((total,)),
         ],
         input_output_aliases=aliases,
@@ -318,9 +469,12 @@
     me = lax.axis_index("tm").astype(jnp.int32)
     odd = lax.rem(lax.axis_index("chan"), 2).astype(jnp.int32)
 
-    *pieces, give, near = spectra(
-        me[None], signal, valid_flags.T, forward_rows(), taper_row(), chunks, local_rows
-    )
+    flags = valid_flags.T
+    table, taper = forward_rows(), taper_row()
+    live = first_flags(flags.astype(f32), chunks[0], local_rows)
+    pieces = list(first_spectra(me[None], signal, live, table, taper, chunks[0], local_rows))
+    *more, give, near = spectra(me[None], signal, flags, table, taper, chunks, local_rows)
+    pieces += more
 
     def back(hops, side):
         return [

time: 108 us -> 129 us (1.19)
  Pallas kernels: 55.6 us -> 74.6 us
  waiting for transfers between devices: 32.2 us -> 23 us
  starting transfers between devices: 14.5 us -> 21.4 us
  local copies, waits for them, and re-layouts: 5.06 us -> 9.39 us
    pallas_call x4 -> x5, Pallas kernels: 43.3 us -> 57 us  [cross_part(): pl.pallas_call(functools.partial(cross_kernel, tuple(parts), row_count, p...]
    ppermute x6 -> x8, waiting for transfers between devices: 32.2 us -> 23 us  [local(): lax.ppermute(x, axes, back(2, i % 2))]
    pallas_call x0 -> x1, Pallas kernels: none -> 4.47 us  [first_spectra(): pl.pallas_call(functools.partial(first_kernel, rows, half, tuple(bounds))...]
    ppermute x6 -> x8, starting transfers between devices: 10.2 us -> 14.5 us  [local(): lax.ppermute(x, axes, back(2, i % 2))]
    unnamed x10 -> x20, local copies, waits for them, and re-layouts: 5.06 us -> 9.24 us
    pallas_call x3 -> x4, Pallas kernels: 2.1 us -> 4.64 us  [payload(): pl.pallas_call(functools.partial(payload_kernel, first, keep.shape[0]), o...]
    ppermute x3 -> x4, starting transfers between devices: 3.74 us -> 6.22 us  [local(): one_away.append(lax.ppermute(load, 'chan', swap))]
    pallas_call x1, Pallas kernels: 10.3 us -> 8.56 us  [spectra(): pl.pallas_call(functools.partial(spectra_kernel, chunks, half), out_shape...]
  transfers between devices with their start and end apart: 11 -> 14, of which waited for: 3 -> 6; matrix products, arithmetic and copies ran while one was open for 0% -> 0% of each run, Pallas kernels for 34% -> 44%
where the time goes in v2:
time: 129 us
  Pallas kernels  74.6 us (58%)
  waiting for transfers between devices  23 us (18%)
  starting transfers between devices  21.4 us (17%)
  local copies, waits for them, and re-layouts  9.39 us (7%)
    pallas_call x5, Pallas kernels, cross_part(): pl.pallas_call(functools.partial(cross_kernel, tuple(parts), row_count, p...  57 us
    ppermute x8, waiting for transfers between devices, local(): lax.ppermute(x, axes, back(2, i % 2))  23 us
    ppermute x8, starting transfers between devices, local(): lax.ppermute(x, axes, back(2, i % 2))  14.5 us
    unnamed x20, local copies, waits for them, and re-layouts  9.24 us
    pallas_call x1, Pallas kernels, spectra(): pl.pallas_call(functools.partial(spectra_kernel, chunks, half), out_shape...  8.56 us
    ppermute x4, starting transfers between devices, local(): one_away.append(lax.ppermute(load, 'chan', swap))  6.22 us
    pallas_call x4, Pallas kernels, payload(): pl.pallas_call(functools.partial(payload_kernel, first, keep.shape[0]), o...  4.64 us
    pallas_call x1, Pallas kernels, first_spectra(): pl.pallas_call(functools.partial(first_kernel, rows, half, tuple(bounds))...  4.47 us
  transfers between devices with their start and end apart: 14, of which 6 were waited for; matrix products, arithmetic and copies ran while one was open for 0% of the time, Pallas kernels for 44%

profile of v2, /device:TPU:0, one launch (start us, length us, event | category | flops | bytes accessed | tf_op | source)
XLA Modules:
  0.0 128.8 jit_solution(12668991116290399876)
XLA Ops:
  0.0 2.0 %copy-done.1 = f32[104,8192]{1,0:T(8,128)S(1)} copy-done((f32[104,8192]{1,0:T(8,128)S(1)}, f32[104,8192]{1,0:T(8,128)}, u32[]{:S(2)}) %copy-start.1) | copy-done | bytes 3407896
  2.0 1.6 %copy-done.3 = bf16[1024,1024]{1,0:T(8,128)(2,1)S(1)} copy-done((bf16[1024,1024]{1,0:T(8,128)(2,1)S(1)}, bf16[1024,1024]{1,0:T(8,128)(2,1)}, u32[]{:S(2)}) %copy-start.3) | copy-done | bytes 2097176
  3.6 0.7 copy-done.5
  4.3 0.7 copy-done.7
  5.0 8.6 %spectra.1 = (bf16[14,64,128]{2,1,0:T(8,128)(2,1)S(1)}, bf16[14,64,128]{2,1,0:T(8,128)(2,1)S(1)}, bf16[12,64,128]{2,1,0:T(8,128)(2,1)S(1)}, bf16[12,64,128]{2,1,...) custom-call(s32[1]{0:T(128)} %bitcast.me_ref, ...), custom_call_target="tpu_custom_call" | custom-call | flops 2147483648 | bytes 12582912 | tf_op jit(solution)/shard_map/spectra/pallas_call | solution.py:253
  13.6 0.6 collective-permute-start
  14.1 0.1 collective-permute-start.1
  14.2 0.1 slice.7
  14.3 0.1 select_maximum_fusion
  14.4 0.1 reshape.3.live_ref
  14.5 2.0 %copy-done.2 = f32[104,8192]{1,0:T(8,128)S(1)} copy-done((f32[104,8192]{1,0:T(8,128)S(1)}, f32[104,8192]{1,0:T(8,128)}, u32[]{:S(2)}) %copy-start.2) | copy-done | bytes 3407896
  16.4 1.6 %copy-done.4 = bf16[1024,1024]{1,0:T(8,128)(2,1)S(1)} copy-done((bf16[1024,1024]{1,0:T(8,128)(2,1)S(1)}, bf16[1024,1024]{1,0:T(8,128)(2,1)}, u32[]{:S(2)}) %copy-start.4) | copy-done | bytes 2097176
  18.0 0.7 copy-done.6
  18.7 4.5 %first.1 = (bf16[14,64,128]{2,1,0:T(8,128)(2,1)S(1)}, bf16[14,64,128]{2,1,0:T(8,128)(2,1)S(1)}) custom-call(s32[1]{0:T(128)} %bitcast.me_ref, f32[104,8192]{1,0:T(8,128)S(1)} %copy-done.2, f32[4,128]{1,0:T(4,128)S(1)} %reshape.3.live_ref, bf16[1024,1024]{1,0:T(8,128)(2,1)S(1)} %copy-done.4, f32[1,1024]{1,0:T(1,128)S(1)} %copy-done.6), custom_call_target="tpu_custom_call" | custom-call | flops 1073741824 | bytes 6291456 | tf_op jit(solution)/shard_map/first/pallas_call | solution.py:158
  23.2 5.1 %collective-permute-start.11 = (bf16[14,64,128]{2,1,0:T(8,128)(2,1)S(1)}, bf16[14,64,128]{2,1,0:T(8,128)(2,1)S(1)}, u32[]{:S(2)}, u32[]{:S(2)}) collective-permute-start(bf16[14,64,128]{2,1,0:T(8,128)(2,1)S(1)} %get-tuple-element.23.keep), channel_id=1, source_target_pairs={{0,12},{1,13},{2,14},{3,15},{4,0},{5,1},{6,2},{7,3},{8,4},{9,5},{1... | collective-permute-start | bytes 688136 | tf_op jit(solution)/shard_map/ppermute | solution.py:487
  28.3 0.0 collective-permute-start.12
  28.3 0.5 collective-permute-start.8
  28.7 5.5 %collective-permute-done.11.near_side.refs_3_ = bf16[14,64,128]{2,1,0:T(8,128)(2,1)S(1)} collective-permute-done((bf16[14,64,128]{2,1,0:T(8,128)(2,1)S(1)}, bf16[14,64,128]{2,1,0:T(8,128)(2,1)S(1)}, u32[]{:S(2)}, u32[]{:S(2)}) %collective-permute-start.11) | collective-permute-done | bytes 229408 | tf_op jit(solution)/shard_map/ppermute | solution.py:487
  34.3 2.2 %collective-permute-start.9 = (bf16[14,64,128]{2,1,0:T(8,128)(2,1)}, bf16[14,64,128]{2,1,0:T(8,128)(2,1)S(1)}, u32[]{:S(2)}, u32[]{:S(2)}) collective-permute-start(bf16[14,64,128]{2,1,0:T(8,128)(2,1)} %copy-done.8), channel_id=1, source_target_pairs={{0,13},{1,12},{2,15},{3,14},{4,1},{5,0},{6,3},{7,2},{8,5},{9,4},{1... | collective-permute-start | bytes 688136 | tf_op jit(solution)/shard_map/ppermute | solution.py:487
  36.5 2.7 %collective-permute-done.12.far_side.refs_4_ = bf16[14,64,128]{2,1,0:T(8,128)(2,1)S(1)} collective-permute-done((bf16[14,64,128]{2,1,0:T(8,128)(2,1)S(1)}, bf16[14,64,128]{2,1,0:T(8,128)(2,1)S(1)}, u32[]{:S(2)}, u32[]{:S(2)}) %collective-permute-start.12) | collective-permute-done | bytes 229408 | tf_op jit(solution)/shard_map/ppermute | solution.py:487
  39.2 2.5 %collective-permute-start.5 = (bf16[12,64,128]{2,1,0:T(8,128)(2,1)S(1)}, bf16[12,64,128]{2,1,0:T(8,128)(2,1)S(1)}, u32[]{:S(2)}, u32[]{:S(2)}) collective-permute-start(bf16[12,64,128]{2,1,0:T(8,128)(2,1)S(1)} %get-tuple-element.19.keep), channel_id=1, source_target_pairs={{0,12},{1,13},{2,14},{3,15},{4,0},{5,1},{6,2},{7,3},{8,4},{9,5},{1... | collective-permute-start | bytes 589832 | tf_op jit(solution)/shard_map/ppermute | solution.py:487
  41.7 0.0 collective-permute-done.1.taken
  41.7 1.2 payload.7
  42.9 1.6 %collective-permute-start.13 = (bf16[2,14,64,128]{3,2,1,0:T(8,128)(2,1)S(1)}, bf16[2,14,64,128]{3,2,1,0:T(8,128)(2,1)S(1)}, u32[]{:S(2)}, u32[]{:S(2)}) collective-permute-start(bf16[2,14,64,128]{3,2,1,0:T(8,128)(2,1)S(1)} %payload.7), channel_id=1, source_target_pairs={{0,2},{2,0},{4,6},{6,4},{8,10},{10,8},{12,14},{14,12},{1,3},{3,1},... | collective-permute-start | bytes 1376264 | tf_op jit(solution)/shard_map/ppermute | solution.py:502
  44.5 7.9 %collective-permute-done.5.near_side.refs_3_ = bf16[12,64,128]{2,1,0:T(8,128)(2,1)S(1)} collective-permute-done((bf16[12,64,128]{2,1,0:T(8,128)(2,1)S(1)}, bf16[12,64,128]{2,1,0:T(8,128)(2,1)S(1)}, u32[]{:S(2)}, u32[]{:S(2)}) %collective-permute-start.5) | collective-permute-done | bytes 196640 | tf_op jit(solution)/shard_map/ppermute | solution.py:487
  52.3 3.1 %collective-permute-start.6 = (bf16[12,64,128]{2,1,0:T(8,128)(2,1)}, bf16[12,64,128]{2,1,0:T(8,128)(2,1)S(1)}, u32[]{:S(2)}, u32[]{:S(2)}) collective-permute-start(bf16[12,64,128]{2,1,0:T(8,128)(2,1)} %copy-done.9), channel_id=1, source_target_pairs={{0,13},{1,12},{2,15},{3,14},{4,1},{5,0},{6,3},{7,2},{8,5},{9,4},{1... | collective-permute-start | bytes 589832 | tf_op jit(solution)/shard_map/ppermute | solution.py:487
  55.4 0.0 collective-permute-done.8.near_side.refs_3_
  55.4 1.2 collective-permute-start.2
  56.6 0.0 collective-permute-done.9.far_side.refs_4_
  56.6 0.0 collective-permute-start.3
  56.6 1.2 payload.6
  57.9 2.6 %collective-permute-done.6.far_side.refs_4_ = bf16[12,64,128]{2,1,0:T(8,128)(2,1)S(1)} collective-permute-done((bf16[12,64,128]{2,1,0:T(8,128)(2,1)}, bf16[12,64,128]{2,1,0:T(8,128)(2,1)S(1)}, u32[]{:S(2)}, u32[]{:S(2)}) %collective-permute-start.6) | collective-permute-done | bytes 196640 | tf_op jit(solution)/shard_map/ppermute | solution.py:487
  60.4 1.5 %collective-permute-start.10 = (bf16[2,14,64,128]{3,2,1,0:T(8,128)(2,1)S(1)}, bf16[2,14,64,128]{3,2,1,0:T(8,128)(2,1)S(1)}, u32[]{:S(2)}, u32[]{:S(2)}) collective-permute-start(bf16[2,14,64,128]{3,2,1,0:T(8,128)(2,1)S(1)} %payload.6), channel_id=1, source_target_pairs={{0,2},{2,0},{4,6},{6,4},{8,10},{10,8},{12,14},{14,12},{1,3},{3,1},... | collective-permute-start | bytes 1376264 | tf_op jit(solution)/shard_map/ppermute | solution.py:502
  62.0 1.0 payload.5
  63.0 1.6 %collective-permute-done.2.near_side.refs_3_ = bf16[12,64,128]{2,1,0:T(8,128)(2,1)S(1)} collective-permute-done((bf16[12,64,128]{2,1,0:T(8,128)(2,1)S(1)}, bf16[12,64,128]{2,1,0:T(8,128)(2,1)S(1)}, u32[]{:S(2)}, u32[]{:S(2)}) %collective-permute-start.2) | collective-permute-done | bytes 196640 | tf_op jit(solution)/shard_map/ppermute | solution.py:487
  64.5 1.5 %collective-permute-start.7 = (bf16[2,12,64,128]{3,2,1,0:T(8,128)(2,1)S(1)}, bf16[2,12,64,128]{3,2,1,0:T(8,128)(2,1)S(1)}, u32[]{:S(2)}, u32[]{:S(2)}) collective-permute-start(bf16[2,12,64,128]{3,2,1,0:T(8,128)(2,1)S(1)} %payload.5), channel_id=1, source_target_pairs={{0,2},{2,0},{4,6},{6,4},{8,10},{10,8},{12,14},{14,12},{1,3},{3,1},... | collective-permute-start | bytes 1179656 | tf_op jit(solution)/shard_map/ppermute | solution.py:502
  66.1 2.7 %collective-permute-done.3.far_side.refs_4_ = bf16[12,64,128]{2,1,0:T(8,128)(2,1)S(1)} collective-permute-done((bf16[12,64,128]{2,1,0:T(8,128)(2,1)S(1)}, bf16[12,64,128]{2,1,0:T(8,128)(2,1)S(1)}, u32[]{:S(2)}, u32[]{:S(2)}) %collective-permute-start.3) | collective-permute-done | bytes 196640 | tf_op jit(solution)/shard_map/ppermute | solution.py:487
  68.8 1.2 payload.4
  70.0 1.6 %collective-permute-start.4 = (bf16[2,12,64,128]{3,2,1,0:T(8,128)(2,1)S(1)}, bf16[2,12,64,128]{3,2,1,0:T(8,128)(2,1)S(1)}, u32[]{:S(2)}, u32[]{:S(2)}) collective-permute-start(bf16[2,12,64,128]{3,2,1,0:T(8,128)(2,1)S(1)} %payload.4), channel_id=1, source_target_pairs={{0,2},{2,0},{4,6},{6,4},{8,10},{10,8},{12,14},{14,12},{1,3},{3,1},... | collective-permute-start | bytes 1179656 | tf_op jit(solution)/shard_map/ppermute | solution.py:502
  71.6 0.0 collective-permute-done.refs_1_
  71.6 10.0 %cross.5.refs_6_ = bf16[2,52,104,512]{3,2,1,0:T(8,128)(2,1)} custom-call(bf16[64,128,256]{2,1,0:T(8,128)(2,1)} %get-tuple-element.15.refs_0_, bf16[64,128,256]{2,1,0:T(8,128)(2,1)} %collective-permute-done.refs_1_, bf16[2,256,512]{2,1,0:T(8,128)(2,1)S(1)} %copy-done, bf16[14,64,128]{2,1,0:T(8,128)(2,1)S(1)} %collective-permute-done.11.near_side.refs_3_, ...), custom_call_target="tpu_custom_call" | custom-call | flops 2100000000 | bytes 12582912 | tf_op jit(solution)/shard_map/cross/pallas_call | solution.py:429
  81.6 12.9 %cross.6.refs_6_ = bf16[2,52,104,512]{3,2,1,0:T(8,128)(2,1)} custom-call(bf16[64,128,256]{2,1,0:T(8,128)(2,1)} %get-tuple-element.15.refs_0_, bf16[64,128,256]{2,1,0:T(8,128)(2,1)} %collective-permute-done.refs_1_, bf16[2,256,512]{2,1,0:T(8,128)(2,1)S(1)} %copy-done, ...), custom_call_target="tpu_custom_call", output_to_operand_aliasing={{}: (6, {})} | custom-call | flops 4200000000 | bytes 12582912 | tf_op jit(solution)/shard_map/cross/pallas_call | solution.py:429
  94.4 0.0 collective-permute-done.10.refs_5_
  94.4 12.5 %cross.7.refs_6_ = bf16[2,52,104,512]{3,2,1,0:T(8,128)(2,1)} custom-call(bf16[64,128,256]{2,1,0:T(8,128)(2,1)} %get-tuple-element.15.refs_0_, bf16[64,128,256]{2,1,0:T(8,128)(2,1)} %collective-permute-done.refs_1_, bf16[2,256,512]{2,1,0:T(8,128)(2,1)S(1)} %copy-done, ...), custom_call_target="tpu_custom_call", output_to_operand_aliasing={{}: (6, {})} | custom-call | flops 3900000000 | bytes 12582912 | tf_op jit(solution)/shard_map/cross/pallas_call | solution.py:429
  106.9 0.0 collective-permute-done.7.refs_5_
  106.9 12.1 %cross.8.refs_4_ = bf16[2,52,104,512]{3,2,1,0:T(8,128)(2,1)} custom-call(bf16[64,128,256]{2,1,0:T(8,128)(2,1)} %get-tuple-element.15.refs_0_, bf16[64,128,256]{2,1,0:T(8,128)(2,1)} %collective-permute-done.refs_1_, bf16[2,256,512]{2,1,0:T(8,128)(2,1)S(1)} %copy-done, ...), custom_call_target="tpu_custom_call", output_to_operand_aliasing={{}: (6, {})} | custom-call | flops 3600000000 | bytes 12582912 | tf_op jit(solution)/shard_map/cross/pallas_call | solution.py:429
  119.0 0.0 collective-permute-done.4.refs_3_
  119.0 9.6 %cross.9 = bf16[2,52,104,512]{3,2,1,0:T(8,128)(2,1)} custom-call(bf16[64,128,256]{2,1,0:T(8,128)(2,1)} %get-tuple-element.15.refs_0_, bf16[64,128,256]{2,1,0:T(8,128)(2,1)} %collective-permute-done.refs_1_, bf16[2,256,512]{2,1,0:T(8,128)(2,1)S(1)} %copy-done, ...), custom_call_target="tpu_custom_call", output_to_operand_aliasing={{}: (4, {})} | custom-call | flops 1800000000 | bytes 12582912 | tf_op jit(solution)/shard_map/cross/pallas_call | solution.py:429
  (15 shorter events, 0.0 us)
Async XLA Ops:
  0.0 71.6 %copy-start = (bf16[2,256,512]{2,1,0:T(8,128)(2,1)S(1)}, bf16[2,256,512]{2,1,0:T(8,128)(2,1)}, u32[]{:S(2)}) copy-start(bf16[2,256,512]{2,1,0:T(8,128)(2,1)} %constant.30.refs_2_) | copy-start | bytes 1572868
  0.0 2.0 %copy-start.1 = (f32[104,8192]{1,0:T(8,128)S(1)}, f32[104,8192]{1,0:T(8,128)}, u32[]{:S(2)}) copy-start(f32[104,8192]{1,0:T(8,128)} %signal_hbm.3) | copy-start | bytes 10223620
  2.0 1.6 %copy-start.3 = (bf16[1024,1024]{1,0:T(8,128)(2,1)S(1)}, bf16[1024,1024]{1,0:T(8,128)(2,1)}, u32[]{:S(2)}) copy-start(bf16[1024,1024]{1,0:T(8,128)(2,1)} %constant.29.table_hbm) | copy-start | bytes 6291460
  3.6 0.7 copy-start.5
  4.3 0.7 copy-start.7
  13.6 9.6 %copy-start.8 = (bf16[14,64,128]{2,1,0:T(8,128)(2,1)}, bf16[14,64,128]{2,1,0:T(8,128)(2,1)S(1)}, u32[]{:S(2)}) copy-start(bf16[14,64,128]{2,1,0:T(8,128)(2,1)S(1)} %get-tuple-element.22) | copy-start | bytes 688132
  13.6 9.6 %copy-start.9 = (bf16[12,64,128]{2,1,0:T(8,128)(2,1)}, bf16[12,64,128]{2,1,0:T(8,128)(2,1)S(1)}, u32[]{:S(2)}) copy-start(bf16[12,64,128]{2,1,0:T(8,128)(2,1)S(1)} %get-tuple-element.20) | copy-start | bytes 589828
  13.6 58.0 %collective-permute-start = (bf16[64,128,256]{2,1,0:T(8,128)(2,1)}, bf16[64,128,256]{2,1,0:T(8,128)(2,1)}, u32[]{:S(2)}, u32[]{:S(2)}) collective-permute-start(bf16[64,128,256]{2,1,0:T(8,128)(2,1)} %get-tuple-element.15.refs_0_), channel_id=1, source_target_pairs={{0,1},{1,0},{2,3},{3,2},{4,5},{5,4},{6,7},{7,6},{8,9},{9,8},{10,11... | collective-permute-start | bytes 12582920 | tf_op jit(solution)/shard_map/ppermute | solution.py:490
  14.1 27.5 %collective-permute-start.1 = (bf16[52,64,128]{2,1,0:T(8,128)(2,1)}, bf16[52,64,128]{2,1,0:T(8,128)(2,1)S(1)}, u32[]{:S(2)}, u32[]{:S(2)}) collective-permute-start(bf16[52,64,128]{2,1,0:T(8,128)(2,1)} %get-tuple-element.17), channel_id=1, source_target_pairs={{0,1},{1,0},{2,3},{3,2},{4,5},{5,4},{6,7},{7,6},{8,9},{9,8},{10,11... | collective-permute-start | bytes 2555912 | tf_op jit(solution)/shard_map/ppermute | solution.py:489
  14.5 2.0 %copy-start.2 = (f32[104,8192]{1,0:T(8,128)S(1)}, f32[104,8192]{1,0:T(8,128)}, u32[]{:S(2)}) copy-start(f32[104,8192]{1,0:T(8,128)} %signal_hbm.3) | copy-start | bytes 10223620
  16.4 1.6 %copy-start.4 = (bf16[1024,1024]{1,0:T(8,128)(2,1)S(1)}, bf16[1024,1024]{1,0:T(8,128)(2,1)}, u32[]{:S(2)}) copy-start(bf16[1024,1024]{1,0:T(8,128)(2,1)} %constant.29.table_hbm) | copy-start | bytes 6291460
  18.0 0.7 copy-start.6
  23.2 11.1 %collective-permute-start.11 = (bf16[14,64,128]{2,1,0:T(8,128)(2,1)S(1)}, bf16[14,64,128]{2,1,0:T(8,128)(2,1)S(1)}, u32[]{:S(2)}, u32[]{:S(2)}) collective-permute-start(bf16[14,64,128]{2,1,0:T(8,128)(2,1)S(1)} %get-tuple-element.23.keep), channel_id=1, source_target_pairs={{0,12},{1,13},{2,14},{3,15},{4,0},{5,1},{6,2},{7,3},{8,4},{9,5},{1... | collective-permute-start | bytes 688136 | tf_op jit(solution)/shard_map/ppermute | solution.py:487
  28.3 10.9 %collective-permute-start.12 = (bf16[14,64,128]{2,1,0:T(8,128)(2,1)S(1)}, bf16[14,64,128]{2,1,0:T(8,128)(2,1)S(1)}, u32[]{:S(2)}, u32[]{:S(2)}) collective-permute-start(bf16[14,64,128]{2,1,0:T(8,128)(2,1)S(1)} %get-tuple-element.24), channel_id=1, source_target_pairs={{0,13},{1,12},{2,15},{3,14},{4,1},{5,0},{6,3},{7,2},{8,5},{9,4},{1... | collective-permute-start | bytes 688136 | tf_op jit(solution)/shard_map/ppermute | solution.py:487
  28.3 27.2 %collective-permute-start.8 = (bf16[14,64,128]{2,1,0:T(8,128)(2,1)S(1)}, bf16[14,64,128]{2,1,0:T(8,128)(2,1)S(1)}, u32[]{:S(2)}, u32[]{:S(2)}) collective-permute-start(bf16[14,64,128]{2,1,0:T(8,128)(2,1)S(1)} %get-tuple-element.21.keep), channel_id=1, source_target_pairs={{0,12},{1,13},{2,14},{3,15},{4,0},{5,1},{6,2},{7,3},{8,4},{9,5},{1... | collective-permute-start | bytes 688136 | tf_op jit(solution)/shard_map/ppermute | solution.py:487
  34.3 22.4 %collective-permute-start.9 = (bf16[14,64,128]{2,1,0:T(8,128)(2,1)}, bf16[14,64,128]{2,1,0:T(8,128)(2,1)S(1)}, u32[]{:S(2)}, u32[]{:S(2)}) collective-permute-start(bf16[14,64,128]{2,1,0:T(8,128)(2,1)} %copy-done.8), channel_id=1, source_target_pairs={{0,13},{1,12},{2,15},{3,14},{4,1},{5,0},{6,3},{7,2},{8,5},{9,4},{1... | collective-permute-start | bytes 688136 | tf_op jit(solution)/shard_map/ppermute | solution.py:487
  39.2 13.1 %collective-permute-start.5 = (bf16[12,64,128]{2,1,0:T(8,128)(2,1)S(1)}, bf16[12,64,128]{2,1,0:T(8,128)(2,1)S(1)}, u32[]{:S(2)}, u32[]{:S(2)}) collective-permute-start(bf16[12,64,128]{2,1,0:T(8,128)(2,1)S(1)} %get-tuple-element.19.keep), channel_id=1, source_target_pairs={{0,12},{1,13},{2,14},{3,15},{4,0},{5,1},{6,2},{7,3},{8,4},{9,5},{1... | collective-permute-start | bytes 589832 | tf_op jit(solution)/shard_map/ppermute | solution.py:487
  42.9 38.7 %collective-permute-start.13 = (bf16[2,14,64,128]{3,2,1,0:T(8,128)(2,1)S(1)}, bf16[2,14,64,128]{3,2,1,0:T(8,128)(2,1)S(1)}, u32[]{:S(2)}, u32[]{:S(2)}) collective-permute-start(bf16[2,14,64,128]{3,2,1,0:T(8,128)(2,1)S(1)} %payload.7), channel_id=1, source_target_pairs={{0,2},{2,0},{4,6},{6,4},{8,10},{10,8},{12,14},{14,12},{1,3},{3,1},... | collective-permute-start | bytes 1376264 | tf_op jit(solution)/shard_map/ppermute | solution.py:502
  52.3 8.1 %collective-permute-start.6 = (bf16[12,64,128]{2,1,0:T(8,128)(2,1)}, bf16[12,64,128]{2,1,0:T(8,128)(2,1)S(1)}, u32[]{:S(2)}, u32[]{:S(2)}) collective-permute-start(bf16[12,64,128]{2,1,0:T(8,128)(2,1)} %copy-done.9), channel_id=1, source_target_pairs={{0,13},{1,12},{2,15},{3,14},{4,1},{5,0},{6,3},{7,2},{8,5},{9,4},{1... | collective-permute-start | bytes 589832 | tf_op jit(solution)/shard_map/ppermute | solution.py:487
  55.4 9.1 %collective-permute-start.2 = (bf16[12,64,128]{2,1,0:T(8,128)(2,1)S(1)}, bf16[12,64,128]{2,1,0:T(8,128)(2,1)S(1)}, u32[]{:S(2)}, u32[]{:S(2)}) collective-permute-start(bf16[12,64,128]{2,1,0:T(8,128)(2,1)S(1)} %get-tuple-element.16.keep), channel_id=1, source_target_pairs={{0,12},{1,13},{2,14},{3,15},{4,0},{5,1},{6,2},{7,3},{8,4},{9,5},{1... | collective-permute-start | bytes 589832 | tf_op jit(solution)/shard_map/ppermute | solution.py:487
  56.6 12.1 %collective-permute-start.3 = (bf16[12,64,128]{2,1,0:T(8,128)(2,1)S(1)}, bf16[12,64,128]{2,1,0:T(8,128)(2,1)S(1)}, u32[]{:S(2)}, u32[]{:S(2)}) collective-permute-start(bf16[12,64,128]{2,1,0:T(8,128)(2,1)S(1)} %get-tuple-element.18), channel_id=1, source_target_pairs={{0,13},{1,12},{2,15},{3,14},{4,1},{5,0},{6,3},{7,2},{8,5},{9,4},{1... | collective-permute-start | bytes 589832 | tf_op jit(solution)/shard_map/ppermute | solution.py:487
  60.4 34.0 %collective-permute-start.10 = (bf16[2,14,64,128]{3,2,1,0:T(8,128)(2,1)S(1)}, bf16[2,14,64,128]{3,2,1,0:T(8,128)(2,1)S(1)}, u32[]{:S(2)}, u32[]{:S(2)}) collective-permute-start(bf16[2,14,64,128]{3,2,1,0:T(8,128)(2,1)S(1)} %payload.6), channel_id=1, source_target_pairs={{0,2},{2,0},{4,6},{6,4},{8,10},{10,8},{12,14},{14,12},{1,3},{3,1},... | collective-permute-start | bytes 1376264 | tf_op jit(solution)/shard_map/ppermute | solution.py:502
  64.5 42.4 %collective-permute-start.7 = (bf16[2,12,64,128]{3,2,1,0:T(8,128)(2,1)S(1)}, bf16[2,12,64,128]{3,2,1,0:T(8,128)(2,1)S(1)}, u32[]{:S(2)}, u32[]{:S(2)}) collective-permute-start(bf16[2,12,64,128]{3,2,1,0:T(8,128)(2,1)S(1)} %payload.5), channel_id=1, source_target_pairs={{0,2},{2,0},{4,6},{6,4},{8,10},{10,8},{12,14},{14,12},{1,3},{3,1},... | collective-permute-start | bytes 1179656 | tf_op jit(solution)/shard_map/ppermute | solution.py:502
  70.0 49.0 %collective-permute-start.4 = (bf16[2,12,64,128]{3,2,1,0:T(8,128)(2,1)S(1)}, bf16[2,12,64,128]{3,2,1,0:T(8,128)(2,1)S(1)}, u32[]{:S(2)}, u32[]{:S(2)}) collective-permute-start(bf16[2,12,64,128]{3,2,1,0:T(8,128)(2,1)S(1)} %payload.4), channel_id=1, source_target_pairs={{0,2},{2,0},{4,6},{6,4},{8,10},{10,8},{12,14},{14,12},{1,3},{3,1},... | collective-permute-start | bytes 1179656 | tf_op jit(solution)/shard_map/ppermute | solution.py:502

commit v3 on v2

--- a/solution.py
+++ b/solution.py
@@ -20,7 +20,7 @@
 GROUP = 8
 OCTETS = BINS // GROUP
 STEPS = OCTETS // 4
-ROWS_PER_CHUNK = (14, 14, 12, 12)
+ROWS_PER_CHUNK = (18, 18, 16)
 
 f32 = jnp.float32
 bf16 = jnp.bfloat16
@@ -90,8 +90,8 @@
 
 
 def first_kernel(
-    rows, half, bounds, me_ref, signal_hbm, live_ref, table_hbm, taper_ref,
-    same_ref, cross_ref, signal, tap, table, rows32, in_sem, table_sem,
+    rows, half, bounds, me_ref, signal_hbm, flags_ref, table_hbm, taper_ref,
+    same_ref, cross_ref, signal, tap, table, rows32, live, in_sem, table_sem,
 ):
     spans = signal.shape[1] // WINDOW
     width = LANES // 2
@@ -106,6 +106,14 @@
     tables = table_copies(table_hbm, table, table_sem)
     for copy in tables:
         copy.start()
+    flags = flags_ref[...].astype(f32)
+    flags = jnp.concatenate(
+        [flags[:, low:high] for low, high in bounds] + [jnp.zeros((spans, width - held), f32)], axis=1
+    )
+    for v in range(spans // 2):
+        live[v : v + 1, :] = jnp.concatenate(
+            [flags[2 * v : 2 * v + 1], flags[2 * v + 1 : 2 * v + 2]], axis=1
+        )
     taper = taper_ref[...]
     tap[...] = jnp.zeros_like(tap)
     for copy in loads:
@@ -120,7 +128,7 @@
             position = g * 16 + o
             plain = jnp.concatenate(
                 [
-                    result[o * 16 : o * 16 + 16, v * LANES : (v + 1) * LANES] * live_ref[v : v + 1, :]
+                    result[o * 16 : o * 16 + 16, v * LANES : (v + 1) * LANES] * live[v : v + 1, :]
                     for v in range(spans // 2)
                 ],
                 axis=0,
@@ -138,15 +146,7 @@
         out[...] = block.astype(bf16).reshape(rows, OCTETS, LANES)
 
 
-def first_flags(flags, rows, half):
-    width = LANES // 2
-    parts = [flags[:, h * half // 8 * 8 : -(-(h * half + rows) // 8) * 8] for h in range(2)]
-    held = jnp.concatenate(parts, axis=1)
-    held = jnp.pad(held, ((0, 0), (0, width - held.shape[1])))
-    return held.reshape(flags.shape[0] // 2, LANES)
-
-
-def first_spectra(me, signal, live, table, taper, rows, half):
+def first_spectra(me, signal, flags, table, taper, rows, half):
     spans = signal.shape[1] // WINDOW
     bounds = []
     for h in range(2):
@@ -165,13 +165,14 @@
             pltpu.VMEM((spans * LANES // 2, WINDOW), bf16),
             pltpu.VMEM((WINDOW, WINDOW), bf16),
             pltpu.VMEM((held * OCTETS, LANES), f32),
+            pltpu.VMEM((spans // 2, LANES), f32),
             pltpu.SemaphoreType.DMA((2,)),
             pltpu.SemaphoreType.DMA((4,)),
         ],
-        compiler_params=pltpu.CompilerParams(vmem_limit_bytes=32 << 20),
+        compiler_params=pltpu.CompilerParams(vmem_limit_bytes=62 << 20),
         cost_estimate=pl.CostEstimate(flops=WINDOW**3, bytes_accessed=6 << 20, transcendentals=0),
         name="first",
-    )(me, signal, live, table, taper)
+    )(me, signal, flags, table, taper)
 
 
 def spectra_kernel(
@@ -268,10 +269,35 @@
             pltpu.SemaphoreType.DMA((4,)),
             pltpu.SemaphoreType.DMA,
         ],
-        compiler_params=pltpu.CompilerParams(vmem_limit_bytes=40 << 20),
+        compiler_params=pltpu.CompilerParams(vmem_limit_bytes=62 << 20),
         cost_estimate=pl.CostEstimate(flops=2 * WINDOW**3, bytes_accessed=12 << 20, transcendentals=0),
         name="spectra",
     )(me, signal, flags, table, taper)
+
+
+def join_kernel(near_hbm, far_hbm, out_ref, sem):
+    copies = [
+        pltpu.make_async_copy(side, out_ref.at[:, pl.ds(i * LANES, LANES), :], sem.at[i])
+        for i, side in enumerate((near_hbm, far_hbm))
+    ]
+    for copy in copies:
+        copy.start()
+    for copy in copies:
+        copy.wait()
+
+
+def join(near, far):
+    hbm = pl.BlockSpec(memory_space=pltpu.MemorySpace.HBM)
+    return pl.pallas_call(
+        join_kernel,
+        out_shape=pltpu.VMEM((OCTETS, 2 * LANES, 2 * LANES), bf16),
+        in_specs=[hbm] * 2,
+        out_specs=pl.BlockSpec(memory_space=pltpu.VMEM),
+        scratch_shapes=[pltpu.SemaphoreType.DMA((2,))],
+        compiler_params=pltpu.CompilerParams(vmem_limit_bytes=48 << 20),
+        cost_estimate=pl.CostEstimate(flops=0, bytes_accessed=17 << 20, transcendentals=0),
+        name="join",
+    )(near, far)
 
 
 def payload_kernel(first, rows, odd_ref, keep, taken, near_side, far_side, out_ref, hold, in_sem, out_sem):
@@ -305,7 +331,7 @@
             pltpu.SemaphoreType.DMA((2,)),
             pltpu.SemaphoreType.DMA((2,)),
         ],
-        compiler_params=pltpu.CompilerParams(vmem_limit_bytes=4 << 20),
+        compiler_params=pltpu.CompilerParams(vmem_limit_bytes=48 << 20),
         cost_estimate=pl.CostEstimate(flops=0, bytes_accessed=2 << 20, transcendentals=0),
         name="payload",
     )(odd, keep, taken, near_side, far_side)
@@ -313,11 +339,11 @@
 
 def cross_kernel(parts, row_count, has_prior, *refs):
     source_count = sum(part[3] for part in parts)
-    near_ref, far_hbm, lag_hbm = refs[:3]
-    sources = refs[3 : 3 + source_count]
-    rest = refs[3 + source_count + (1 if has_prior else 0) :]
-    out_ref, far_ref, lag_ref, packed, rows32, cross, mixed, result = rest[:8]
-    in_sem, far_sem, lag_sem, out_sem = rest[8:]
+    weight_ref, lag_hbm = refs[:2]
+    sources = refs[2 : 2 + source_count]
+    rest = refs[2 + source_count + (1 if has_prior else 0) :]
+    out_ref, lag_ref, packed, rows32, cross, mixed, result = rest[:7]
+    in_sem, lag_sem, out_sem = rest[7:]
     total = sum(part[2] for part in parts)
     pairs = total // 2
 
@@ -333,12 +359,6 @@
         cursor += arrays
         row += rows
 
-    def far_copy(m):
-        part = pl.ds(m * 4, 4)
-        return pltpu.make_async_copy(far_hbm.at[part], far_ref.at[part], far_sem.at[m])
-
-    for m in range(STEPS):
-        far_copy(m).start()
     lag_copy = pltpu.make_async_copy(lag_hbm, lag_ref, lag_sem)
     lag_copy.start()
     for copy, side, row, rows in loads:
@@ -352,7 +372,6 @@
     top = sub == 0
 
     def step(m, first):
-        far_copy(m).wait()
         products = []
         for j in range(4):
             position = m * 4 + j
@@ -368,7 +387,7 @@
                 ]
                 blocks.append(jnp.concatenate(halves, axis=1))
             left = jnp.concatenate(blocks, axis=0).astype(bf16)
-            weight = jnp.concatenate([near_ref[position], far_ref[position]], axis=0)
+            weight = weight_ref[position]
             products.append(jnp.dot(left, weight, preferred_element_type=f32))
         base = pl.multiple_of(m * 16, 16)
         for d in range(total):
@@ -415,12 +434,12 @@
         copy.wait()
 
 
-def cross_part(near, far, lag_table, parts, sources, prior, local_rows, row_count):
+def cross_part(weights, lag_table, parts, sources, prior, local_rows, row_count):
     total = sum(part[2] for part in parts)
     any_space = pl.BlockSpec(memory_space=pl.ANY)
-    operands = [near, far, lag_table] + sources
+    operands = [weights, lag_table] + sources
     specs = [pl.BlockSpec(memory_space=pltpu.VMEM)]
-    specs += [pl.BlockSpec(memory_space=pltpu.MemorySpace.HBM)] * (len(sources) + 2)
+    specs += [pl.BlockSpec(memory_space=pltpu.MemorySpace.HBM)] * (len(sources) + 1)
     aliases = {}
     if prior is not None:
         aliases = {len(operands): 0}
@@ -432,7 +451,6 @@
         in_specs=specs,
         out_specs=any_space,
         scratch_shapes=[
-            pltpu.VMEM(far.shape, bf16),
             pltpu.VMEM(lag_table.shape, bf16),
             pltpu.VMEM((2, total, OCTETS, LANES), bf16),
             pltpu.VMEM((2, total, OCTETS, LANES), f32),
@@ -440,7 +458,6 @@
             pltpu.VMEM((2, 2, LAGS, LANES), f32),
             pltpu.VMEM((total, row_count, LAGS), bf16),
             pltpu.SemaphoreType.DMA((len(parts), 2)),
-            pltpu.SemaphoreType.DMA((STEPS,)),
             pltpu.SemaphoreType.DMA,
             pltpu.SemaphoreType.DMA((total,)),
         ],
@@ -471,8 +488,7 @@
 
     flags = valid_flags.T
     table, taper = forward_rows(), taper_row()
-    live = first_flags(flags.astype(f32), chunks[0], local_rows)
-    pieces = list(first_spectra(me[None], signal, live, table, taper, chunks[0], local_rows))
+    pieces = list(first_spectra(me[None], signal, flags, table, taper, chunks[0], local_rows))
     *more, give, near = spectra(me[None], signal, flags, table, taper, chunks, local_rows)
     pieces += more
 
@@ -488,6 +504,7 @@
     other = [(t, 1 - t) for t in range(owner_count)]
     taken = lax.ppermute(give, "tm", other)
     far = lax.ppermute(near, "tm", other)
+    weights = join(near, far)
     swap = [(b, b - 1 if b % 2 else b + 1) for b in range(blocks)]
 
     lag_table = lag_rows(span_windows * owner_count)
@@ -505,7 +522,7 @@
         if k > 0:
             parts.append((0, int(starts[k - 1]), chunks[k - 1], 1))
             sources.append(one_away[k - 1])
-        out = cross_part(near, far, lag_table, parts, sources, out, local_rows, row_count)
+        out = cross_part(weights, lag_table, parts, sources, out, local_rows, row_count)
     return out
 
 

time: 129 us -> 109 us (0.84)
  Pallas kernels: 74.6 us -> 56.9 us
  waiting for transfers between devices: 23 us -> 33 us
  local copies, waits for them, and re-layouts: 9.39 us -> 1.92 us
  starting transfers between devices: 21.4 us -> 16.2 us
    pallas_call x5 -> x4, Pallas kernels: 57 us -> 33.3 us  [cross_part(): pl.pallas_call(functools.partial(cross_kernel, tuple(parts), row_count, p...]
    unnamed x20 -> x8, local copies, waits for them, and re-layouts: 9.24 us -> 1.92 us
    ppermute x8 -> x6, waiting for transfers between devices: 23 us -> 29.2 us  [local(): lax.ppermute(x, axes, back(2, i % 2))]
    ppermute x4 -> x3, waiting for transfers between devices: 0.01 us -> 3.81 us  [local(): one_away.append(lax.ppermute(load, 'chan', swap))]
    pallas_call x4 -> x3, Pallas kernels: 4.64 us -> 0.88 us  [payload(): pl.pallas_call(functools.partial(payload_kernel, first, keep.shape[0]), o...]
    pallas_call x0 -> x1, Pallas kernels: none -> 3.48 us  [join(): pl.pallas_call(join_kernel, out_shape=pltpu.VMEM((OCTETS, 2 * LANES, 2 *...]
    pallas_call x1, Pallas kernels: 4.47 us -> 7.91 us  [first_spectra(): pl.pallas_call(functools.partial(first_kernel, rows, half, tuple(bounds))...]
    pallas_call x1, Pallas kernels: 8.56 us -> 11.3 us  [spectra(): pl.pallas_call(functools.partial(spectra_kernel, chunks, half), out_shape...]
  transfers between devices with their start and end apart: 14 -> 11, of which waited for: 6 -> 4; matrix products, arithmetic and copies ran while one was open for 0% -> 0% of each run, Pallas kernels for 44% -> 36%
where the time goes in v3:
time: 109 us; the launch traced here: 108 us
  Pallas kernels  56.9 us (52%)
  waiting for transfers between devices  33 us (30%)
  starting transfers between devices  16.2 us (15%)
  local copies, waits for them, and re-layouts  1.92 us (2%)
    pallas_call x4, Pallas kernels, cross_part(): pl.pallas_call(functools.partial(cross_kernel, tuple(parts), row_count, p...  33.3 us
    ppermute x6, waiting for transfers between devices, local(): lax.ppermute(x, axes, back(2, i % 2))  29.2 us
    ppermute x6, starting transfers between devices, local(): lax.ppermute(x, axes, back(2, i % 2))  11.9 us
    pallas_call x1, Pallas kernels, spectra(): pl.pallas_call(functools.partial(spectra_kernel, chunks, half), out_shape...  11.3 us
    pallas_call x1, Pallas kernels, first_spectra(): pl.pallas_call(functools.partial(first_kernel, rows, half, tuple(bounds))...  7.91 us
    ppermute x3, waiting for transfers between devices, local(): one_away.append(lax.ppermute(load, 'chan', swap))  3.81 us
    ppermute x3, starting transfers between devices, local(): one_away.append(lax.ppermute(load, 'chan', swap))  3.75 us
    pallas_call x1, Pallas kernels, join(): pl.pallas_call(join_kernel, out_shape=pltpu.VMEM((OCTETS, 2 * LANES, 2 *...  3.48 us
  transfers between devices with their start and end apart: 11, of which 4 were waited for; matrix products, arithmetic and copies ran while one was open for 0% of the time, Pallas kernels for 36%

profile of v3, /device:TPU:0, one launch (start us, length us, event | category | flops | bytes accessed | tf_op | source)
XLA Modules:
  0.0 108.4 jit_solution(6445029357033080432)
XLA Ops:
  0.0 11.3 %spectra.1 = (bf16[18,64,128]{2,1,0:T(8,128)(2,1)}, bf16[18,64,128]{2,1,0:T(8,128)(2,1)}, bf16[16,64,128]{2,1,0:T(8,128)(2,1)}, bf16[16,64,128]{2,1,0:T(8,128)(2...) custom-call(s32[1]{0:T(128)} %bitcast.me_ref, f32[104,8192]{1,0:T(8,128)} %signal_hbm.3, ...), custom_call_target="tpu_custom_call" | custom-call | flops 2147483648 | bytes 12582912 | tf_op jit(solution)/shard_map/spectra/pallas_call | solution.py:254
  11.3 0.0 copy-start.1
  11.3 0.6 collective-permute-start
  11.9 0.1 collective-permute-start.1
  12.0 7.9 %first.1 = (bf16[18,64,128]{2,1,0:T(8,128)(2,1)}, bf16[18,64,128]{2,1,0:T(8,128)(2,1)}) custom-call(s32[1]{0:T(128)} %bitcast.me_ref, f32[104,8192]{1,0:T(8,128)} %signal_hbm.3, s32[8,104]{1,0:T(8,128)} %bitcast.4, bf16[1024,1024]{1,0:T(8,128)(2,1)} %constant.24.table_hbm, f32[1,1024]{1,0:T(1,128)} %constant.20.clone.taper_ref), custom_call_target="tpu_custom_call" | custom-call | flops 1073741824 | bytes 6291456 | tf_op jit(solution)/shard_map/first/pallas_call | solution.py:158
  19.9 4.8 %collective-permute-start.9 = (bf16[18,64,128]{2,1,0:T(8,128)(2,1)}, bf16[18,64,128]{2,1,0:T(8,128)(2,1)S(1)}, u32[]{:S(2)}, u32[]{:S(2)}) collective-permute-start(bf16[18,64,128]{2,1,0:T(8,128)(2,1)} %get-tuple-element.20), channel_id=1, source_target_pairs={{0,13},{1,12},{2,15},{3,14},{4,1},{5,0},{6,3},{7,2},{8,5},{9,4},{1... | collective-permute-start | bytes 884744 | tf_op jit(solution)/shard_map/ppermute | solution.py:503
  24.6 0.5 collective-permute-start.8
  25.1 0.2 collective-permute-start.3
  25.3 7.1 %collective-permute-done.9.far_side.refs_3_ = bf16[18,64,128]{2,1,0:T(8,128)(2,1)S(1)} collective-permute-done((bf16[18,64,128]{2,1,0:T(8,128)(2,1)}, bf16[18,64,128]{2,1,0:T(8,128)(2,1)S(1)}, u32[]{:S(2)}, u32[]{:S(2)}) %collective-permute-start.9) | collective-permute-done | bytes 294944 | tf_op jit(solution)/shard_map/ppermute | solution.py:503
  32.4 6.3 %collective-permute-done.8.near_side.refs_2_ = bf16[18,64,128]{2,1,0:T(8,128)(2,1)S(1)} collective-permute-done((bf16[18,64,128]{2,1,0:T(8,128)(2,1)}, bf16[18,64,128]{2,1,0:T(8,128)(2,1)S(1)}, u32[]{:S(2)}, u32[]{:S(2)}) %collective-permute-start.8) | collective-permute-done | bytes 294944 | tf_op jit(solution)/shard_map/ppermute | solution.py:503
  38.7 0.0 collective-permute-done.1.taken
  38.7 0.0 copy-start.2
  38.7 1.0 copy-done.2
  39.6 0.3 payload.5
  39.9 1.6 %collective-permute-start.10 = (bf16[2,18,64,128]{3,2,1,0:T(8,128)(2,1)S(1)}, bf16[2,18,64,128]{3,2,1,0:T(8,128)(2,1)S(1)}, u32[]{:S(2)}, u32[]{:S(2)}) collective-permute-start(bf16[2,18,64,128]{3,2,1,0:T(8,128)(2,1)S(1)} %payload.5), channel_id=1, source_target_pairs={{0,2},{2,0},{4,6},{6,4},{8,10},{10,8},{12,14},{14,12},{1,3},{3,1},... | collective-permute-start | bytes 1769480 | tf_op jit(solution)/shard_map/ppermute | solution.py:519
  41.5 3.1 %collective-permute-start.6 = (bf16[18,64,128]{2,1,0:T(8,128)(2,1)}, bf16[18,64,128]{2,1,0:T(8,128)(2,1)S(1)}, u32[]{:S(2)}, u32[]{:S(2)}) collective-permute-start(bf16[18,64,128]{2,1,0:T(8,128)(2,1)} %get-tuple-element.18), channel_id=1, source_target_pairs={{0,13},{1,12},{2,15},{3,14},{4,1},{5,0},{6,3},{7,2},{8,5},{9,4},{1... | collective-permute-start | bytes 884744 | tf_op jit(solution)/shard_map/ppermute | solution.py:503
  44.7 1.1 collective-permute-start.5
  45.7 0.0 collective-permute-done.3.far_side.refs_3_
  45.7 2.3 %collective-permute-start.2 = (bf16[16,64,128]{2,1,0:T(8,128)(2,1)}, bf16[16,64,128]{2,1,0:T(8,128)(2,1)S(1)}, u32[]{:S(2)}, u32[]{:S(2)}) collective-permute-start(bf16[16,64,128]{2,1,0:T(8,128)(2,1)} %get-tuple-element.14.keep), channel_id=1, source_target_pairs={{0,12},{1,13},{2,14},{3,15},{4,0},{5,1},{6,2},{7,3},{8,4},{9,5},{1... | collective-permute-start | bytes 786440 | tf_op jit(solution)/shard_map/ppermute | solution.py:503
  48.0 15.9 %collective-permute-done.2.near_side.refs_2_ = bf16[16,64,128]{2,1,0:T(8,128)(2,1)S(1)} collective-permute-done((bf16[16,64,128]{2,1,0:T(8,128)(2,1)}, bf16[16,64,128]{2,1,0:T(8,128)(2,1)S(1)}, u32[]{:S(2)}, u32[]{:S(2)}) %collective-permute-start.2) | collective-permute-done | bytes 262176 | tf_op jit(solution)/shard_map/ppermute | solution.py:503
  63.8 0.0 copy-start.3
  63.8 0.9 copy-done.3
  64.8 0.1 payload.3
  64.9 0.6 collective-permute-start.4
  65.5 0.0 collective-permute-done.6.far_side.refs_3_
  65.5 0.0 collective-permute-done.5.near_side.refs_2_
  65.5 0.0 copy-done.1
  65.5 0.5 payload.4
  66.0 0.0 copy-start
  66.0 1.6 %collective-permute-start.7 = (bf16[2,18,64,128]{3,2,1,0:T(8,128)(2,1)S(1)}, bf16[2,18,64,128]{3,2,1,0:T(8,128)(2,1)S(1)}, u32[]{:S(2)}, u32[]{:S(2)}) collective-permute-start(bf16[2,18,64,128]{3,2,1,0:T(8,128)(2,1)S(1)} %payload.4), channel_id=1, source_target_pairs={{0,2},{2,0},{4,6},{6,4},{8,10},{10,8},{12,14},{14,12},{1,3},{3,1},... | collective-permute-start | bytes 1769480 | tf_op jit(solution)/shard_map/ppermute | solution.py:519
  67.6 0.0 collective-permute-done.far_hbm
  67.6 3.5 %join.1.refs_0_ = bf16[64,256,256]{2,1,0:T(8,128)(2,1)S(1)} custom-call(bf16[64,128,256]{2,1,0:T(8,128)(2,1)} %get-tuple-element.13.near_hbm, bf16[64,128,256]{2,1,0:T(8,128)(2,1)} %collective-permute-done.far_hbm), custom_call_target="tpu_custom_call" | custom-call | bytes 17825792 | tf_op jit(solution)/shard_map/join/pallas_call | solution.py:291
  71.1 0.0 copy-done
  71.1 6.9 %cross.4.refs_5_ = bf16[2,52,104,512]{3,2,1,0:T(8,128)(2,1)} custom-call(bf16[64,256,256]{2,1,0:T(8,128)(2,1)S(1)} %join.1.refs_0_, bf16[2,256,512]{2,1,0:T(8,128)(2,1)S(1)} %copy-done, bf16[18,64,128]{2,1,0:T(8,128)(2,1)S(1)} %collective-permute-done.8.near_side.refs_2_, bf16[18,64,128]{2,1,0:T(8,128)(2,1)S(1)} %collective-permute-done.9.far_side.refs_3_), custom_call_target="tpu_custom_call" | custom-call | flops 2700000000 | bytes 12582912 | tf_op jit(solution)/shard_map/cross/pallas_call | solution.py:448
  78.0 0.0 collective-permute-done.10.refs_4_
  78.0 10.2 %cross.5.refs_5_ = bf16[2,52,104,512]{3,2,1,0:T(8,128)(2,1)} custom-call(bf16[64,256,256]{2,1,0:T(8,128)(2,1)S(1)} %join.1.refs_0_, bf16[2,256,512]{2,1,0:T(8,128)(2,1)S(1)} %copy-done, bf16[18,64,128]{2,1,0:T(8,128)(2,1)S(1)} %collective-permute-done.5.near_side.refs_2_, ...), custom_call_target="tpu_custom_call", output_to_operand_aliasing={{}: (5, {})} | custom-call | flops 5400000000 | bytes 12582912 | tf_op jit(solution)/shard_map/cross/pallas_call | solution.py:448
  88.2 3.8 %collective-permute-done.7.refs_4_ = bf16[2,18,64,128]{3,2,1,0:T(8,128)(2,1)S(1)} collective-permute-done((bf16[2,18,64,128]{3,2,1,0:T(8,128)(2,1)S(1)}, bf16[2,18,64,128]{3,2,1,0:T(8,128)(2,1)S(1)}, u32[]{:S(2)}, u32[]{:S(2)}) %collective-permute-start.7) | collective-permute-done | bytes 589856 | tf_op jit(solution)/shard_map/ppermute | solution.py:519
  92.0 9.7 %cross.6.refs_3_ = bf16[2,52,104,512]{3,2,1,0:T(8,128)(2,1)} custom-call(bf16[64,256,256]{2,1,0:T(8,128)(2,1)S(1)} %join.1.refs_0_, bf16[2,256,512]{2,1,0:T(8,128)(2,1)S(1)} %copy-done, bf16[16,64,128]{2,1,0:T(8,128)(2,1)S(1)} %collective-permute-done.2.near_side.refs_2_, ...), custom_call_target="tpu_custom_call", output_to_operand_aliasing={{}: (5, {})} | custom-call | flops 5100000256 | bytes 12582912 | tf_op jit(solution)/shard_map/cross/pallas_call | solution.py:448
  101.7 0.0 collective-permute-done.4.refs_2_
  101.8 6.5 %cross.7 = bf16[2,52,104,512]{3,2,1,0:T(8,128)(2,1)} custom-call(bf16[64,256,256]{2,1,0:T(8,128)(2,1)S(1)} %join.1.refs_0_, bf16[2,256,512]{2,1,0:T(8,128)(2,1)S(1)} %copy-done, bf16[2,16,64,128]{3,2,1,0:T(8,128)(2,1)S(1)} %collective-permute-done.4.refs_2_, bf16[2,52,104,512]{3,2,1,0:T(8,128)(2,1)} %cross.6.refs_3_), custom_call_target="tpu_custom_call", output_to_operand_aliasing={{}: (3, {})} | custom-call | flops 2400000000 | bytes 12582912 | tf_op jit(solution)/shard_map/cross/pallas_call | solution.py:448
Async XLA Ops:
  11.3 54.1 %copy-start.1 = (bf16[18,64,128]{2,1,0:T(8,128)(2,1)S(1)}, bf16[18,64,128]{2,1,0:T(8,128)(2,1)}, u32[]{:S(2)}) copy-start(bf16[18,64,128]{2,1,0:T(8,128)(2,1)} %get-tuple-element.17.keep) | copy-start | bytes 884740
  11.3 56.2 %collective-permute-start = (bf16[64,128,256]{2,1,0:T(8,128)(2,1)}, bf16[64,128,256]{2,1,0:T(8,128)(2,1)}, u32[]{:S(2)}, u32[]{:S(2)}) collective-permute-start(bf16[64,128,256]{2,1,0:T(8,128)(2,1)} %get-tuple-element.13.near_hbm), channel_id=1, source_target_pairs={{0,1},{1,0},{2,3},{3,2},{4,5},{5,4},{6,7},{7,6},{8,9},{9,8},{10,11... | collective-permute-start | bytes 12582920 | tf_op jit(solution)/shard_map/ppermute | solution.py:506
  11.9 26.8 %collective-permute-start.1 = (bf16[52,64,128]{2,1,0:T(8,128)(2,1)}, bf16[52,64,128]{2,1,0:T(8,128)(2,1)S(1)}, u32[]{:S(2)}, u32[]{:S(2)}) collective-permute-start(bf16[52,64,128]{2,1,0:T(8,128)(2,1)} %get-tuple-element.15), channel_id=1, source_target_pairs={{0,1},{1,0},{2,3},{3,2},{4,5},{5,4},{6,7},{7,6},{8,9},{9,8},{10,11... | collective-permute-start | bytes 2555912 | tf_op jit(solution)/shard_map/ppermute | solution.py:505
  19.9 12.5 %collective-permute-start.9 = (bf16[18,64,128]{2,1,0:T(8,128)(2,1)}, bf16[18,64,128]{2,1,0:T(8,128)(2,1)S(1)}, u32[]{:S(2)}, u32[]{:S(2)}) collective-permute-start(bf16[18,64,128]{2,1,0:T(8,128)(2,1)} %get-tuple-element.20), channel_id=1, source_target_pairs={{0,13},{1,12},{2,15},{3,14},{4,1},{5,0},{6,3},{7,2},{8,5},{9,4},{1... | collective-permute-start | bytes 884744 | tf_op jit(solution)/shard_map/ppermute | solution.py:503
  24.6 14.0 %collective-permute-start.8 = (bf16[18,64,128]{2,1,0:T(8,128)(2,1)}, bf16[18,64,128]{2,1,0:T(8,128)(2,1)S(1)}, u32[]{:S(2)}, u32[]{:S(2)}) collective-permute-start(bf16[18,64,128]{2,1,0:T(8,128)(2,1)} %get-tuple-element.19.keep), channel_id=1, source_target_pairs={{0,12},{1,13},{2,14},{3,15},{4,0},{5,1},{6,2},{7,3},{8,4},{9,5},{1... | collective-permute-start | bytes 884744 | tf_op jit(solution)/shard_map/ppermute | solution.py:503
  25.1 20.6 %collective-permute-start.3 = (bf16[16,64,128]{2,1,0:T(8,128)(2,1)}, bf16[16,64,128]{2,1,0:T(8,128)(2,1)S(1)}, u32[]{:S(2)}, u32[]{:S(2)}) collective-permute-start(bf16[16,64,128]{2,1,0:T(8,128)(2,1)} %get-tuple-element.16), channel_id=1, source_target_pairs={{0,13},{1,12},{2,15},{3,14},{4,1},{5,0},{6,3},{7,2},{8,5},{9,4},{1... | collective-permute-start | bytes 786440 | tf_op jit(solution)/shard_map/ppermute | solution.py:503
  38.7 1.0 copy-start.2
  39.9 38.1 %collective-permute-start.10 = (bf16[2,18,64,128]{3,2,1,0:T(8,128)(2,1)S(1)}, bf16[2,18,64,128]{3,2,1,0:T(8,128)(2,1)S(1)}, u32[]{:S(2)}, u32[]{:S(2)}) collective-permute-start(bf16[2,18,64,128]{3,2,1,0:T(8,128)(2,1)S(1)} %payload.5), channel_id=1, source_target_pairs={{0,2},{2,0},{4,6},{6,4},{8,10},{10,8},{12,14},{14,12},{1,3},{3,1},... | collective-permute-start | bytes 1769480 | tf_op jit(solution)/shard_map/ppermute | solution.py:519
  41.5 23.9 %collective-permute-start.6 = (bf16[18,64,128]{2,1,0:T(8,128)(2,1)}, bf16[18,64,128]{2,1,0:T(8,128)(2,1)S(1)}, u32[]{:S(2)}, u32[]{:S(2)}) collective-permute-start(bf16[18,64,128]{2,1,0:T(8,128)(2,1)} %get-tuple-element.18), channel_id=1, source_target_pairs={{0,13},{1,12},{2,15},{3,14},{4,1},{5,0},{6,3},{7,2},{8,5},{9,4},{1... | collective-permute-start | bytes 884744 | tf_op jit(solution)/shard_map/ppermute | solution.py:503
  44.7 20.8 %collective-permute-start.5 = (bf16[18,64,128]{2,1,0:T(8,128)(2,1)}, bf16[18,64,128]{2,1,0:T(8,128)(2,1)S(1)}, u32[]{:S(2)}, u32[]{:S(2)}) collective-permute-start(bf16[18,64,128]{2,1,0:T(8,128)(2,1)} %get-tuple-element.17.keep), channel_id=1, source_target_pairs={{0,12},{1,13},{2,14},{3,15},{4,0},{5,1},{6,2},{7,3},{8,4},{9,5},{1... | collective-permute-start | bytes 884744 | tf_op jit(solution)/shard_map/ppermute | solution.py:503
  45.7 18.1 %collective-permute-start.2 = (bf16[16,64,128]{2,1,0:T(8,128)(2,1)}, bf16[16,64,128]{2,1,0:T(8,128)(2,1)S(1)}, u32[]{:S(2)}, u32[]{:S(2)}) collective-permute-start(bf16[16,64,128]{2,1,0:T(8,128)(2,1)} %get-tuple-element.14.keep), channel_id=1, source_target_pairs={{0,12},{1,13},{2,14},{3,15},{4,0},{5,1},{6,2},{7,3},{8,4},{9,5},{1... | collective-permute-start | bytes 786440 | tf_op jit(solution)/shard_map/ppermute | solution.py:503
  63.8 0.9 copy-start.3
  64.9 36.8 %collective-permute-start.4 = (bf16[2,16,64,128]{3,2,1,0:T(8,128)(2,1)S(1)}, bf16[2,16,64,128]{3,2,1,0:T(8,128)(2,1)S(1)}, u32[]{:S(2)}, u32[]{:S(2)}) collective-permute-start(bf16[2,16,64,128]{3,2,1,0:T(8,128)(2,1)S(1)} %payload.3), channel_id=1, source_target_pairs={{0,2},{2,0},{4,6},{6,4},{8,10},{10,8},{12,14},{14,12},{1,3},{3,1},... | collective-permute-start | bytes 1572872 | tf_op jit(solution)/shard_map/ppermute | solution.py:519
  66.0 5.1 %copy-start = (bf16[2,256,512]{2,1,0:T(8,128)(2,1)S(1)}, bf16[2,256,512]{2,1,0:T(8,128)(2,1)}, u32[]{:S(2)}) copy-start(bf16[2,256,512]{2,1,0:T(8,128)(2,1)} %constant.25.refs_1_) | copy-start | bytes 1572868
  66.0 26.1 %collective-permute-start.7 = (bf16[2,18,64,128]{3,2,1,0:T(8,128)(2,1)S(1)}, bf16[2,18,64,128]{3,2,1,0:T(8,128)(2,1)S(1)}, u32[]{:S(2)}, u32[]{:S(2)}) collective-permute-start(bf16[2,18,64,128]{3,2,1,0:T(8,128)(2,1)S(1)} %payload.4), channel_id=1, source_target_pairs={{0,2},{2,0},{4,6},{6,4},{8,10},{10,8},{12,14},{14,12},{1,3},{3,1},... | collective-permute-start | bytes 1769480 | tf_op jit(solution)/shard_map/ppermute | solution.py:519

commit v4 on v3

--- a/solution.py
+++ b/solution.py
@@ -216,9 +216,7 @@
                 for s in range(2)
             ]
             plain = jnp.concatenate([p for pair in zip(real, imag) for p in pair], axis=0)
-            turned = jnp.concatenate([p for r, i in zip(real, imag) for p in (i, -r)], axis=0)
-            own[position, :, :LANES] = plain.astype(bf16)
-            own[position, :, LANES:] = turned.astype(bf16)
+            own[position] = plain.astype(bf16)
             flipped = jnp.transpose(plain)
             for c in range(0, row_count, 8):
                 rows32[pl.ds(c * OCTETS + position, 8, stride=OCTETS), :] = flipped[c : c + 8]
@@ -248,7 +246,7 @@
     row_count = signal.shape[0]
     spans = signal.shape[1] // WINDOW
     shapes = [(rows, OCTETS, LANES) for rows in chunks[1:] for _ in range(2)]
-    give, own = (half, OCTETS, LANES), (OCTETS, LANES, 2 * LANES)
+    give, own = (half, OCTETS, LANES), (OCTETS, LANES, LANES)
     vmem = pl.BlockSpec(memory_space=pltpu.VMEM)
     hbm = pl.BlockSpec(memory_space=pltpu.MemorySpace.HBM)
     return pl.pallas_call(
@@ -275,15 +273,37 @@
     )(me, signal, flags, table, taper)
 
 
-def join_kernel(near_hbm, far_hbm, out_ref, sem):
-    copies = [
-        pltpu.make_async_copy(side, out_ref.at[:, pl.ds(i * LANES, LANES), :], sem.at[i])
-        for i, side in enumerate((near_hbm, far_hbm))
-    ]
-    for copy in copies:
-        copy.start()
-    for copy in copies:
-        copy.wait()
+def join_kernel(near_hbm, far_hbm, out_ref, held, sem):
+    groups = sem.shape[1]
+    per = OCTETS // groups
+
+    def copies(g):
+        part = pl.ds(g * per, per)
+        return [
+            pltpu.make_async_copy(side.at[part], held.at[i, part], sem.at[i, g])
+            for i, side in enumerate((near_hbm, far_hbm))
+        ]
+
+    for g in range(groups):
+        for copy in copies(g):
+            copy.start()
+
+    def group(g, carry):
+        for copy in copies(g):
+            copy.wait()
+        for i in range(2):
+            for n in range(per):
+                value = held[i, g * per + n]
+                wide = value.astype(f32)
+                turned = []
+                for r in range(0, LANES, 16):
+                    turned += [wide[r + 8 : r + 16], -wide[r : r + 8]]
+                rows = pl.ds(i * LANES, LANES)
+                out_ref[g * per + n, rows, :LANES] = value
+                out_ref[g * per + n, rows, LANES:] = jnp.concatenate(turned, axis=0).astype(bf16)
+        return carry
+
+    lax.fori_loop(0, groups, group, 0)
 
 
 def join(near, far):
@@ -293,9 +313,12 @@
         out_shape=pltpu.VMEM((OCTETS, 2 * LANES, 2 * LANES), bf16),
         in_specs=[hbm] * 2,
         out_specs=pl.BlockSpec(memory_space=pltpu.VMEM),
-        scratch_shapes=[pltpu.SemaphoreType.DMA((2,))],
+        scratch_shapes=[
+            pltpu.VMEM((2,) + near.shape, bf16),
+            pltpu.SemaphoreType.DMA((2, 8)),
+        ],
         compiler_params=pltpu.CompilerParams(vmem_limit_bytes=48 << 20),
-        cost_estimate=pl.CostEstimate(flops=0, bytes_accessed=17 << 20, transcendentals=0),
+        cost_estimate=pl.CostEstimate(flops=0, bytes_accessed=13 << 20, transcendentals=0),
         name="join",
     )(near, far)
 

time: 109 us -> 108 us (level)
  Pallas kernels: 56.9 us -> 55.6 us
  waiting for transfers between devices: 33 us -> 34.2 us
    ppermute x3, waiting for transfers between devices: 3.81 us -> 4.94 us  [local(): one_away.append(lax.ppermute(load, 'chan', swap))]
  transfers between devices with their start and end apart: 11 -> 11, of which waited for: 4 -> 4; matrix products, arithmetic and copies ran while one was open for 0% -> 0% of each run, Pallas kernels for 36% -> 35%
where the time goes in v4:
time: 108 us
  Pallas kernels  55.6 us (51%)
  waiting for transfers between devices  34.2 us (32%)
  starting transfers between devices  16.2 us (15%)
  local copies, waits for them, and re-layouts  1.92 us (2%)
    pallas_call x4, Pallas kernels, cross_part(): pl.pallas_call(functools.partial(cross_kernel, tuple(parts), row_count, p...  33.4 us
    ppermute x6, waiting for transfers between devices, local(): lax.ppermute(x, axes, back(2, i % 2))  29.2 us
    ppermute x6, starting transfers between devices, local(): lax.ppermute(x, axes, back(2, i % 2))  11.8 us
    pallas_call x1, Pallas kernels, spectra(): pl.pallas_call(functools.partial(spectra_kernel, chunks, half), out_shape...  11 us
    pallas_call x1, Pallas kernels, first_spectra(): pl.pallas_call(functools.partial(first_kernel, rows, half, tuple(bounds))...  7.91 us
    ppermute x3, waiting for transfers between devices, local(): one_away.append(lax.ppermute(load, 'chan', swap))  4.94 us
    ppermute x3, starting transfers between devices, local(): one_away.append(lax.ppermute(load, 'chan', swap))  3.79 us
    pallas_call x1, Pallas kernels, join(): pl.pallas_call(join_kernel, out_shape=pltpu.VMEM((OCTETS, 2 * LANES, 2 *...  2.42 us
  transfers between devices with their start and end apart: 11, of which 4 were waited for; matrix products, arithmetic and copies ran while one was open for 0% of the time, Pallas kernels for 35%

profile of v4, /device:TPU:0, one launch (start us, length us, event | category | flops | bytes accessed | tf_op | source)
XLA Modules:
  0.0 108.1 jit_solution(15745779239620653501)
XLA Ops:
  0.0 11.0 %spectra.1 = (bf16[18,64,128]{2,1,0:T(8,128)(2,1)}, bf16[18,64,128]{2,1,0:T(8,128)(2,1)}, bf16[16,64,128]{2,1,0:T(8,128)(2,1)}, bf16[16,64,128]{2,1,0:T(8,128)(2...) custom-call(s32[1]{0:T(128)} %bitcast.me_ref, f32[104,8192]{1,0:T(8,128)} %signal_hbm.3, ...), custom_call_target="tpu_custom_call" | custom-call | flops 2147483648 | bytes 12582912 | tf_op jit(solution)/shard_map/spectra/pallas_call | solution.py:252
  11.0 0.0 copy-start.1
  11.0 0.5 collective-permute-start
  11.6 0.1 collective-permute-start.1
  11.6 7.9 %first.1 = (bf16[18,64,128]{2,1,0:T(8,128)(2,1)}, bf16[18,64,128]{2,1,0:T(8,128)(2,1)}) custom-call(s32[1]{0:T(128)} %bitcast.me_ref, f32[104,8192]{1,0:T(8,128)} %signal_hbm.3, s32[8,104]{1,0:T(8,128)} %bitcast.4, bf16[1024,1024]{1,0:T(8,128)(2,1)} %constant.24.table_hbm, f32[1,1024]{1,0:T(1,128)} %constant.20.clone.taper_ref), custom_call_target="tpu_custom_call" | custom-call | flops 1073741824 | bytes 6291456 | tf_op jit(solution)/shard_map/first/pallas_call | solution.py:158
  19.5 4.7 %collective-permute-start.9 = (bf16[18,64,128]{2,1,0:T(8,128)(2,1)}, bf16[18,64,128]{2,1,0:T(8,128)(2,1)S(1)}, u32[]{:S(2)}, u32[]{:S(2)}) collective-permute-start(bf16[18,64,128]{2,1,0:T(8,128)(2,1)} %get-tuple-element.20), channel_id=1, source_target_pairs={{0,13},{1,12},{2,15},{3,14},{4,1},{5,0},{6,3},{7,2},{8,5},{9,4},{1... | collective-permute-start | bytes 884744 | tf_op jit(solution)/shard_map/ppermute | solution.py:526
  24.3 0.5 collective-permute-start.8
  24.8 0.2 collective-permute-start.3
  24.9 7.1 %collective-permute-done.9.far_side.refs_3_ = bf16[18,64,128]{2,1,0:T(8,128)(2,1)S(1)} collective-permute-done((bf16[18,64,128]{2,1,0:T(8,128)(2,1)}, bf16[18,64,128]{2,1,0:T(8,128)(2,1)S(1)}, u32[]{:S(2)}, u32[]{:S(2)}) %collective-permute-start.9) | collective-permute-done | bytes 294944 | tf_op jit(solution)/shard_map/ppermute | solution.py:526
  32.0 6.3 %collective-permute-done.8.near_side.refs_2_ = bf16[18,64,128]{2,1,0:T(8,128)(2,1)S(1)} collective-permute-done((bf16[18,64,128]{2,1,0:T(8,128)(2,1)}, bf16[18,64,128]{2,1,0:T(8,128)(2,1)S(1)}, u32[]{:S(2)}, u32[]{:S(2)}) %collective-permute-start.8) | collective-permute-done | bytes 294944 | tf_op jit(solution)/shard_map/ppermute | solution.py:526
  38.3 0.0 collective-permute-done.1.taken
  38.3 0.0 copy-start.2
  38.3 1.0 copy-done.2
  39.3 0.3 payload.5
  39.6 1.6 %collective-permute-start.10 = (bf16[2,18,64,128]{3,2,1,0:T(8,128)(2,1)S(1)}, bf16[2,18,64,128]{3,2,1,0:T(8,128)(2,1)S(1)}, u32[]{:S(2)}, u32[]{:S(2)}) collective-permute-start(bf16[2,18,64,128]{3,2,1,0:T(8,128)(2,1)S(1)} %payload.5), channel_id=1, source_target_pairs={{0,2},{2,0},{4,6},{6,4},{8,10},{10,8},{12,14},{14,12},{1,3},{3,1},... | collective-permute-start | bytes 1769480 | tf_op jit(solution)/shard_map/ppermute | solution.py:542
  41.2 3.1 %collective-permute-start.6 = (bf16[18,64,128]{2,1,0:T(8,128)(2,1)}, bf16[18,64,128]{2,1,0:T(8,128)(2,1)S(1)}, u32[]{:S(2)}, u32[]{:S(2)}) collective-permute-start(bf16[18,64,128]{2,1,0:T(8,128)(2,1)} %get-tuple-element.18), channel_id=1, source_target_pairs={{0,13},{1,12},{2,15},{3,14},{4,1},{5,0},{6,3},{7,2},{8,5},{9,4},{1... | collective-permute-start | bytes 884744 | tf_op jit(solution)/shard_map/ppermute | solution.py:526
  44.3 1.1 %collective-permute-start.5 = (bf16[18,64,128]{2,1,0:T(8,128)(2,1)}, bf16[18,64,128]{2,1,0:T(8,128)(2,1)S(1)}, u32[]{:S(2)}, u32[]{:S(2)}) collective-permute-start(bf16[18,64,128]{2,1,0:T(8,128)(2,1)} %get-tuple-element.17.keep), channel_id=1, source_target_pairs={{0,12},{1,13},{2,14},{3,15},{4,0},{5,1},{6,2},{7,3},{8,4},{9,5},{1... | collective-permute-start | bytes 884744 | tf_op jit(solution)/shard_map/ppermute | solution.py:526
  45.4 0.0 collective-permute-done.3.far_side.refs_3_
  45.4 0.0 copy-start
  45.4 2.2 %collective-permute-start.2 = (bf16[16,64,128]{2,1,0:T(8,128)(2,1)}, bf16[16,64,128]{2,1,0:T(8,128)(2,1)S(1)}, u32[]{:S(2)}, u32[]{:S(2)}) collective-permute-start(bf16[16,64,128]{2,1,0:T(8,128)(2,1)} %get-tuple-element.14.keep), channel_id=1, source_target_pairs={{0,12},{1,13},{2,14},{3,15},{4,0},{5,1},{6,2},{7,3},{8,4},{9,5},{1... | collective-permute-start | bytes 786440 | tf_op jit(solution)/shard_map/ppermute | solution.py:526
  47.6 15.8 %collective-permute-done.2.near_side.refs_2_ = bf16[16,64,128]{2,1,0:T(8,128)(2,1)S(1)} collective-permute-done((bf16[16,64,128]{2,1,0:T(8,128)(2,1)}, bf16[16,64,128]{2,1,0:T(8,128)(2,1)S(1)}, u32[]{:S(2)}, u32[]{:S(2)}) %collective-permute-start.2) | collective-permute-done | bytes 262176 | tf_op jit(solution)/shard_map/ppermute | solution.py:526
  63.4 0.0 copy-start.3
  63.4 0.9 copy-done.3
  64.4 0.1 payload.3
  64.5 0.6 collective-permute-start.4
  65.1 0.0 collective-permute-done.6.far_side.refs_3_
  65.1 0.0 collective-permute-done.5.near_side.refs_2_
  65.1 0.0 copy-done.1
  65.1 0.5 payload.4
  65.6 1.6 %collective-permute-start.7 = (bf16[2,18,64,128]{3,2,1,0:T(8,128)(2,1)S(1)}, bf16[2,18,64,128]{3,2,1,0:T(8,128)(2,1)S(1)}, u32[]{:S(2)}, u32[]{:S(2)}) collective-permute-start(bf16[2,18,64,128]{3,2,1,0:T(8,128)(2,1)S(1)} %payload.4), channel_id=1, source_target_pairs={{0,2},{2,0},{4,6},{6,4},{8,10},{10,8},{12,14},{14,12},{1,3},{3,1},... | collective-permute-start | bytes 1769480 | tf_op jit(solution)/shard_map/ppermute | solution.py:542
  67.1 0.0 collective-permute-done.far_hbm
  67.1 2.4 %join.1.refs_0_ = bf16[64,256,256]{2,1,0:T(8,128)(2,1)S(1)} custom-call(bf16[64,128,128]{2,1,0:T(8,128)(2,1)} %get-tuple-element.13.near_hbm, bf16[64,128,128]{2,1,0:T(8,128)(2,1)} %collective-permute-done.far_hbm), custom_call_target="tpu_custom_call" | custom-call | bytes 13631488 | tf_op jit(solution)/shard_map/join/pallas_call | solution.py:311
  69.6 0.0 copy-done
  69.6 6.9 %cross.4.refs_5_ = bf16[2,52,104,512]{3,2,1,0:T(8,128)(2,1)} custom-call(bf16[64,256,256]{2,1,0:T(8,128)(2,1)S(1)} %join.1.refs_0_, bf16[2,256,512]{2,1,0:T(8,128)(2,1)S(1)} %copy-done, bf16[18,64,128]{2,1,0:T(8,128)(2,1)S(1)} %collective-permute-done.8.near_side.refs_2_, bf16[18,64,128]{2,1,0:T(8,128)(2,1)S(1)} %collective-permute-done.9.far_side.refs_3_), custom_call_target="tpu_custom_call" | custom-call | flops 2700000000 | bytes 12582912 | tf_op jit(solution)/shard_map/cross/pallas_call | solution.py:471
  76.5 0.0 collective-permute-done.10.refs_4_
  76.5 10.2 %cross.5.refs_5_ = bf16[2,52,104,512]{3,2,1,0:T(8,128)(2,1)} custom-call(bf16[64,256,256]{2,1,0:T(8,128)(2,1)S(1)} %join.1.refs_0_, bf16[2,256,512]{2,1,0:T(8,128)(2,1)S(1)} %copy-done, bf16[18,64,128]{2,1,0:T(8,128)(2,1)S(1)} %collective-permute-done.5.near_side.refs_2_, ...), custom_call_target="tpu_custom_call", output_to_operand_aliasing={{}: (5, {})} | custom-call | flops 5400000000 | bytes 12582912 | tf_op jit(solution)/shard_map/cross/pallas_call | solution.py:471
  86.7 4.9 %collective-permute-done.7.refs_4_ = bf16[2,18,64,128]{3,2,1,0:T(8,128)(2,1)S(1)} collective-permute-done((bf16[2,18,64,128]{3,2,1,0:T(8,128)(2,1)S(1)}, bf16[2,18,64,128]{3,2,1,0:T(8,128)(2,1)S(1)}, u32[]{:S(2)}, u32[]{:S(2)}) %collective-permute-start.7) | collective-permute-done | bytes 589856 | tf_op jit(solution)/shard_map/ppermute | solution.py:542
  91.7 9.7 %cross.6.refs_3_ = bf16[2,52,104,512]{3,2,1,0:T(8,128)(2,1)} custom-call(bf16[64,256,256]{2,1,0:T(8,128)(2,1)S(1)} %join.1.refs_0_, bf16[2,256,512]{2,1,0:T(8,128)(2,1)S(1)} %copy-done, bf16[16,64,128]{2,1,0:T(8,128)(2,1)S(1)} %collective-permute-done.2.near_side.refs_2_, ...), custom_call_target="tpu_custom_call", output_to_operand_aliasing={{}: (5, {})} | custom-call | flops 5100000256 | bytes 12582912 | tf_op jit(solution)/shard_map/cross/pallas_call | solution.py:471
  101.4 0.0 collective-permute-done.4.refs_2_
  101.4 6.5 %cross.7 = bf16[2,52,104,512]{3,2,1,0:T(8,128)(2,1)} custom-call(bf16[64,256,256]{2,1,0:T(8,128)(2,1)S(1)} %join.1.refs_0_, bf16[2,256,512]{2,1,0:T(8,128)(2,1)S(1)} %copy-done, bf16[2,16,64,128]{3,2,1,0:T(8,128)(2,1)S(1)} %collective-permute-done.4.refs_2_, bf16[2,52,104,512]{3,2,1,0:T(8,128)(2,1)} %cross.6.refs_3_), custom_call_target="tpu_custom_call", output_to_operand_aliasing={{}: (3, {})} | custom-call | flops 2400000000 | bytes 12582912 | tf_op jit(solution)/shard_map/cross/pallas_call | solution.py:471
Async XLA Ops:
  11.0 54.1 %copy-start.1 = (bf16[18,64,128]{2,1,0:T(8,128)(2,1)S(1)}, bf16[18,64,128]{2,1,0:T(8,128)(2,1)}, u32[]{:S(2)}) copy-start(bf16[18,64,128]{2,1,0:T(8,128)(2,1)} %get-tuple-element.17.keep) | copy-start | bytes 884740
  11.0 56.1 %collective-permute-start = (bf16[64,128,128]{2,1,0:T(8,128)(2,1)}, bf16[64,128,128]{2,1,0:T(8,128)(2,1)}, u32[]{:S(2)}, u32[]{:S(2)}) collective-permute-start(bf16[64,128,128]{2,1,0:T(8,128)(2,1)} %get-tuple-element.13.near_hbm), channel_id=1, source_target_pairs={{0,1},{1,0},{2,3},{3,2},{4,5},{5,4},{6,7},{7,6},{8,9},{9,8},{10,11... | collective-permute-start | bytes 6291464 | tf_op jit(solution)/shard_map/ppermute | solution.py:529
  11.6 26.8 %collective-permute-start.1 = (bf16[52,64,128]{2,1,0:T(8,128)(2,1)}, bf16[52,64,128]{2,1,0:T(8,128)(2,1)S(1)}, u32[]{:S(2)}, u32[]{:S(2)}) collective-permute-start(bf16[52,64,128]{2,1,0:T(8,128)(2,1)} %get-tuple-element.15), channel_id=1, source_target_pairs={{0,1},{1,0},{2,3},{3,2},{4,5},{5,4},{6,7},{7,6},{8,9},{9,8},{10,11... | collective-permute-start | bytes 2555912 | tf_op jit(solution)/shard_map/ppermute | solution.py:528
  19.5 12.5 %collective-permute-start.9 = (bf16[18,64,128]{2,1,0:T(8,128)(2,1)}, bf16[18,64,128]{2,1,0:T(8,128)(2,1)S(1)}, u32[]{:S(2)}, u32[]{:S(2)}) collective-permute-start(bf16[18,64,128]{2,1,0:T(8,128)(2,1)} %get-tuple-element.20), channel_id=1, source_target_pairs={{0,13},{1,12},{2,15},{3,14},{4,1},{5,0},{6,3},{7,2},{8,5},{9,4},{1... | collective-permute-start | bytes 884744 | tf_op jit(solution)/shard_map/ppermute | solution.py:526
  24.3 14.0 %collective-permute-start.8 = (bf16[18,64,128]{2,1,0:T(8,128)(2,1)}, bf16[18,64,128]{2,1,0:T(8,128)(2,1)S(1)}, u32[]{:S(2)}, u32[]{:S(2)}) collective-permute-start(bf16[18,64,128]{2,1,0:T(8,128)(2,1)} %get-tuple-element.19.keep), channel_id=1, source_target_pairs={{0,12},{1,13},{2,14},{3,15},{4,0},{5,1},{6,2},{7,3},{8,4},{9,5},{1... | collective-permute-start | bytes 884744 | tf_op jit(solution)/shard_map/ppermute | solution.py:526
  24.8 20.6 %collective-permute-start.3 = (bf16[16,64,128]{2,1,0:T(8,128)(2,1)}, bf16[16,64,128]{2,1,0:T(8,128)(2,1)S(1)}, u32[]{:S(2)}, u32[]{:S(2)}) collective-permute-start(bf16[16,64,128]{2,1,0:T(8,128)(2,1)} %get-tuple-element.16), channel_id=1, source_target_pairs={{0,13},{1,12},{2,15},{3,14},{4,1},{5,0},{6,3},{7,2},{8,5},{9,4},{1... | collective-permute-start | bytes 786440 | tf_op jit(solution)/shard_map/ppermute | solution.py:526
  38.3 1.0 copy-start.2
  39.6 37.0 %collective-permute-start.10 = (bf16[2,18,64,128]{3,2,1,0:T(8,128)(2,1)S(1)}, bf16[2,18,64,128]{3,2,1,0:T(8,128)(2,1)S(1)}, u32[]{:S(2)}, u32[]{:S(2)}) collective-permute-start(bf16[2,18,64,128]{3,2,1,0:T(8,128)(2,1)S(1)} %payload.5), channel_id=1, source_target_pairs={{0,2},{2,0},{4,6},{6,4},{8,10},{10,8},{12,14},{14,12},{1,3},{3,1},... | collective-permute-start | bytes 1769480 | tf_op jit(solution)/shard_map/ppermute | solution.py:542
  41.2 23.8 %collective-permute-start.6 = (bf16[18,64,128]{2,1,0:T(8,128)(2,1)}, bf16[18,64,128]{2,1,0:T(8,128)(2,1)S(1)}, u32[]{:S(2)}, u32[]{:S(2)}) collective-permute-start(bf16[18,64,128]{2,1,0:T(8,128)(2,1)} %get-tuple-element.18), channel_id=1, source_target_pairs={{0,13},{1,12},{2,15},{3,14},{4,1},{5,0},{6,3},{7,2},{8,5},{9,4},{1... | collective-permute-start | bytes 884744 | tf_op jit(solution)/shard_map/ppermute | solution.py:526
  44.3 20.8 %collective-permute-start.5 = (bf16[18,64,128]{2,1,0:T(8,128)(2,1)}, bf16[18,64,128]{2,1,0:T(8,128)(2,1)S(1)}, u32[]{:S(2)}, u32[]{:S(2)}) collective-permute-start(bf16[18,64,128]{2,1,0:T(8,128)(2,1)} %get-tuple-element.17.keep), channel_id=1, source_target_pairs={{0,12},{1,13},{2,14},{3,15},{4,0},{5,1},{6,2},{7,3},{8,4},{9,5},{1... | collective-permute-start | bytes 884744 | tf_op jit(solution)/shard_map/ppermute | solution.py:526
  45.4 24.2 %copy-start = (bf16[2,256,512]{2,1,0:T(8,128)(2,1)S(1)}, bf16[2,256,512]{2,1,0:T(8,128)(2,1)}, u32[]{:S(2)}) copy-start(bf16[2,256,512]{2,1,0:T(8,128)(2,1)} %constant.25.refs_1_) | copy-start | bytes 1572868
  45.4 18.0 %collective-permute-start.2 = (bf16[16,64,128]{2,1,0:T(8,128)(2,1)}, bf16[16,64,128]{2,1,0:T(8,128)(2,1)S(1)}, u32[]{:S(2)}, u32[]{:S(2)}) collective-permute-start(bf16[16,64,128]{2,1,0:T(8,128)(2,1)} %get-tuple-element.14.keep), channel_id=1, source_target_pairs={{0,12},{1,13},{2,14},{3,15},{4,0},{5,1},{6,2},{7,3},{8,4},{9,5},{1... | collective-permute-start | bytes 786440 | tf_op jit(solution)/shard_map/ppermute | solution.py:526
  63.4 0.9 copy-start.3
  64.5 36.9 %collective-permute-start.4 = (bf16[2,16,64,128]{3,2,1,0:T(8,128)(2,1)S(1)}, bf16[2,16,64,128]{3,2,1,0:T(8,128)(2,1)S(1)}, u32[]{:S(2)}, u32[]{:S(2)}) collective-permute-start(bf16[2,16,64,128]{3,2,1,0:T(8,128)(2,1)S(1)} %payload.3), channel_id=1, source_target_pairs={{0,2},{2,0},{4,6},{6,4},{8,10},{10,8},{12,14},{14,12},{1,3},{3,1},... | collective-permute-start | bytes 1572872 | tf_op jit(solution)/shard_map/ppermute | solution.py:542
  65.6 26.1 %collective-permute-start.7 = (bf16[2,18,64,128]{3,2,1,0:T(8,128)(2,1)S(1)}, bf16[2,18,64,128]{3,2,1,0:T(8,128)(2,1)S(1)}, u32[]{:S(2)}, u32[]{:S(2)}) collective-permute-start(bf16[2,18,64,128]{3,2,1,0:T(8,128)(2,1)S(1)} %payload.4), channel_id=1, source_target_pairs={{0,2},{2,0},{4,6},{6,4},{8,10},{10,8},{12,14},{14,12},{1,3},{3,1},... | collective-permute-start | bytes 1769480 | tf_op jit(solution)/shard_map/ppermute | solution.py:542

commit v5 on v4

--- a/solution.py
+++ b/solution.py
@@ -115,7 +115,6 @@
             [flags[2 * v : 2 * v + 1], flags[2 * v + 1 : 2 * v + 2]], axis=1
         )
     taper = taper_ref[...]
-    tap[...] = jnp.zeros_like(tap)
     for copy in loads:
         copy.wait()
     for w in range(spans):
@@ -179,8 +178,8 @@
     chunks, half, me_ref, signal_hbm, flags_ref, table_hbm, taper_ref, *refs
 ):
     count = 2 * len(chunks) - 2
-    pieces, (give_hbm, own_hbm) = refs[:count], refs[count : count + 2]
-    signal, tap, table, rows32, live, own, give, in_sem, table_sem, own_sem, give_sem = refs[count + 2 :]
+    pieces, own_hbm = refs[:count], refs[count]
+    signal, tap, table, rows32, live, own, in_sem, table_sem, own_sem = refs[count + 1 :]
     row_count = signal.shape[0]
     spans = signal.shape[1] // WINDOW
     loads = []
@@ -193,7 +192,6 @@
     for copy in tables:
         copy.start()
     taper = taper_ref[...]
-    tap[...] = jnp.zeros_like(tap)
     live[...] = jnp.zeros_like(live)
     live[:, :row_count] = flags_ref[...].astype(f32)
     for w in range(spans):
@@ -230,9 +228,6 @@
         value = rows32[pl.ds(pl.multiple_of(first * OCTETS, OCTETS), rows * OCTETS), :]
         return value.astype(bf16).reshape(rows, OCTETS, LANES)
 
-    give[...] = block(1, 0, half)
-    leaving.append(pltpu.make_async_copy(give, give_hbm, give_sem))
-    leaving[-1].start()
     start = chunks[0]
     for k, rows in enumerate(chunks[1:]):
         for side in range(2):
@@ -246,14 +241,14 @@
     row_count = signal.shape[0]
     spans = signal.shape[1] // WINDOW
     shapes = [(rows, OCTETS, LANES) for rows in chunks[1:] for _ in range(2)]
-    give, own = (half, OCTETS, LANES), (OCTETS, LANES, LANES)
+    own = (OCTETS, LANES, LANES)
     vmem = pl.BlockSpec(memory_space=pltpu.VMEM)
     hbm = pl.BlockSpec(memory_space=pltpu.MemorySpace.HBM)
     return pl.pallas_call(
         functools.partial(spectra_kernel, chunks, half),
-        out_shape=[jax.ShapeDtypeStruct(shape, bf16) for shape in shapes + [give, own]],
+        out_shape=[jax.ShapeDtypeStruct(shape, bf16) for shape in shapes + [own]],
         in_specs=[pl.BlockSpec(memory_space=pltpu.SMEM), hbm, vmem, hbm, vmem],
-        out_specs=[vmem] * len(shapes) + [hbm] * 2,
+        out_specs=[vmem] * len(shapes) + [hbm],
         scratch_shapes=[
             pltpu.VMEM((row_count, spans * WINDOW), f32),
             pltpu.VMEM((spans * LANES, WINDOW), bf16),
@@ -261,11 +256,9 @@
             pltpu.VMEM((row_count * OCTETS, LANES), f32),
             pltpu.VMEM((spans, LANES), f32),
             pltpu.VMEM(own, bf16),
-            pltpu.VMEM(give, bf16),
             pltpu.SemaphoreType.DMA((spans,)),
             pltpu.SemaphoreType.DMA((4,)),
             pltpu.SemaphoreType.DMA((4,)),
-            pltpu.SemaphoreType.DMA,
         ],
         compiler_params=pltpu.CompilerParams(vmem_limit_bytes=62 << 20),
         cost_estimate=pl.CostEstimate(flops=2 * WINDOW**3, bytes_accessed=12 << 20, transcendentals=0),
@@ -317,17 +310,16 @@
             pltpu.VMEM((2,) + near.shape, bf16),
             pltpu.SemaphoreType.DMA((2, 8)),
         ],
-        compiler_params=pltpu.CompilerParams(vmem_limit_bytes=48 << 20),
+        compiler_params=pltpu.CompilerParams(vmem_limit_bytes=54 << 20),
         cost_estimate=pl.CostEstimate(flops=0, bytes_accessed=13 << 20, transcendentals=0),
         name="join",
     )(near, far)
 
 
-def payload_kernel(first, rows, odd_ref, keep, taken, near_side, far_side, out_ref, hold, in_sem, out_sem):
+def payload_kernel(odd_ref, keep, taken, near_side, far_side, out_ref, hold, in_sem, out_sem):
     odd = odd_ref[0]
-    span = pl.ds(first, rows)
     own = [pltpu.make_async_copy(keep, hold.at[0], in_sem.at[0]),
-           pltpu.make_async_copy(taken.at[span], hold.at[1], in_sem.at[1])]
+           pltpu.make_async_copy(taken, hold.at[1], in_sem.at[1])]
     come = [pltpu.make_async_copy(near_side, hold.at[0], in_sem.at[0]),
             pltpu.make_async_copy(far_side, hold.at[1], in_sem.at[1])]
     for i in range(2):
@@ -341,11 +333,11 @@
         leave[i].wait()
 
 
-def payload(odd, keep, taken, near_side, far_side, first):
+def payload(odd, keep, taken, near_side, far_side, grant):
     hbm = pl.BlockSpec(memory_space=pltpu.MemorySpace.HBM)
     shape = (2,) + keep.shape
     return pl.pallas_call(
-        functools.partial(payload_kernel, first, keep.shape[0]),
+        payload_kernel,
         out_shape=jax.ShapeDtypeStruct(shape, bf16),
         in_specs=[pl.BlockSpec(memory_space=pltpu.SMEM)] + [hbm] * 4,
         out_specs=hbm,
@@ -354,7 +346,7 @@
             pltpu.SemaphoreType.DMA((2,)),
             pltpu.SemaphoreType.DMA((2,)),
         ],
-        compiler_params=pltpu.CompilerParams(vmem_limit_bytes=48 << 20),
+        compiler_params=pltpu.CompilerParams(vmem_limit_bytes=grant << 20),
         cost_estimate=pl.CostEstimate(flops=0, bytes_accessed=2 << 20, transcendentals=0),
         name="payload",
     )(odd, keep, taken, near_side, far_side)
@@ -512,7 +504,7 @@
     flags = valid_flags.T
     table, taper = forward_rows(), taper_row()
     pieces = list(first_spectra(me[None], signal, flags, table, taper, chunks[0], local_rows))
-    *more, give, near = spectra(me[None], signal, flags, table, taper, chunks, local_rows)
+    *more, near = spectra(me[None], signal, flags, table, taper, chunks, local_rows)
     pieces += more
 
     def back(hops, side):
@@ -525,7 +517,7 @@
     axes = ("chan", "tm")
     two_away = [lax.ppermute(x, axes, back(2, i % 2)) for i, x in enumerate(pieces)]
     other = [(t, 1 - t) for t in range(owner_count)]
-    taken = lax.ppermute(give, "tm", other)
+    taken = [lax.ppermute(x, "tm", other) for x in pieces[1::2]]
     far = lax.ppermute(near, "tm", other)
     weights = join(near, far)
     swap = [(b, b - 1 if b % 2 else b + 1) for b in range(blocks)]
@@ -538,7 +530,7 @@
         parts, sources = [], []
         if k < len(chunks):
             sent = two_away[2 * k : 2 * k + 2]
-            load = payload(odd[None], pieces[2 * k], taken, *sent, int(starts[k]))
+            load = payload(odd[None], pieces[2 * k], taken[k], *sent, 52 if k else 60)
             one_away.append(lax.ppermute(load, "chan", swap))
             parts.append((1, int(starts[k]), chunks[k], 2))
             sources += sent

time: 108 us -> 103 us (0.954)
  waiting for transfers between devices: 34.2 us -> 18.1 us
  starting transfers between devices: 16.2 us -> 21.6 us
  Pallas kernels: 55.6 us -> 60.1 us
    ppermute x6, waiting for transfers between devices: 29.2 us -> 18.1 us  [local(): lax.ppermute(x, axes, back(2, i % 2))]
    ppermute x3, waiting for transfers between devices: 4.94 us -> 0.01 us  [local(): one_away.append(lax.ppermute(load, 'chan', swap))]
    ppermute x6, starting transfers between devices: 11.8 us -> 16.1 us  [local(): lax.ppermute(x, axes, back(2, i % 2))]
    pallas_call x3, Pallas kernels: 0.88 us -> 3.83 us  [payload(): pl.pallas_call(payload_kernel, out_shape=jax.ShapeDtypeStruct(shape, bf16...]
    pallas_call x4, Pallas kernels: 33.4 us -> 35.8 us  [cross_part(): pl.pallas_call(functools.partial(cross_kernel, tuple(parts), row_count, p...]
    unnamed x8 -> x20, local copies, waits for them, and re-layouts: 1.92 us -> 2.73 us
  transfers between devices with their start and end apart: 11 -> 13, of which waited for: 4 -> 6; matrix products, arithmetic and copies ran while one was open for 0% -> 0% of each run, Pallas kernels for 35% -> 41%
where the time goes in v5:
time: 103 us
  Pallas kernels  60.1 us (58%)
  starting transfers between devices  21.6 us (21%)
  waiting for transfers between devices  18.1 us (18%)
  local copies, waits for them, and re-layouts  2.73 us (3%)
    pallas_call x4, Pallas kernels, cross_part(): pl.pallas_call(functools.partial(cross_kernel, tuple(parts), row_count, p...  35.8 us
    ppermute x6, waiting for transfers between devices, local(): lax.ppermute(x, axes, back(2, i % 2))  18.1 us
    ppermute x6, starting transfers between devices, local(): lax.ppermute(x, axes, back(2, i % 2))  16.1 us
    pallas_call x1, Pallas kernels, spectra(): pl.pallas_call(functools.partial(spectra_kernel, chunks, half), out_shape...  10.1 us
    pallas_call x1, Pallas kernels, first_spectra(): pl.pallas_call(functools.partial(first_kernel, rows, half, tuple(bounds))...  7.92 us
    ppermute x3, starting transfers between devices, local(): one_away.append(lax.ppermute(load, 'chan', swap))  4.7 us
    pallas_call x3, Pallas kernels, payload(): pl.pallas_call(payload_kernel, out_shape=jax.ShapeDtypeStruct(shape, bf16...  3.83 us
    unnamed x20, local copies, waits for them, and re-layouts  2.73 us
  transfers between devices with their start and end apart: 13, of which 6 were waited for; matrix products, arithmetic and copies ran while one was open for 0% of the time, Pallas kernels for 41%

profile of v5, /device:TPU:0, one launch (start us, length us, event | category | flops | bytes accessed | tf_op | source)
XLA Modules:
  0.0 102.9 jit_solution(2132949661702596970)
XLA Ops:
  0.0 10.1 %spectra.1 = (bf16[18,64,128]{2,1,0:T(8,128)(2,1)}, bf16[18,64,128]{2,1,0:T(8,128)(2,1)}, bf16[16,64,128]{2,1,0:T(8,128)(2,1)}, bf16[16,64,128]{2,1,0:T(8,128)(2,1)}, bf16[64,128,128]{2,1,0:T(8,128)(2,1)}) custom-call(s32[1]{0:T(128)} %bitcast.me_ref, f32[104,8192]{1,0:T(8,128)} %signal_hbm.3, s32[8,104]{1,0:T(8,128)} %bitcast.3, ...), custom_call_target="tpu_custom_call" | custom-call | flops 2147483648 | bytes 12582912 | tf_op jit(solution)/shard_map/spectra/pallas_call | solution.py:247
  10.1 0.6 collective-permute-start
  10.7 7.9 %first.1 = (bf16[18,64,128]{2,1,0:T(8,128)(2,1)}, bf16[18,64,128]{2,1,0:T(8,128)(2,1)}) custom-call(s32[1]{0:T(128)} %bitcast.me_ref, f32[104,8192]{1,0:T(8,128)} %signal_hbm.3, s32[8,104]{1,0:T(8,128)} %bitcast.4, bf16[1024,1024]{1,0:T(8,128)(2,1)} %constant.24.table_hbm, f32[1,1024]{1,0:T(1,128)} %constant.20.clone.taper_ref), custom_call_target="tpu_custom_call" | custom-call | flops 1073741824 | bytes 6291456 | tf_op jit(solution)/shard_map/first/pallas_call | solution.py:157
  18.6 4.7 %collective-permute-start.10 = (bf16[18,64,128]{2,1,0:T(8,128)(2,1)}, bf16[18,64,128]{2,1,0:T(8,128)(2,1)S(1)}, u32[]{:S(2)}, u32[]{:S(2)}) collective-permute-start(bf16[18,64,128]{2,1,0:T(8,128)(2,1)} %get-tuple-element.17.keep), channel_id=1, source_target_pairs={{0,12},{1,13},{2,14},{3,15},{4,0},{5,1},{6,2},{7,3},{8,4},{9,5},{1... | collective-permute-start | bytes 884744 | tf_op jit(solution)/shard_map/ppermute | solution.py:518
  23.3 0.3 collective-permute-start.11
  23.5 0.3 collective-permute-start.9
  23.8 0.4 collective-permute-start.2
  24.3 6.7 %collective-permute-done.10.near_side.refs_2_ = bf16[18,64,128]{2,1,0:T(8,128)(2,1)S(1)} collective-permute-done((bf16[18,64,128]{2,1,0:T(8,128)(2,1)}, bf16[18,64,128]{2,1,0:T(8,128)(2,1)S(1)}, u32[]{:S(2)}, u32[]{:S(2)}) %collective-permute-start.10) | collective-permute-done | bytes 294944 | tf_op jit(solution)/shard_map/ppermute | solution.py:518
  31.0 2.9 %collective-permute-start.3 = (bf16[16,64,128]{2,1,0:T(8,128)(2,1)}, bf16[16,64,128]{2,1,0:T(8,128)(2,1)S(1)}, u32[]{:S(2)}, u32[]{:S(2)}) collective-permute-start(bf16[16,64,128]{2,1,0:T(8,128)(2,1)} %get-tuple-element.14), channel_id=1, source_target_pairs={{0,13},{1,12},{2,15},{3,14},{4,1},{5,0},{6,3},{7,2},{8,5},{9,4},{1... | collective-permute-start | bytes 786440 | tf_op jit(solution)/shard_map/ppermute | solution.py:518
  33.9 3.4 %collective-permute-done.11.far_side.refs_3_ = bf16[18,64,128]{2,1,0:T(8,128)(2,1)S(1)} collective-permute-done((bf16[18,64,128]{2,1,0:T(8,128)(2,1)}, bf16[18,64,128]{2,1,0:T(8,128)(2,1)S(1)}, u32[]{:S(2)}, u32[]{:S(2)}) %collective-permute-start.11) | collective-permute-done | bytes 294944 | tf_op jit(solution)/shard_map/ppermute | solution.py:518
  37.3 0.0 collective-permute-start.1
  37.3 0.0 collective-permute-done.9.taken
  37.3 0.0 copy-done.1
  37.3 0.7 copy-done.3
  38.0 0.1 copy-done.9
  38.1 1.8 %payload.5 = bf16[2,18,64,128]{3,2,1,0:T(8,128)(2,1)} custom-call(s32[1]{0:T(128)} %bitcast.2.odd_ref, bf16[18,64,128]{2,1,0:T(8,128)(2,1)} %get-tuple-element.17.keep, bf16[18,64,128]{2,1,0:T(8,128)(2,1)} %copy-done.9, bf16[18,64,128]{2,1,0:T(8,128)(2,1)} %copy-done.1, bf16[18,64,128]{2,1,0:T(8,128)(2,1)} %copy-done.3), custom_call_target="tpu_custom_call" | custom-call | bytes 2097152 | tf_op jit(solution)/shard_map/payload/pallas_call | solution.py:339
  40.0 0.0 copy-start
  40.0 0.0 copy-start.2
  40.0 0.0 copy-start.4
  40.0 1.6 %collective-permute-start.12 = (bf16[2,18,64,128]{3,2,1,0:T(8,128)(2,1)}, bf16[2,18,64,128]{3,2,1,0:T(8,128)(2,1)}, u32[]{:S(2)}, u32[]{:S(2)}) collective-permute-start(bf16[2,18,64,128]{3,2,1,0:T(8,128)(2,1)} %payload.5), channel_id=1, source_target_pairs={{0,2},{2,0},{4,6},{6,4},{8,10},{10,8},{12,14},{14,12},{1,3},{3,1},... | collective-permute-start | bytes 1769480 | tf_op jit(solution)/shard_map/ppermute | solution.py:534
  41.6 1.4 %collective-permute-done.2.near_side.refs_2_ = bf16[16,64,128]{2,1,0:T(8,128)(2,1)S(1)} collective-permute-done((bf16[16,64,128]{2,1,0:T(8,128)(2,1)}, bf16[16,64,128]{2,1,0:T(8,128)(2,1)S(1)}, u32[]{:S(2)}, u32[]{:S(2)}) %collective-permute-start.2) | collective-permute-done | bytes 262176 | tf_op jit(solution)/shard_map/ppermute | solution.py:518
  42.9 4.2 %collective-permute-start.6 = (bf16[18,64,128]{2,1,0:T(8,128)(2,1)}, bf16[18,64,128]{2,1,0:T(8,128)(2,1)S(1)}, u32[]{:S(2)}, u32[]{:S(2)}) collective-permute-start(bf16[18,64,128]{2,1,0:T(8,128)(2,1)} %get-tuple-element.15.keep), channel_id=1, source_target_pairs={{0,12},{1,13},{2,14},{3,15},{4,0},{5,1},{6,2},{7,3},{8,4},{9,5},{1... | collective-permute-start | bytes 884744 | tf_op jit(solution)/shard_map/ppermute | solution.py:518
  47.1 1.4 %collective-permute-done.3.far_side.refs_3_ = bf16[16,64,128]{2,1,0:T(8,128)(2,1)S(1)} collective-permute-done((bf16[16,64,128]{2,1,0:T(8,128)(2,1)}, bf16[16,64,128]{2,1,0:T(8,128)(2,1)S(1)}, u32[]{:S(2)}, u32[]{:S(2)}) %collective-permute-start.3) | collective-permute-done | bytes 262176 | tf_op jit(solution)/shard_map/ppermute | solution.py:518
  48.5 3.6 %collective-permute-start.7 = (bf16[18,64,128]{2,1,0:T(8,128)(2,1)}, bf16[18,64,128]{2,1,0:T(8,128)(2,1)S(1)}, u32[]{:S(2)}, u32[]{:S(2)}) collective-permute-start(bf16[18,64,128]{2,1,0:T(8,128)(2,1)} %get-tuple-element.16), channel_id=1, source_target_pairs={{0,13},{1,12},{2,15},{3,14},{4,1},{5,0},{6,3},{7,2},{8,5},{9,4},{1... | collective-permute-start | bytes 884744 | tf_op jit(solution)/shard_map/ppermute | solution.py:518
  52.1 0.0 collective-permute-done.1.taken
  52.1 0.0 collective-permute-start.5
  52.2 0.9 copy-done.8
  53.1 0.9 payload.3
  54.0 0.9 collective-permute-done.6.near_side.refs_2_
  54.9 1.5 %collective-permute-start.4 = (bf16[2,16,64,128]{3,2,1,0:T(8,128)(2,1)}, bf16[2,16,64,128]{3,2,1,0:T(8,128)(2,1)}, u32[]{:S(2)}, u32[]{:S(2)}) collective-permute-start(bf16[2,16,64,128]{3,2,1,0:T(8,128)(2,1)} %payload.3), channel_id=1, source_target_pairs={{0,2},{2,0},{4,6},{6,4},{8,10},{10,8},{12,14},{14,12},{1,3},{3,1},... | collective-permute-start | bytes 1572872 | tf_op jit(solution)/shard_map/ppermute | solution.py:534
  56.4 4.3 %collective-permute-done.7.far_side.refs_3_ = bf16[18,64,128]{2,1,0:T(8,128)(2,1)S(1)} collective-permute-done((bf16[18,64,128]{2,1,0:T(8,128)(2,1)}, bf16[18,64,128]{2,1,0:T(8,128)(2,1)S(1)}, u32[]{:S(2)}, u32[]{:S(2)}) %collective-permute-start.7) | collective-permute-done | bytes 294944 | tf_op jit(solution)/shard_map/ppermute | solution.py:518
  60.7 0.0 collective-permute-done.5.taken
  60.7 1.0 copy-done.7
  61.7 1.1 %payload.4 = bf16[2,18,64,128]{3,2,1,0:T(8,128)(2,1)} custom-call(s32[1]{0:T(128)} %bitcast.2.odd_ref, bf16[18,64,128]{2,1,0:T(8,128)(2,1)S(1)} %copy-done.7, bf16[18,64,128]{2,1,0:T(8,128)(2,1)S(1)} %collective-permute-done.5.taken, bf16[18,64,128]{2,1,0:T(8,128)(2,1)S(1)} %collective-permute-done.6.near_side.refs_2_, ...), custom_call_target="tpu_custom_call" | custom-call | bytes 2097152 | tf_op jit(solution)/shard_map/payload/pallas_call | solution.py:339
  62.8 1.6 %collective-permute-start.8 = (bf16[2,18,64,128]{3,2,1,0:T(8,128)(2,1)}, bf16[2,18,64,128]{3,2,1,0:T(8,128)(2,1)}, u32[]{:S(2)}, u32[]{:S(2)}) collective-permute-start(bf16[2,18,64,128]{3,2,1,0:T(8,128)(2,1)} %payload.4), channel_id=1, source_target_pairs={{0,2},{2,0},{4,6},{6,4},{8,10},{10,8},{12,14},{14,12},{1,3},{3,1},... | collective-permute-start | bytes 1769480 | tf_op jit(solution)/shard_map/ppermute | solution.py:534
  64.4 0.0 copy-done.5
  64.4 0.0 collective-permute-done.far_hbm
  64.4 2.4 %join.1.refs_0_ = bf16[64,256,256]{2,1,0:T(8,128)(2,1)S(1)} custom-call(bf16[64,128,128]{2,1,0:T(8,128)(2,1)} %get-tuple-element.12.near_hbm, bf16[64,128,128]{2,1,0:T(8,128)(2,1)} %collective-permute-done.far_hbm), custom_call_target="tpu_custom_call" | custom-call | bytes 13631488 | tf_op jit(solution)/shard_map/join/pallas_call | solution.py:304
  66.8 0.0 copy-done
  66.9 0.0 copy-done.2
  66.9 0.0 copy-done.4
  66.9 6.9 %cross.4.refs_5_ = bf16[2,52,104,512]{3,2,1,0:T(8,128)(2,1)} custom-call(bf16[64,256,256]{2,1,0:T(8,128)(2,1)S(1)} %join.1.refs_0_, bf16[2,256,512]{2,1,0:T(8,128)(2,1)S(1)} %copy-done, bf16[18,64,128]{2,1,0:T(8,128)(2,1)S(1)} %copy-done.2, bf16[18,64,128]{2,1,0:T(8,128)(2,1)S(1)} %copy-done.4), custom_call_target="tpu_custom_call" | custom-call | flops 2700000000 | bytes 12582912 | tf_op jit(solution)/shard_map/cross/pallas_call | solution.py:463
  73.8 0.0 collective-permute-done.12.refs_4_
  73.8 11.0 %cross.5.refs_5_ = bf16[2,52,104,512]{3,2,1,0:T(8,128)(2,1)} custom-call(bf16[64,256,256]{2,1,0:T(8,128)(2,1)S(1)} %join.1.refs_0_, bf16[2,256,512]{2,1,0:T(8,128)(2,1)S(1)} %copy-done, bf16[18,64,128]{2,1,0:T(8,128)(2,1)S(1)} %collective-permute-done.6.near_side.refs_2_, ...), custom_call_target="tpu_custom_call", output_to_operand_aliasing={{}: (5, {})} | custom-call | flops 5400000000 | bytes 12582912 | tf_op jit(solution)/shard_map/cross/pallas_call | solution.py:463
  84.8 0.0 collective-permute-done.8.refs_4_
  84.8 10.5 %cross.6.refs_3_ = bf16[2,52,104,512]{3,2,1,0:T(8,128)(2,1)} custom-call(bf16[64,256,256]{2,1,0:T(8,128)(2,1)S(1)} %join.1.refs_0_, bf16[2,256,512]{2,1,0:T(8,128)(2,1)S(1)} %copy-done, bf16[16,64,128]{2,1,0:T(8,128)(2,1)S(1)} %collective-permute-done.2.near_side.refs_2_, bf16[16,64,128]{2,1,0:T(8,128)(2,1)S(1)} %copy-done.6, ...), custom_call_target="tpu_custom_call", output_to_operand_aliasing={{}: (5, {})} | custom-call | flops 5100000256 | bytes 12582912 | tf_op jit(solution)/shard_map/cross/pallas_call | solution.py:463
  95.3 0.0 collective-permute-done.4.refs_2_
  95.3 7.4 %cross.7 = bf16[2,52,104,512]{3,2,1,0:T(8,128)(2,1)} custom-call(bf16[64,256,256]{2,1,0:T(8,128)(2,1)S(1)} %join.1.refs_0_, bf16[2,256,512]{2,1,0:T(8,128)(2,1)S(1)} %copy-done, bf16[2,16,64,128]{3,2,1,0:T(8,128)(2,1)} %collective-permute-done.4.refs_2_, bf16[2,52,104,512]{3,2,1,0:T(8,128)(2,1)} %cross.6.refs_3_), custom_call_target="tpu_custom_call", output_to_operand_aliasing={{}: (3, {})} | custom-call | flops 2400000000 | bytes 12582912 | tf_op jit(solution)/shard_map/cross/pallas_call | solution.py:463
  (8 shorter events, 0.0 us)
Async XLA Ops:
  10.1 54.3 %collective-permute-start = (bf16[64,128,128]{2,1,0:T(8,128)(2,1)}, bf16[64,128,128]{2,1,0:T(8,128)(2,1)}, u32[]{:S(2)}, u32[]{:S(2)}) collective-permute-start(bf16[64,128,128]{2,1,0:T(8,128)(2,1)} %get-tuple-element.12.near_hbm), channel_id=1, source_target_pairs={{0,1},{1,0},{2,3},{3,2},{4,5},{5,4},{6,7},{7,6},{8,9},{9,8},{10,11... | collective-permute-start | bytes 6291464 | tf_op jit(solution)/shard_map/ppermute | solution.py:521
  18.6 12.4 %collective-permute-start.10 = (bf16[18,64,128]{2,1,0:T(8,128)(2,1)}, bf16[18,64,128]{2,1,0:T(8,128)(2,1)S(1)}, u32[]{:S(2)}, u32[]{:S(2)}) collective-permute-start(bf16[18,64,128]{2,1,0:T(8,128)(2,1)} %get-tuple-element.17.keep), channel_id=1, source_target_pairs={{0,12},{1,13},{2,14},{3,15},{4,0},{5,1},{6,2},{7,3},{8,4},{9,5},{1... | collective-permute-start | bytes 884744 | tf_op jit(solution)/shard_map/ppermute | solution.py:518
  23.3 14.0 %collective-permute-start.11 = (bf16[18,64,128]{2,1,0:T(8,128)(2,1)}, bf16[18,64,128]{2,1,0:T(8,128)(2,1)S(1)}, u32[]{:S(2)}, u32[]{:S(2)}) collective-permute-start(bf16[18,64,128]{2,1,0:T(8,128)(2,1)} %get-tuple-element.18), channel_id=1, source_target_pairs={{0,13},{1,12},{2,15},{3,14},{4,1},{5,0},{6,3},{7,2},{8,5},{9,4},{1... | collective-permute-start | bytes 884744 | tf_op jit(solution)/shard_map/ppermute | solution.py:518
  23.5 13.8 %collective-permute-start.9 = (bf16[18,64,128]{2,1,0:T(8,128)(2,1)}, bf16[18,64,128]{2,1,0:T(8,128)(2,1)S(1)}, u32[]{:S(2)}, u32[]{:S(2)}) collective-permute-start(bf16[18,64,128]{2,1,0:T(8,128)(2,1)} %get-tuple-element.18), channel_id=1, source_target_pairs={{0,1},{1,0},{2,3},{3,2},{4,5},{5,4},{6,7},{7,6},{8,9},{9,8},{10,11... | collective-permute-start | bytes 884744 | tf_op jit(solution)/shard_map/ppermute | solution.py:520
  23.8 19.1 %collective-permute-start.2 = (bf16[16,64,128]{2,1,0:T(8,128)(2,1)}, bf16[16,64,128]{2,1,0:T(8,128)(2,1)S(1)}, u32[]{:S(2)}, u32[]{:S(2)}) collective-permute-start(bf16[16,64,128]{2,1,0:T(8,128)(2,1)} %get-tuple-element.13.keep), channel_id=1, source_target_pairs={{0,12},{1,13},{2,14},{3,15},{4,0},{5,1},{6,2},{7,3},{8,4},{9,5},{1... | collective-permute-start | bytes 786440 | tf_op jit(solution)/shard_map/ppermute | solution.py:518
  31.0 6.3 %copy-start.1 = (bf16[18,64,128]{2,1,0:T(8,128)(2,1)}, bf16[18,64,128]{2,1,0:T(8,128)(2,1)S(1)}, u32[]{:S(2)}) copy-start(bf16[18,64,128]{2,1,0:T(8,128)(2,1)S(1)} %collective-permute-done.10.near_side.refs_2_) | copy-start | bytes 884740
  31.0 17.6 %collective-permute-start.3 = (bf16[16,64,128]{2,1,0:T(8,128)(2,1)}, bf16[16,64,128]{2,1,0:T(8,128)(2,1)S(1)}, u32[]{:S(2)}, u32[]{:S(2)}) collective-permute-start(bf16[16,64,128]{2,1,0:T(8,128)(2,1)} %get-tuple-element.14), channel_id=1, source_target_pairs={{0,13},{1,12},{2,15},{3,14},{4,1},{5,0},{6,3},{7,2},{8,5},{9,4},{1... | collective-permute-start | bytes 786440 | tf_op jit(solution)/shard_map/ppermute | solution.py:518
  37.3 0.7 copy-start.3
  37.3 14.8 %collective-permute-start.1 = (bf16[16,64,128]{2,1,0:T(8,128)(2,1)}, bf16[16,64,128]{2,1,0:T(8,128)(2,1)S(1)}, u32[]{:S(2)}, u32[]{:S(2)}) collective-permute-start(bf16[16,64,128]{2,1,0:T(8,128)(2,1)} %get-tuple-element.14), channel_id=1, source_target_pairs={{0,1},{1,0},{2,3},{3,2},{4,5},{5,4},{6,7},{7,6},{8,9},{9,8},{10,11... | collective-permute-start | bytes 786440 | tf_op jit(solution)/shard_map/ppermute | solution.py:520
  37.3 0.8 copy-start.9
  40.0 26.9 %copy-start = (bf16[2,256,512]{2,1,0:T(8,128)(2,1)S(1)}, bf16[2,256,512]{2,1,0:T(8,128)(2,1)}, u32[]{:S(2)}) copy-start(bf16[2,256,512]{2,1,0:T(8,128)(2,1)} %constant.25.refs_1_) | copy-start | bytes 1572868
  40.0 26.9 %copy-start.2 = (bf16[18,64,128]{2,1,0:T(8,128)(2,1)S(1)}, bf16[18,64,128]{2,1,0:T(8,128)(2,1)}, u32[]{:S(2)}) copy-start(bf16[18,64,128]{2,1,0:T(8,128)(2,1)} %copy-done.1) | copy-start | bytes 884740
  40.0 26.9 %copy-start.4 = (bf16[18,64,128]{2,1,0:T(8,128)(2,1)S(1)}, bf16[18,64,128]{2,1,0:T(8,128)(2,1)}, u32[]{:S(2)}) copy-start(bf16[18,64,128]{2,1,0:T(8,128)(2,1)} %copy-done.3) | copy-start | bytes 884740
  40.0 33.9 %collective-permute-start.12 = (bf16[2,18,64,128]{3,2,1,0:T(8,128)(2,1)}, bf16[2,18,64,128]{3,2,1,0:T(8,128)(2,1)}, u32[]{:S(2)}, u32[]{:S(2)}) collective-permute-start(bf16[2,18,64,128]{3,2,1,0:T(8,128)(2,1)} %payload.5), channel_id=1, source_target_pairs={{0,2},{2,0},{4,6},{6,4},{8,10},{10,8},{12,14},{14,12},{1,3},{3,1},... | collective-permute-start | bytes 1769480 | tf_op jit(solution)/shard_map/ppermute | solution.py:534
  42.9 11.9 %collective-permute-start.6 = (bf16[18,64,128]{2,1,0:T(8,128)(2,1)}, bf16[18,64,128]{2,1,0:T(8,128)(2,1)S(1)}, u32[]{:S(2)}, u32[]{:S(2)}) collective-permute-start(bf16[18,64,128]{2,1,0:T(8,128)(2,1)} %get-tuple-element.15.keep), channel_id=1, source_target_pairs={{0,12},{1,13},{2,14},{3,15},{4,0},{5,1},{6,2},{7,3},{8,4},{9,5},{1... | collective-permute-start | bytes 884744 | tf_op jit(solution)/shard_map/ppermute | solution.py:518
  48.5 15.9 %copy-start.5 = (bf16[16,64,128]{2,1,0:T(8,128)(2,1)}, bf16[16,64,128]{2,1,0:T(8,128)(2,1)S(1)}, u32[]{:S(2)}) copy-start(bf16[16,64,128]{2,1,0:T(8,128)(2,1)S(1)} %collective-permute-done.3.far_side.refs_3_) | copy-start | bytes 786436
  48.5 12.2 %collective-permute-start.7 = (bf16[18,64,128]{2,1,0:T(8,128)(2,1)}, bf16[18,64,128]{2,1,0:T(8,128)(2,1)S(1)}, u32[]{:S(2)}, u32[]{:S(2)}) collective-permute-start(bf16[18,64,128]{2,1,0:T(8,128)(2,1)} %get-tuple-element.16), channel_id=1, source_target_pairs={{0,13},{1,12},{2,15},{3,14},{4,1},{5,0},{6,3},{7,2},{8,5},{9,4},{1... | collective-permute-start | bytes 884744 | tf_op jit(solution)/shard_map/ppermute | solution.py:518
  52.1 8.6 %collective-permute-start.5 = (bf16[18,64,128]{2,1,0:T(8,128)(2,1)}, bf16[18,64,128]{2,1,0:T(8,128)(2,1)S(1)}, u32[]{:S(2)}, u32[]{:S(2)}) collective-permute-start(bf16[18,64,128]{2,1,0:T(8,128)(2,1)} %get-tuple-element.16), channel_id=1, source_target_pairs={{0,1},{1,0},{2,3},{3,2},{4,5},{5,4},{6,7},{7,6},{8,9},{9,8},{10,11... | collective-permute-start | bytes 884744 | tf_op jit(solution)/shard_map/ppermute | solution.py:520
  52.2 1.0 copy-start.8
  54.9 40.5 %collective-permute-start.4 = (bf16[2,16,64,128]{3,2,1,0:T(8,128)(2,1)}, bf16[2,16,64,128]{3,2,1,0:T(8,128)(2,1)}, u32[]{:S(2)}, u32[]{:S(2)}) collective-permute-start(bf16[2,16,64,128]{3,2,1,0:T(8,128)(2,1)} %payload.3), channel_id=1, source_target_pairs={{0,2},{2,0},{4,6},{6,4},{8,10},{10,8},{12,14},{14,12},{1,3},{3,1},... | collective-permute-start | bytes 1572872 | tf_op jit(solution)/shard_map/ppermute | solution.py:534
  60.7 1.0 copy-start.7
  62.8 22.0 %collective-permute-start.8 = (bf16[2,18,64,128]{3,2,1,0:T(8,128)(2,1)}, bf16[2,18,64,128]{3,2,1,0:T(8,128)(2,1)}, u32[]{:S(2)}, u32[]{:S(2)}) collective-permute-start(bf16[2,18,64,128]{3,2,1,0:T(8,128)(2,1)} %payload.4), channel_id=1, source_target_pairs={{0,2},{2,0},{4,6},{6,4},{8,10},{10,8},{12,14},{14,12},{1,3},{3,1},... | collective-permute-start | bytes 1769480 | tf_op jit(solution)/shard_map/ppermute | solution.py:534
  73.8 11.0 %copy-start.6 = (bf16[16,64,128]{2,1,0:T(8,128)(2,1)S(1)}, bf16[16,64,128]{2,1,0:T(8,128)(2,1)}, u32[]{:S(2)}) copy-start(bf16[16,64,128]{2,1,0:T(8,128)(2,1)} %copy-done.5) | copy-start | bytes 786436

commit v6 on v5

--- a/solution.py
+++ b/solution.py
@@ -20,7 +20,7 @@
 GROUP = 8
 OCTETS = BINS // GROUP
 STEPS = OCTETS // 4
-ROWS_PER_CHUNK = (18, 18, 16)
+ROWS_PER_CHUNK = (18, 20, 14)
 
 f32 = jnp.float32
 bf16 = jnp.bfloat16
@@ -120,8 +120,9 @@
     for w in range(spans):
         x = signal[:, w * WINDOW : (w + 1) * WINDOW]
         tap[pl.ds(w * width, held), :] = taper_rows(x, taper)
+    for copy in tables:
+        copy.wait()
     for g in range(4):
-        tables[g].wait()
         result = transform(table, tap, g)
         for o in range(16):
             position = g * 16 + o
@@ -200,8 +201,9 @@
         tap[pl.ds(w * LANES, row_count), :] = taper_rows(x, taper)
     order = window_order(spans)
     leaving = []
+    for copy in tables:
+        copy.wait()
     for g in range(4):
-        tables[g].wait()
         result = transform(table, tap, g)
         for o in range(16):
             position = g * 16 + o
@@ -333,7 +335,7 @@
         leave[i].wait()
 
 
-def payload(odd, keep, taken, near_side, far_side, grant):
+def payload(odd, keep, taken, near_side, far_side):
     hbm = pl.BlockSpec(memory_space=pltpu.MemorySpace.HBM)
     shape = (2,) + keep.shape
     return pl.pallas_call(
@@ -346,7 +348,7 @@
             pltpu.SemaphoreType.DMA((2,)),
             pltpu.SemaphoreType.DMA((2,)),
         ],
-        compiler_params=pltpu.CompilerParams(vmem_limit_bytes=grant << 20),
+        compiler_params=pltpu.CompilerParams(vmem_limit_bytes=48 << 20),
         cost_estimate=pl.CostEstimate(flops=0, bytes_accessed=2 << 20, transcendentals=0),
         name="payload",
     )(odd, keep, taken, near_side, far_side)
@@ -530,7 +532,7 @@
         parts, sources = [], []
         if k < len(chunks):
             sent = two_away[2 * k : 2 * k + 2]
-            load = payload(odd[None], pieces[2 * k], taken[k], *sent, 52 if k else 60)
+            load = payload(odd[None], pieces[2 * k], taken[k], *sent)
             one_away.append(lax.ppermute(load, "chan", swap))
             parts.append((1, int(starts[k]), chunks[k], 2))
             sources += sent

time: 103 us -> 102 us (level)
  Pallas kernels: 60.1 us -> 58.5 us
    pallas_call x1, Pallas kernels: 7.92 us -> 6.54 us  [first_spectra(): pl.pallas_call(functools.partial(first_kernel, rows, half, tuple(bounds))...]
    unnamed x20 -> x12, local copies, waits for them, and re-layouts: 2.73 us -> 2.89 us
where the time goes in v6:
time: 102 us
  Pallas kernels  58.5 us (57%)
  starting transfers between devices  21.7 us (21%)
  waiting for transfers between devices  18.3 us (18%)
  local copies, waits for them, and re-layouts  2.89 us (3%)
    pallas_call x4, Pallas kernels, cross_part(): pl.pallas_call(functools.partial(cross_kernel, tuple(parts), row_count, p...  36.5 us
    ppermute x6, waiting for transfers between devices, local(): lax.ppermute(x, axes, back(2, i % 2))  18.3 us
    ppermute x6, starting transfers between devices, local(): lax.ppermute(x, axes, back(2, i % 2))  16.1 us
    pallas_call x1, Pallas kernels, spectra(): pl.pallas_call(functools.partial(spectra_kernel, chunks, half), out_shape...  9.41 us
    pallas_call x1, Pallas kernels, first_spectra(): pl.pallas_call(functools.partial(first_kernel, rows, half, tuple(bounds))...  6.54 us
    ppermute x3, starting transfers between devices, local(): one_away.append(lax.ppermute(load, 'chan', swap))  4.72 us
    pallas_call x3, Pallas kernels, payload(): pl.pallas_call(payload_kernel, out_shape=jax.ShapeDtypeStruct(shape, bf16...  3.59 us
    unnamed x12, local copies, waits for them, and re-layouts  2.89 us
  transfers between devices with their start and end apart: 13, of which 6 were waited for; matrix products, arithmetic and copies ran while one was open for 0% of the time, Pallas kernels for 41%

profile of v6, /device:TPU:0, one launch (start us, length us, event | category | flops | bytes accessed | tf_op | source)
XLA Modules:
  0.0 101.6 jit_solution(17880315663215951211)
XLA Ops:
  0.0 9.4 %spectra.1 = (bf16[20,64,128]{2,1,0:T(8,128)(2,1)}, bf16[20,64,128]{2,1,0:T(8,128)(2,1)}, bf16[14,64,128]{2,1,0:T(8,128)(2,1)}, bf16[14,64,128]{2,1,0:T(8,128)(2,1)}, bf16[64,128,128]{2,1,0:T(8,128)(2,1)}) custom-call(s32[1]{0:T(128)} %bitcast.me_ref, f32[104,8192]{1,0:T(8,128)} %signal_hbm.3, s32[8,104]{1,0:T(8,128)} %bitcast.3, ...), custom_call_target="tpu_custom_call" | custom-call | flops 2147483648 | bytes 12582912 | tf_op jit(solution)/shard_map/spectra/pallas_call | solution.py:249
  9.4 0.6 collective-permute-start
  10.0 6.5 %first.1 = (bf16[18,64,128]{2,1,0:T(8,128)(2,1)}, bf16[18,64,128]{2,1,0:T(8,128)(2,1)}) custom-call(s32[1]{0:T(128)} %bitcast.me_ref, f32[104,8192]{1,0:T(8,128)} %signal_hbm.3, s32[8,104]{1,0:T(8,128)} %bitcast.4, bf16[1024,1024]{1,0:T(8,128)(2,1)} %constant.24.table_hbm, f32[1,1024]{1,0:T(1,128)} %constant.20.clone.taper_ref), custom_call_target="tpu_custom_call" | custom-call | flops 1073741824 | bytes 6291456 | tf_op jit(solution)/shard_map/first/pallas_call | solution.py:158
  16.5 4.7 %collective-permute-start.10 = (bf16[18,64,128]{2,1,0:T(8,128)(2,1)}, bf16[18,64,128]{2,1,0:T(8,128)(2,1)S(1)}, u32[]{:S(2)}, u32[]{:S(2)}) collective-permute-start(bf16[18,64,128]{2,1,0:T(8,128)(2,1)} %get-tuple-element.17.keep), channel_id=1, source_target_pairs={{0,12},{1,13},{2,14},{3,15},{4,0},{5,1},{6,2},{7,3},{8,4},{9,5},{1... | collective-permute-start | bytes 884744 | tf_op jit(solution)/shard_map/ppermute | solution.py:520
  21.2 0.3 collective-permute-start.11
  21.4 0.3 collective-permute-start.9
  21.7 0.4 collective-permute-start.2
  22.2 6.7 %collective-permute-done.10.near_side.refs_2_ = bf16[18,64,128]{2,1,0:T(8,128)(2,1)S(1)} collective-permute-done((bf16[18,64,128]{2,1,0:T(8,128)(2,1)}, bf16[18,64,128]{2,1,0:T(8,128)(2,1)S(1)}, u32[]{:S(2)}, u32[]{:S(2)}) %collective-permute-start.10) | collective-permute-done | bytes 294944 | tf_op jit(solution)/shard_map/ppermute | solution.py:520
  28.9 2.9 %collective-permute-start.3 = (bf16[14,64,128]{2,1,0:T(8,128)(2,1)}, bf16[14,64,128]{2,1,0:T(8,128)(2,1)S(1)}, u32[]{:S(2)}, u32[]{:S(2)}) collective-permute-start(bf16[14,64,128]{2,1,0:T(8,128)(2,1)} %get-tuple-element.14), channel_id=1, source_target_pairs={{0,13},{1,12},{2,15},{3,14},{4,1},{5,0},{6,3},{7,2},{8,5},{9,4},{1... | collective-permute-start | bytes 688136 | tf_op jit(solution)/shard_map/ppermute | solution.py:520
  31.8 3.4 %collective-permute-done.11.far_side.refs_3_ = bf16[18,64,128]{2,1,0:T(8,128)(2,1)S(1)} collective-permute-done((bf16[18,64,128]{2,1,0:T(8,128)(2,1)}, bf16[18,64,128]{2,1,0:T(8,128)(2,1)S(1)}, u32[]{:S(2)}, u32[]{:S(2)}) %collective-permute-start.11) | collective-permute-done | bytes 294944 | tf_op jit(solution)/shard_map/ppermute | solution.py:520
  35.2 0.0 collective-permute-start.1
  35.2 0.0 collective-permute-done.9.taken
  35.2 0.0 copy-start.4
  35.2 1.0 copy-done.4
  36.2 1.0 payload.5
  37.1 0.0 copy-start
  37.2 1.6 %collective-permute-start.12 = (bf16[2,18,64,128]{3,2,1,0:T(8,128)(2,1)}, bf16[2,18,64,128]{3,2,1,0:T(8,128)(2,1)}, u32[]{:S(2)}, u32[]{:S(2)}) collective-permute-start(bf16[2,18,64,128]{3,2,1,0:T(8,128)(2,1)} %payload.5), channel_id=1, source_target_pairs={{0,2},{2,0},{4,6},{6,4},{8,10},{10,8},{12,14},{14,12},{1,3},{3,1},... | collective-permute-start | bytes 1769480 | tf_op jit(solution)/shard_map/ppermute | solution.py:536
  38.8 1.4 %collective-permute-done.2.near_side.refs_2_ = bf16[14,64,128]{2,1,0:T(8,128)(2,1)S(1)} collective-permute-done((bf16[14,64,128]{2,1,0:T(8,128)(2,1)}, bf16[14,64,128]{2,1,0:T(8,128)(2,1)S(1)}, u32[]{:S(2)}, u32[]{:S(2)}) %collective-permute-start.2) | collective-permute-done | bytes 229408 | tf_op jit(solution)/shard_map/ppermute | solution.py:520
  40.1 4.2 %collective-permute-start.6 = (bf16[20,64,128]{2,1,0:T(8,128)(2,1)}, bf16[20,64,128]{2,1,0:T(8,128)(2,1)S(1)}, u32[]{:S(2)}, u32[]{:S(2)}) collective-permute-start(bf16[20,64,128]{2,1,0:T(8,128)(2,1)} %get-tuple-element.15.keep), channel_id=1, source_target_pairs={{0,12},{1,13},{2,14},{3,15},{4,0},{5,1},{6,2},{7,3},{8,4},{9,5},{1... | collective-permute-start | bytes 983048 | tf_op jit(solution)/shard_map/ppermute | solution.py:520
  44.3 0.7 collective-permute-done.3.far_side.refs_3_
  45.0 0.0 copy-start.1
  45.0 3.6 %collective-permute-start.7 = (bf16[20,64,128]{2,1,0:T(8,128)(2,1)}, bf16[20,64,128]{2,1,0:T(8,128)(2,1)S(1)}, u32[]{:S(2)}, u32[]{:S(2)}) collective-permute-start(bf16[20,64,128]{2,1,0:T(8,128)(2,1)} %get-tuple-element.16), channel_id=1, source_target_pairs={{0,13},{1,12},{2,15},{3,14},{4,1},{5,0},{6,3},{7,2},{8,5},{9,4},{1... | collective-permute-start | bytes 983048 | tf_op jit(solution)/shard_map/ppermute | solution.py:520
  48.6 0.0 collective-permute-done.1.taken
  48.6 0.0 collective-permute-start.5
  48.6 0.0 copy-start.5
  48.6 0.9 copy-done.5
  49.6 1.4 %payload.3 = bf16[2,14,64,128]{3,2,1,0:T(8,128)(2,1)} custom-call(s32[1]{0:T(128)} %bitcast.2.odd_ref, bf16[14,64,128]{2,1,0:T(8,128)(2,1)S(1)} %copy-done.5, bf16[14,64,128]{2,1,0:T(8,128)(2,1)S(1)} %collective-permute-done.1.taken, bf16[14,64,128]{2,1,0:T(8,128)(2,1)S(1)} %collective-permute-done.2.near_side.refs_2_, ...), custom_call_target="tpu_custom_call" | custom-call | bytes 2097152 | tf_op jit(solution)/shard_map/payload/pallas_call | solution.py:341
  50.9 1.8 %collective-permute-done.6.near_side.refs_2_ = bf16[20,64,128]{2,1,0:T(8,128)(2,1)S(1)} collective-permute-done((bf16[20,64,128]{2,1,0:T(8,128)(2,1)}, bf16[20,64,128]{2,1,0:T(8,128)(2,1)S(1)}, u32[]{:S(2)}, u32[]{:S(2)}) %collective-permute-start.6) | collective-permute-done | bytes 327712 | tf_op jit(solution)/shard_map/ppermute | solution.py:520
  52.7 1.5 %collective-permute-start.4 = (bf16[2,14,64,128]{3,2,1,0:T(8,128)(2,1)}, bf16[2,14,64,128]{3,2,1,0:T(8,128)(2,1)}, u32[]{:S(2)}, u32[]{:S(2)}) collective-permute-start(bf16[2,14,64,128]{3,2,1,0:T(8,128)(2,1)} %payload.3), channel_id=1, source_target_pairs={{0,2},{2,0},{4,6},{6,4},{8,10},{10,8},{12,14},{14,12},{1,3},{3,1},... | collective-permute-start | bytes 1376264 | tf_op jit(solution)/shard_map/ppermute | solution.py:536
  54.2 4.4 %collective-permute-done.7.far_side.refs_3_ = bf16[20,64,128]{2,1,0:T(8,128)(2,1)S(1)} collective-permute-done((bf16[20,64,128]{2,1,0:T(8,128)(2,1)}, bf16[20,64,128]{2,1,0:T(8,128)(2,1)S(1)}, u32[]{:S(2)}, u32[]{:S(2)}) %collective-permute-start.7) | collective-permute-done | bytes 327712 | tf_op jit(solution)/shard_map/ppermute | solution.py:520
  58.6 0.0 collective-permute-done.5.taken
  58.6 0.0 copy-start.3
  58.6 1.0 copy-done.3
  59.6 1.3 %payload.4 = bf16[2,20,64,128]{3,2,1,0:T(8,128)(2,1)} custom-call(s32[1]{0:T(128)} %bitcast.2.odd_ref, bf16[20,64,128]{2,1,0:T(8,128)(2,1)S(1)} %copy-done.3, bf16[20,64,128]{2,1,0:T(8,128)(2,1)S(1)} %collective-permute-done.5.taken, bf16[20,64,128]{2,1,0:T(8,128)(2,1)S(1)} %collective-permute-done.6.near_side.refs_2_, ...), custom_call_target="tpu_custom_call" | custom-call | bytes 2097152 | tf_op jit(solution)/shard_map/payload/pallas_call | solution.py:341
  60.9 1.6 %collective-permute-start.8 = (bf16[2,20,64,128]{3,2,1,0:T(8,128)(2,1)}, bf16[2,20,64,128]{3,2,1,0:T(8,128)(2,1)}, u32[]{:S(2)}, u32[]{:S(2)}) collective-permute-start(bf16[2,20,64,128]{3,2,1,0:T(8,128)(2,1)} %payload.4), channel_id=1, source_target_pairs={{0,2},{2,0},{4,6},{6,4},{8,10},{10,8},{12,14},{14,12},{1,3},{3,1},... | collective-permute-start | bytes 1966088 | tf_op jit(solution)/shard_map/ppermute | solution.py:536
  62.5 0.0 copy-done.1
  62.5 0.0 collective-permute-done.far_hbm
  62.5 2.4 %join.1.refs_0_ = bf16[64,256,256]{2,1,0:T(8,128)(2,1)S(1)} custom-call(bf16[64,128,128]{2,1,0:T(8,128)(2,1)} %get-tuple-element.12.near_hbm, bf16[64,128,128]{2,1,0:T(8,128)(2,1)} %collective-permute-done.far_hbm), custom_call_target="tpu_custom_call" | custom-call | bytes 13631488 | tf_op jit(solution)/shard_map/join/pallas_call | solution.py:306
  64.9 0.0 copy-done
  64.9 6.9 %cross.4.refs_5_ = bf16[2,52,104,512]{3,2,1,0:T(8,128)(2,1)} custom-call(bf16[64,256,256]{2,1,0:T(8,128)(2,1)S(1)} %join.1.refs_0_, bf16[2,256,512]{2,1,0:T(8,128)(2,1)S(1)} %copy-done, bf16[18,64,128]{2,1,0:T(8,128)(2,1)S(1)} %collective-permute-done.10.near_side.refs_2_, bf16[18,64,128]{2,1,0:T(8,128)(2,1)S(1)} %collective-permute-done.11.far_side.refs_3_), custom_call_target="tpu_custom_call" | custom-call | flops 2700000000 | bytes 12582912 | tf_op jit(solution)/shard_map/cross/pallas_call | solution.py:465
  71.8 0.0 copy-start.2
  71.9 0.0 collective-permute-done.12.refs_4_
  71.9 11.3 %cross.5.refs_5_ = bf16[2,52,104,512]{3,2,1,0:T(8,128)(2,1)} custom-call(bf16[64,256,256]{2,1,0:T(8,128)(2,1)S(1)} %join.1.refs_0_, bf16[2,256,512]{2,1,0:T(8,128)(2,1)S(1)} %copy-done, bf16[20,64,128]{2,1,0:T(8,128)(2,1)S(1)} %collective-permute-done.6.near_side.refs_2_, ...), custom_call_target="tpu_custom_call", output_to_operand_aliasing={{}: (5, {})} | custom-call | flops 5699999744 | bytes 12582912 | tf_op jit(solution)/shard_map/cross/pallas_call | solution.py:465
  83.2 0.0 collective-permute-done.8.refs_4_
  83.2 0.0 copy-done.2
  83.2 11.1 %cross.6.refs_3_ = bf16[2,52,104,512]{3,2,1,0:T(8,128)(2,1)} custom-call(bf16[64,256,256]{2,1,0:T(8,128)(2,1)S(1)} %join.1.refs_0_, bf16[2,256,512]{2,1,0:T(8,128)(2,1)S(1)} %copy-done, bf16[14,64,128]{2,1,0:T(8,128)(2,1)S(1)} %collective-permute-done.2.near_side.refs_2_, bf16[14,64,128]{2,1,0:T(8,128)(2,1)S(1)} %copy-done.2, ...), custom_call_target="tpu_custom_call", output_to_operand_aliasing={{}: (5, {})} | custom-call | flops 5100000256 | bytes 12582912 | tf_op jit(solution)/shard_map/cross/pallas_call | solution.py:465
  94.3 0.0 collective-permute-done.4.refs_2_
  94.3 7.2 %cross.7 = bf16[2,52,104,512]{3,2,1,0:T(8,128)(2,1)} custom-call(bf16[64,256,256]{2,1,0:T(8,128)(2,1)S(1)} %join.1.refs_0_, bf16[2,256,512]{2,1,0:T(8,128)(2,1)S(1)} %copy-done, bf16[2,14,64,128]{3,2,1,0:T(8,128)(2,1)} %collective-permute-done.4.refs_2_, bf16[2,52,104,512]{3,2,1,0:T(8,128)(2,1)} %cross.6.refs_3_), custom_call_target="tpu_custom_call", output_to_operand_aliasing={{}: (3, {})} | custom-call | flops 2100000000 | bytes 12582912 | tf_op jit(solution)/shard_map/cross/pallas_call | solution.py:465
Async XLA Ops:
  9.4 53.0 %collective-permute-start = (bf16[64,128,128]{2,1,0:T(8,128)(2,1)}, bf16[64,128,128]{2,1,0:T(8,128)(2,1)}, u32[]{:S(2)}, u32[]{:S(2)}) collective-permute-start(bf16[64,128,128]{2,1,0:T(8,128)(2,1)} %get-tuple-element.12.near_hbm), channel_id=1, source_target_pairs={{0,1},{1,0},{2,3},{3,2},{4,5},{5,4},{6,7},{7,6},{8,9},{9,8},{10,11... | collective-permute-start | bytes 6291464 | tf_op jit(solution)/shard_map/ppermute | solution.py:523
  16.5 12.4 %collective-permute-start.10 = (bf16[18,64,128]{2,1,0:T(8,128)(2,1)}, bf16[18,64,128]{2,1,0:T(8,128)(2,1)S(1)}, u32[]{:S(2)}, u32[]{:S(2)}) collective-permute-start(bf16[18,64,128]{2,1,0:T(8,128)(2,1)} %get-tuple-element.17.keep), channel_id=1, source_target_pairs={{0,12},{1,13},{2,14},{3,15},{4,0},{5,1},{6,2},{7,3},{8,4},{9,5},{1... | collective-permute-start | bytes 884744 | tf_op jit(solution)/shard_map/ppermute | solution.py:520
  21.2 14.0 %collective-permute-start.11 = (bf16[18,64,128]{2,1,0:T(8,128)(2,1)}, bf16[18,64,128]{2,1,0:T(8,128)(2,1)S(1)}, u32[]{:S(2)}, u32[]{:S(2)}) collective-permute-start(bf16[18,64,128]{2,1,0:T(8,128)(2,1)} %get-tuple-element.18), channel_id=1, source_target_pairs={{0,13},{1,12},{2,15},{3,14},{4,1},{5,0},{6,3},{7,2},{8,5},{9,4},{1... | collective-permute-start | bytes 884744 | tf_op jit(solution)/shard_map/ppermute | solution.py:520
  21.4 13.8 %collective-permute-start.9 = (bf16[18,64,128]{2,1,0:T(8,128)(2,1)}, bf16[18,64,128]{2,1,0:T(8,128)(2,1)S(1)}, u32[]{:S(2)}, u32[]{:S(2)}) collective-permute-start(bf16[18,64,128]{2,1,0:T(8,128)(2,1)} %get-tuple-element.18), channel_id=1, source_target_pairs={{0,1},{1,0},{2,3},{3,2},{4,5},{5,4},{6,7},{7,6},{8,9},{9,8},{10,11... | collective-permute-start | bytes 884744 | tf_op jit(solution)/shard_map/ppermute | solution.py:522
  21.7 18.4 %collective-permute-start.2 = (bf16[14,64,128]{2,1,0:T(8,128)(2,1)}, bf16[14,64,128]{2,1,0:T(8,128)(2,1)S(1)}, u32[]{:S(2)}, u32[]{:S(2)}) collective-permute-start(bf16[14,64,128]{2,1,0:T(8,128)(2,1)} %get-tuple-element.13.keep), channel_id=1, source_target_pairs={{0,12},{1,13},{2,14},{3,15},{4,0},{5,1},{6,2},{7,3},{8,4},{9,5},{1... | collective-permute-start | bytes 688136 | tf_op jit(solution)/shard_map/ppermute | solution.py:520
  28.9 16.1 %collective-permute-start.3 = (bf16[14,64,128]{2,1,0:T(8,128)(2,1)}, bf16[14,64,128]{2,1,0:T(8,128)(2,1)S(1)}, u32[]{:S(2)}, u32[]{:S(2)}) collective-permute-start(bf16[14,64,128]{2,1,0:T(8,128)(2,1)} %get-tuple-element.14), channel_id=1, source_target_pairs={{0,13},{1,12},{2,15},{3,14},{4,1},{5,0},{6,3},{7,2},{8,5},{9,4},{1... | collective-permute-start | bytes 688136 | tf_op jit(solution)/shard_map/ppermute | solution.py:520
  35.2 13.4 %collective-permute-start.1 = (bf16[14,64,128]{2,1,0:T(8,128)(2,1)}, bf16[14,64,128]{2,1,0:T(8,128)(2,1)S(1)}, u32[]{:S(2)}, u32[]{:S(2)}) collective-permute-start(bf16[14,64,128]{2,1,0:T(8,128)(2,1)} %get-tuple-element.14), channel_id=1, source_target_pairs={{0,1},{1,0},{2,3},{3,2},{4,5},{5,4},{6,7},{7,6},{8,9},{9,8},{10,11... | collective-permute-start | bytes 688136 | tf_op jit(solution)/shard_map/ppermute | solution.py:522
  35.2 1.0 copy-start.4
  37.1 27.7 %copy-start = (bf16[2,256,512]{2,1,0:T(8,128)(2,1)S(1)}, bf16[2,256,512]{2,1,0:T(8,128)(2,1)}, u32[]{:S(2)}) copy-start(bf16[2,256,512]{2,1,0:T(8,128)(2,1)} %constant.25.refs_1_) | copy-start | bytes 1572868
  37.2 34.7 %collective-permute-start.12 = (bf16[2,18,64,128]{3,2,1,0:T(8,128)(2,1)}, bf16[2,18,64,128]{3,2,1,0:T(8,128)(2,1)}, u32[]{:S(2)}, u32[]{:S(2)}) collective-permute-start(bf16[2,18,64,128]{3,2,1,0:T(8,128)(2,1)} %payload.5), channel_id=1, source_target_pairs={{0,2},{2,0},{4,6},{6,4},{8,10},{10,8},{12,14},{14,12},{1,3},{3,1},... | collective-permute-start | bytes 1769480 | tf_op jit(solution)/shard_map/ppermute | solution.py:536
  40.1 12.6 %collective-permute-start.6 = (bf16[20,64,128]{2,1,0:T(8,128)(2,1)}, bf16[20,64,128]{2,1,0:T(8,128)(2,1)S(1)}, u32[]{:S(2)}, u32[]{:S(2)}) collective-permute-start(bf16[20,64,128]{2,1,0:T(8,128)(2,1)} %get-tuple-element.15.keep), channel_id=1, source_target_pairs={{0,12},{1,13},{2,14},{3,15},{4,0},{5,1},{6,2},{7,3},{8,4},{9,5},{1... | collective-permute-start | bytes 983048 | tf_op jit(solution)/shard_map/ppermute | solution.py:520
  45.0 17.4 %copy-start.1 = (bf16[14,64,128]{2,1,0:T(8,128)(2,1)}, bf16[14,64,128]{2,1,0:T(8,128)(2,1)S(1)}, u32[]{:S(2)}) copy-start(bf16[14,64,128]{2,1,0:T(8,128)(2,1)S(1)} %collective-permute-done.3.far_side.refs_3_) | copy-start | bytes 688132
  45.0 13.6 %collective-permute-start.7 = (bf16[20,64,128]{2,1,0:T(8,128)(2,1)}, bf16[20,64,128]{2,1,0:T(8,128)(2,1)S(1)}, u32[]{:S(2)}, u32[]{:S(2)}) collective-permute-start(bf16[20,64,128]{2,1,0:T(8,128)(2,1)} %get-tuple-element.16), channel_id=1, source_target_pairs={{0,13},{1,12},{2,15},{3,14},{4,1},{5,0},{6,3},{7,2},{8,5},{9,4},{1... | collective-permute-start | bytes 983048 | tf_op jit(solution)/shard_map/ppermute | solution.py:520
  48.6 10.0 %collective-permute-start.5 = (bf16[20,64,128]{2,1,0:T(8,128)(2,1)}, bf16[20,64,128]{2,1,0:T(8,128)(2,1)S(1)}, u32[]{:S(2)}, u32[]{:S(2)}) collective-permute-start(bf16[20,64,128]{2,1,0:T(8,128)(2,1)} %get-tuple-element.16), channel_id=1, source_target_pairs={{0,1},{1,0},{2,3},{3,2},{4,5},{5,4},{6,7},{7,6},{8,9},{9,8},{10,11... | collective-permute-start | bytes 983048 | tf_op jit(solution)/shard_map/ppermute | solution.py:522
  48.6 0.9 copy-start.5
  52.7 41.6 %collective-permute-start.4 = (bf16[2,14,64,128]{3,2,1,0:T(8,128)(2,1)}, bf16[2,14,64,128]{3,2,1,0:T(8,128)(2,1)}, u32[]{:S(2)}, u32[]{:S(2)}) collective-permute-start(bf16[2,14,64,128]{3,2,1,0:T(8,128)(2,1)} %payload.3), channel_id=1, source_target_pairs={{0,2},{2,0},{4,6},{6,4},{8,10},{10,8},{12,14},{14,12},{1,3},{3,1},... | collective-permute-start | bytes 1376264 | tf_op jit(solution)/shard_map/ppermute | solution.py:536
  58.6 1.0 copy-start.3
  60.9 22.3 %collective-permute-start.8 = (bf16[2,20,64,128]{3,2,1,0:T(8,128)(2,1)}, bf16[2,20,64,128]{3,2,1,0:T(8,128)(2,1)}, u32[]{:S(2)}, u32[]{:S(2)}) collective-permute-start(bf16[2,20,64,128]{3,2,1,0:T(8,128)(2,1)} %payload.4), channel_id=1, source_target_pairs={{0,2},{2,0},{4,6},{6,4},{8,10},{10,8},{12,14},{14,12},{1,3},{3,1},... | collective-permute-start | bytes 1966088 | tf_op jit(solution)/shard_map/ppermute | solution.py:536
  71.8 11.4 %copy-start.2 = (bf16[14,64,128]{2,1,0:T(8,128)(2,1)S(1)}, bf16[14,64,128]{2,1,0:T(8,128)(2,1)}, u32[]{:S(2)}) copy-start(bf16[14,64,128]{2,1,0:T(8,128)(2,1)} %copy-done.1) | copy-start | bytes 688132

commit v7 on v6

--- a/solution.py
+++ b/solution.py
@@ -20,7 +20,7 @@
 GROUP = 8
 OCTETS = BINS // GROUP
 STEPS = OCTETS // 4
-ROWS_PER_CHUNK = (18, 20, 14)
+ROWS_PER_CHUNK = (16, 12, 12, 12)
 
 f32 = jnp.float32
 bf16 = jnp.bfloat16
@@ -312,7 +312,7 @@
             pltpu.VMEM((2,) + near.shape, bf16),
             pltpu.SemaphoreType.DMA((2, 8)),
         ],
-        compiler_params=pltpu.CompilerParams(vmem_limit_bytes=54 << 20),
+        compiler_params=pltpu.CompilerParams(vmem_limit_bytes=51 << 20),
         cost_estimate=pl.CostEstimate(flops=0, bytes_accessed=13 << 20, transcendentals=0),
         name="join",
     )(near, far)
@@ -429,7 +429,7 @@
                 ).astype(bf16)
 
     step(0, True)
-    lax.fori_loop(1, STEPS, lambda m, c: (step(m, False), c)[1], 0)
+    lax.fori_loop(1, STEPS, lambda m, c: (step(m, False), c)[1], 0, unroll=5)
 
     lag_copy.wait()
     targets = [(part[0], part[1] + i) for part in parts for i in range(part[2])]

time: 102 us -> 92.1 us (0.903)
  waiting for transfers between devices: 18.3 us -> 10.5 us
  Pallas kernels: 58.5 us -> 53 us
  starting transfers between devices: 21.7 us -> 24.2 us
    ppermute x6 -> x8, waiting for transfers between devices: 18.3 us -> 10.5 us  [local(): lax.ppermute(x, axes, back(2, i % 2))]
    pallas_call x4 -> x5, Pallas kernels: 36.5 us -> 30.9 us  [cross_part(): pl.pallas_call(functools.partial(cross_kernel, tuple(parts), row_count, p...]
    ppermute x6 -> x8, starting transfers between devices: 16.1 us -> 18 us  [local(): lax.ppermute(x, axes, back(2, i % 2))]
    unnamed x12 -> x10, local copies, waits for them, and re-layouts: 2.89 us -> 3.72 us
    ppermute x3 -> x4, starting transfers between devices: 4.72 us -> 5.28 us  [local(): one_away.append(lax.ppermute(load, 'chan', swap))]
    pallas_call x3 -> x4, Pallas kernels: 3.59 us -> 4.07 us  [payload(): pl.pallas_call(payload_kernel, out_shape=jax.ShapeDtypeStruct(shape, bf16...]
  transfers between devices with their start and end apart: 13 -> 17, of which waited for: 6 -> 4; matrix products, arithmetic and copies ran while one was open for 0% -> 0% of each run, Pallas kernels for 41% -> 42%
where the time goes in v7:
time: 92.1 us; the launch traced here: 91.8 us
  Pallas kernels  53 us (58%)
  starting transfers between devices  24.2 us (26%)
  waiting for transfers between devices  10.5 us (11%)
  local copies, waits for them, and re-layouts  3.72 us (4%)
    pallas_call x5, Pallas kernels, cross_part(): pl.pallas_call(functools.partial(cross_kernel, tuple(parts), row_count, p...  30.9 us
    ppermute x8, starting transfers between devices, local(): lax.ppermute(x, axes, back(2, i % 2))  18 us
    ppermute x8, waiting for transfers between devices, local(): lax.ppermute(x, axes, back(2, i % 2))  10.5 us
    pallas_call x1, Pallas kernels, spectra(): pl.pallas_call(functools.partial(spectra_kernel, chunks, half), out_shape...  9.43 us
    pallas_call x1, Pallas kernels, first_spectra(): pl.pallas_call(functools.partial(first_kernel, rows, half, tuple(bounds))...  6.14 us
    ppermute x4, starting transfers between devices, local(): one_away.append(lax.ppermute(load, 'chan', swap))  5.28 us
    pallas_call x4, Pallas kernels, payload(): pl.pallas_call(payload_kernel, out_shape=jax.ShapeDtypeStruct(shape, bf16...  4.07 us
    unnamed x10, local copies, waits for them, and re-layouts  3.72 us
  transfers between devices with their start and end apart: 17, of which 4 were waited for; matrix products, arithmetic and copies ran while one was open for 0% of the time, Pallas kernels for 42%

profile of v7, /device:TPU:0, one launch (start us, length us, event | category | flops | bytes accessed | tf_op | source)
XLA Modules:
  0.0 91.8 jit_solution(11446012181869366951)
XLA Ops:
  0.0 9.4 %spectra.1 = (bf16[12,64,128]{2,1,0:T(8,128)(2,1)}, bf16[12,64,128]{2,1,0:T(8,128)(2,1)}, bf16[12,64,128]{2,1,0:T(8,128)(2,1)}, bf16[12,64,128]{2,1,0:T(8,128)(2...) custom-call(s32[1]{0:T(128)} %bitcast.me_ref, ...), custom_call_target="tpu_custom_call" | custom-call | flops 2147483648 | bytes 12582912 | tf_op jit(solution)/shard_map/spectra/pallas_call | solution.py:249
  9.4 0.6 collective-permute-start
  10.0 4.7 %collective-permute-start.10 = (bf16[12,64,128]{2,1,0:T(8,128)(2,1)}, bf16[12,64,128]{2,1,0:T(8,128)(2,1)S(1)}, u32[]{:S(2)}, u32[]{:S(2)}) collective-permute-start(bf16[12,64,128]{2,1,0:T(8,128)(2,1)} %get-tuple-element.19.keep), channel_id=1, source_target_pairs={{0,12},{1,13},{2,14},{3,15},{4,0},{5,1},{6,2},{7,3},{8,4},{9,5},{1... | collective-permute-start | bytes 589832 | tf_op jit(solution)/shard_map/ppermute | solution.py:520
  14.7 0.2 collective-permute-start.11
  14.9 6.1 %first.1 = (bf16[16,64,128]{2,1,0:T(8,128)(2,1)}, bf16[16,64,128]{2,1,0:T(8,128)(2,1)}) custom-call(s32[1]{0:T(128)} %bitcast.me_ref, f32[104,8192]{1,0:T(8,128)} %signal_hbm.3, s32[8,104]{1,0:T(8,128)} %bitcast.4, bf16[1024,1024]{1,0:T(8,128)(2,1)} %constant.24.table_hbm, f32[1,1024]{1,0:T(1,128)} %constant.20.clone.taper_ref), custom_call_target="tpu_custom_call" | custom-call | flops 1073741824 | bytes 6291456 | tf_op jit(solution)/shard_map/first/pallas_call | solution.py:158
  21.0 0.5 collective-permute-start.14
  21.5 0.0 collective-permute-start.15
  21.5 0.0 collective-permute-done.10.near_side.refs_2_
  21.6 0.4 collective-permute-start.13
  22.0 2.5 %collective-permute-done.11.far_side.refs_3_ = bf16[12,64,128]{2,1,0:T(8,128)(2,1)S(1)} collective-permute-done((bf16[12,64,128]{2,1,0:T(8,128)(2,1)}, bf16[12,64,128]{2,1,0:T(8,128)(2,1)S(1)}, u32[]{:S(2)}, u32[]{:S(2)}) %collective-permute-start.11) | collective-permute-done | bytes 196640 | tf_op jit(solution)/shard_map/ppermute | solution.py:520
  24.5 0.0 collective-permute-start.9
  24.5 6.0 %collective-permute-done.14.near_side.refs_2_ = bf16[16,64,128]{2,1,0:T(8,128)(2,1)S(1)} collective-permute-done((bf16[16,64,128]{2,1,0:T(8,128)(2,1)}, bf16[16,64,128]{2,1,0:T(8,128)(2,1)S(1)}, u32[]{:S(2)}, u32[]{:S(2)}) %collective-permute-start.14) | collective-permute-done | bytes 262176 | tf_op jit(solution)/shard_map/ppermute | solution.py:520
  30.5 3.8 %collective-permute-start.6 = (bf16[12,64,128]{2,1,0:T(8,128)(2,1)}, bf16[12,64,128]{2,1,0:T(8,128)(2,1)S(1)}, u32[]{:S(2)}, u32[]{:S(2)}) collective-permute-start(bf16[12,64,128]{2,1,0:T(8,128)(2,1)} %get-tuple-element.17.keep), channel_id=1, source_target_pairs={{0,12},{1,13},{2,14},{3,15},{4,0},{5,1},{6,2},{7,3},{8,4},{9,5},{1... | collective-permute-start | bytes 589832 | tf_op jit(solution)/shard_map/ppermute | solution.py:520
  34.3 1.4 %collective-permute-done.15.far_side.refs_3_ = bf16[16,64,128]{2,1,0:T(8,128)(2,1)S(1)} collective-permute-done((bf16[16,64,128]{2,1,0:T(8,128)(2,1)}, bf16[16,64,128]{2,1,0:T(8,128)(2,1)S(1)}, u32[]{:S(2)}, u32[]{:S(2)}) %collective-permute-start.15) | collective-permute-done | bytes 262176 | tf_op jit(solution)/shard_map/ppermute | solution.py:520
  35.7 3.6 %collective-permute-start.7 = (bf16[12,64,128]{2,1,0:T(8,128)(2,1)}, bf16[12,64,128]{2,1,0:T(8,128)(2,1)S(1)}, u32[]{:S(2)}, u32[]{:S(2)}) collective-permute-start(bf16[12,64,128]{2,1,0:T(8,128)(2,1)} %get-tuple-element.18), channel_id=1, source_target_pairs={{0,13},{1,12},{2,15},{3,14},{4,1},{5,0},{6,3},{7,2},{8,5},{9,4},{1... | collective-permute-start | bytes 589832 | tf_op jit(solution)/shard_map/ppermute | solution.py:520
  39.3 0.0 collective-permute-done.13.taken
  39.3 0.0 collective-permute-start.5
  39.3 0.9 %copy-done.1 = bf16[16,64,128]{2,1,0:T(8,128)(2,1)S(1)} copy-done((bf16[16,64,128]{2,1,0:T(8,128)(2,1)S(1)}, bf16[16,64,128]{2,1,0:T(8,128)(2,1)}, u32[]{:S(2)}) %copy-start.1) | copy-done | bytes 262168
  40.3 0.1 payload.7
  40.4 0.0 collective-permute-done.9.taken
  40.4 1.6 %collective-permute-start.16 = (bf16[2,16,64,128]{3,2,1,0:T(8,128)(2,1)S(1)}, bf16[2,16,64,128]{3,2,1,0:T(8,128)(2,1)S(1)}, u32[]{:S(2)}, u32[]{:S(2)}) collective-permute-start(bf16[2,16,64,128]{3,2,1,0:T(8,128)(2,1)S(1)} %payload.7), channel_id=1, source_target_pairs={{0,2},{2,0},{4,6},{6,4},{8,10},{10,8},{12,14},{14,12},{1,3},{3,1},... | collective-permute-start | bytes 1572872 | tf_op jit(solution)/shard_map/ppermute | solution.py:536
  42.0 0.0 collective-permute-done.6.near_side.refs_2_
  42.0 1.6 %collective-permute-start.2 = (bf16[12,64,128]{2,1,0:T(8,128)(2,1)}, bf16[12,64,128]{2,1,0:T(8,128)(2,1)S(1)}, u32[]{:S(2)}, u32[]{:S(2)}) collective-permute-start(bf16[12,64,128]{2,1,0:T(8,128)(2,1)} %get-tuple-element.15.keep), channel_id=1, source_target_pairs={{0,12},{1,13},{2,14},{3,15},{4,0},{5,1},{6,2},{7,3},{8,4},{9,5},{1... | collective-permute-start | bytes 589832 | tf_op jit(solution)/shard_map/ppermute | solution.py:520
  43.6 0.6 collective-permute-done.7.far_side.refs_3_
  44.1 3.6 %collective-permute-start.3 = (bf16[12,64,128]{2,1,0:T(8,128)(2,1)}, bf16[12,64,128]{2,1,0:T(8,128)(2,1)S(1)}, u32[]{:S(2)}, u32[]{:S(2)}) collective-permute-start(bf16[12,64,128]{2,1,0:T(8,128)(2,1)} %get-tuple-element.16), channel_id=1, source_target_pairs={{0,13},{1,12},{2,15},{3,14},{4,1},{5,0},{6,3},{7,2},{8,5},{9,4},{1... | collective-permute-start | bytes 589832 | tf_op jit(solution)/shard_map/ppermute | solution.py:520
  47.7 0.0 collective-permute-done.5.taken
  47.7 0.0 collective-permute-start.1
  47.8 0.9 %copy-done.4 = bf16[12,64,128]{2,1,0:T(8,128)(2,1)S(1)} copy-done((bf16[12,64,128]{2,1,0:T(8,128)(2,1)S(1)}, bf16[12,64,128]{2,1,0:T(8,128)(2,1)}, u32[]{:S(2)}) %copy-start.4) | copy-done | bytes 196632
  48.7 1.3 %payload.6 = bf16[2,12,64,128]{3,2,1,0:T(8,128)(2,1)} custom-call(s32[1]{0:T(128)} %bitcast.2.odd_ref, bf16[12,64,128]{2,1,0:T(8,128)(2,1)S(1)} %copy-done.4, bf16[12,64,128]{2,1,0:T(8,128)(2,1)S(1)} %collective-permute-done.9.taken, bf16[12,64,128]{2,1,0:T(8,128)(2,1)S(1)} %collective-permute-done.10.near_side.refs_2_, ...), custom_call_target="tpu_custom_call" | custom-call | bytes 2097152 | tf_op jit(solution)/shard_map/payload/pallas_call | solution.py:341
  50.0 0.9 copy-done.3
  50.9 1.2 %payload.5 = bf16[2,12,64,128]{3,2,1,0:T(8,128)(2,1)} custom-call(s32[1]{0:T(128)} %bitcast.2.odd_ref, bf16[12,64,128]{2,1,0:T(8,128)(2,1)S(1)} %copy-done.3, bf16[12,64,128]{2,1,0:T(8,128)(2,1)S(1)} %collective-permute-done.5.taken, bf16[12,64,128]{2,1,0:T(8,128)(2,1)S(1)} %collective-permute-done.6.near_side.refs_2_, ...), custom_call_target="tpu_custom_call" | custom-call | bytes 2097152 | tf_op jit(solution)/shard_map/payload/pallas_call | solution.py:341
  52.1 0.0 collective-permute-done.2.near_side.refs_2_
  52.1 1.6 %collective-permute-start.12 = (bf16[2,12,64,128]{3,2,1,0:T(8,128)(2,1)}, bf16[2,12,64,128]{3,2,1,0:T(8,128)(2,1)S(1)}, u32[]{:S(2)}, u32[]{:S(2)}) collective-permute-start(bf16[2,12,64,128]{3,2,1,0:T(8,128)(2,1)} %payload.6), channel_id=1, source_target_pairs={{0,2},{2,0},{4,6},{6,4},{8,10},{10,8},{12,14},{14,12},{1,3},{3,1},... | collective-permute-start | bytes 1179656 | tf_op jit(solution)/shard_map/ppermute | solution.py:536
  53.7 0.0 collective-permute-done.3.far_side.refs_3_
  53.7 0.5 collective-permute-start.8
  54.2 0.0 collective-permute-done.1.taken
  54.2 0.9 %copy-done.2 = bf16[12,64,128]{2,1,0:T(8,128)(2,1)S(1)} copy-done((bf16[12,64,128]{2,1,0:T(8,128)(2,1)S(1)}, bf16[12,64,128]{2,1,0:T(8,128)(2,1)}, u32[]{:S(2)}) %copy-start.2) | copy-done | bytes 196632
  55.2 1.4 %payload.4 = bf16[2,12,64,128]{3,2,1,0:T(8,128)(2,1)} custom-call(s32[1]{0:T(128)} %bitcast.2.odd_ref, bf16[12,64,128]{2,1,0:T(8,128)(2,1)S(1)} %copy-done.2, bf16[12,64,128]{2,1,0:T(8,128)(2,1)S(1)} %collective-permute-done.1.taken, bf16[12,64,128]{2,1,0:T(8,128)(2,1)S(1)} %collective-permute-done.2.near_side.refs_2_, ...), custom_call_target="tpu_custom_call" | custom-call | bytes 2097152 | tf_op jit(solution)/shard_map/payload/pallas_call | solution.py:341
  56.6 1.6 %collective-permute-start.4 = (bf16[2,12,64,128]{3,2,1,0:T(8,128)(2,1)}, bf16[2,12,64,128]{3,2,1,0:T(8,128)(2,1)S(1)}, u32[]{:S(2)}, u32[]{:S(2)}) collective-permute-start(bf16[2,12,64,128]{3,2,1,0:T(8,128)(2,1)} %payload.4), channel_id=1, source_target_pairs={{0,2},{2,0},{4,6},{6,4},{8,10},{10,8},{12,14},{14,12},{1,3},{3,1},... | collective-permute-start | bytes 1179656 | tf_op jit(solution)/shard_map/ppermute | solution.py:536
  58.2 0.0 collective-permute-done.far_hbm
  58.2 2.4 %join.1.refs_0_ = bf16[64,256,256]{2,1,0:T(8,128)(2,1)S(1)} custom-call(bf16[64,128,128]{2,1,0:T(8,128)(2,1)} %get-tuple-element.14.near_hbm, bf16[64,128,128]{2,1,0:T(8,128)(2,1)} %collective-permute-done.far_hbm), custom_call_target="tpu_custom_call" | custom-call | bytes 13631488 | tf_op jit(solution)/shard_map/join/pallas_call | solution.py:306
  60.7 4.7 %cross.5.refs_5_ = bf16[2,52,104,512]{3,2,1,0:T(8,128)(2,1)} custom-call(bf16[64,256,256]{2,1,0:T(8,128)(2,1)S(1)} %join.1.refs_0_, bf16[2,256,512]{2,1,0:T(8,128)(2,1)S(1)} %copy-done, bf16[16,64,128]{2,1,0:T(8,128)(2,1)S(1)} %collective-permute-done.14.near_side.refs_2_, bf16[16,64,128]{2,1,0:T(8,128)(2,1)S(1)} %collective-permute-done.15.far_side.refs_3_), custom_call_target="tpu_custom_call" | custom-call | flops 2400000000 | bytes 12582912 | tf_op jit(solution)/shard_map/cross/pallas_call | solution.py:465
  65.4 7.2 %cross.6.refs_5_ = bf16[2,52,104,512]{3,2,1,0:T(8,128)(2,1)} custom-call(bf16[64,256,256]{2,1,0:T(8,128)(2,1)S(1)} %join.1.refs_0_, bf16[2,256,512]{2,1,0:T(8,128)(2,1)S(1)} %copy-done, bf16[12,64,128]{2,1,0:T(8,128)(2,1)S(1)} %collective-permute-done.10.near_side.refs_2_, ...), custom_call_target="tpu_custom_call", output_to_operand_aliasing={{}: (5, {})} | custom-call | flops 4200000000 | bytes 12582912 | tf_op jit(solution)/shard_map/cross/pallas_call | solution.py:465
  72.6 0.0 collective-permute-done.12.refs_4_
  72.6 7.0 %cross.7.refs_5_ = bf16[2,52,104,512]{3,2,1,0:T(8,128)(2,1)} custom-call(bf16[64,256,256]{2,1,0:T(8,128)(2,1)S(1)} %join.1.refs_0_, bf16[2,256,512]{2,1,0:T(8,128)(2,1)S(1)} %copy-done, bf16[12,64,128]{2,1,0:T(8,128)(2,1)S(1)} %collective-permute-done.6.near_side.refs_2_, ...), custom_call_target="tpu_custom_call", output_to_operand_aliasing={{}: (5, {})} | custom-call | flops 3600000000 | bytes 12582912 | tf_op jit(solution)/shard_map/cross/pallas_call | solution.py:465
  79.7 7.3 %cross.8.refs_3_ = bf16[2,52,104,512]{3,2,1,0:T(8,128)(2,1)} custom-call(bf16[64,256,256]{2,1,0:T(8,128)(2,1)S(1)} %join.1.refs_0_, bf16[2,256,512]{2,1,0:T(8,128)(2,1)S(1)} %copy-done, bf16[12,64,128]{2,1,0:T(8,128)(2,1)S(1)} %collective-permute-done.2.near_side.refs_2_, ...), custom_call_target="tpu_custom_call", output_to_operand_aliasing={{}: (5, {})} | custom-call | flops 3600000000 | bytes 12582912 | tf_op jit(solution)/shard_map/cross/pallas_call | solution.py:465
  87.0 0.0 collective-permute-done.4.refs_2_
  87.0 4.7 %cross.9 = bf16[2,52,104,512]{3,2,1,0:T(8,128)(2,1)} custom-call(bf16[64,256,256]{2,1,0:T(8,128)(2,1)S(1)} %join.1.refs_0_, bf16[2,256,512]{2,1,0:T(8,128)(2,1)S(1)} %copy-done, bf16[2,12,64,128]{3,2,1,0:T(8,128)(2,1)S(1)} %collective-permute-done.4.refs_2_, bf16[2,52,104,512]{3,2,1,0:T(8,128)(2,1)} %cross.8.refs_3_), custom_call_target="tpu_custom_call", output_to_operand_aliasing={{}: (3, {})} | custom-call | flops 1800000000 | bytes 12582912 | tf_op jit(solution)/shard_map/cross/pallas_call | solution.py:465
  (8 shorter events, 0.0 us)
Async XLA Ops:
  9.4 48.8 %collective-permute-start = (bf16[64,128,128]{2,1,0:T(8,128)(2,1)}, bf16[64,128,128]{2,1,0:T(8,128)(2,1)}, u32[]{:S(2)}, u32[]{:S(2)}) collective-permute-start(bf16[64,128,128]{2,1,0:T(8,128)(2,1)} %get-tuple-element.14.near_hbm), channel_id=1, source_target_pairs={{0,1},{1,0},{2,3},{3,2},{4,5},{5,4},{6,7},{7,6},{8,9},{9,8},{10,11... | collective-permute-start | bytes 6291464 | tf_op jit(solution)/shard_map/ppermute | solution.py:523
  10.0 11.6 %collective-permute-start.10 = (bf16[12,64,128]{2,1,0:T(8,128)(2,1)}, bf16[12,64,128]{2,1,0:T(8,128)(2,1)S(1)}, u32[]{:S(2)}, u32[]{:S(2)}) collective-permute-start(bf16[12,64,128]{2,1,0:T(8,128)(2,1)} %get-tuple-element.19.keep), channel_id=1, source_target_pairs={{0,12},{1,13},{2,14},{3,15},{4,0},{5,1},{6,2},{7,3},{8,4},{9,5},{1... | collective-permute-start | bytes 589832 | tf_op jit(solution)/shard_map/ppermute | solution.py:520
  14.7 46.0 %copy-start = (bf16[2,256,512]{2,1,0:T(8,128)(2,1)S(1)}, bf16[2,256,512]{2,1,0:T(8,128)(2,1)}, u32[]{:S(2)}) copy-start(bf16[2,256,512]{2,1,0:T(8,128)(2,1)} %constant.25.refs_1_) | copy-start | bytes 1572868
  14.7 9.8 %collective-permute-start.11 = (bf16[12,64,128]{2,1,0:T(8,128)(2,1)}, bf16[12,64,128]{2,1,0:T(8,128)(2,1)S(1)}, u32[]{:S(2)}, u32[]{:S(2)}) collective-permute-start(bf16[12,64,128]{2,1,0:T(8,128)(2,1)} %get-tuple-element.20), channel_id=1, source_target_pairs={{0,13},{1,12},{2,15},{3,14},{4,1},{5,0},{6,3},{7,2},{8,5},{9,4},{1... | collective-permute-start | bytes 589832 | tf_op jit(solution)/shard_map/ppermute | solution.py:520
  21.0 9.4 %collective-permute-start.14 = (bf16[16,64,128]{2,1,0:T(8,128)(2,1)}, bf16[16,64,128]{2,1,0:T(8,128)(2,1)S(1)}, u32[]{:S(2)}, u32[]{:S(2)}) collective-permute-start(bf16[16,64,128]{2,1,0:T(8,128)(2,1)} %get-tuple-element.21.keep), channel_id=1, source_target_pairs={{0,12},{1,13},{2,14},{3,15},{4,0},{5,1},{6,2},{7,3},{8,4},{9,5},{1... | collective-permute-start | bytes 786440 | tf_op jit(solution)/shard_map/ppermute | solution.py:520
  21.5 14.2 %collective-permute-start.15 = (bf16[16,64,128]{2,1,0:T(8,128)(2,1)}, bf16[16,64,128]{2,1,0:T(8,128)(2,1)S(1)}, u32[]{:S(2)}, u32[]{:S(2)}) collective-permute-start(bf16[16,64,128]{2,1,0:T(8,128)(2,1)} %get-tuple-element.22), channel_id=1, source_target_pairs={{0,13},{1,12},{2,15},{3,14},{4,1},{5,0},{6,3},{7,2},{8,5},{9,4},{1... | collective-permute-start | bytes 786440 | tf_op jit(solution)/shard_map/ppermute | solution.py:520
  21.6 17.8 %collective-permute-start.13 = (bf16[16,64,128]{2,1,0:T(8,128)(2,1)}, bf16[16,64,128]{2,1,0:T(8,128)(2,1)S(1)}, u32[]{:S(2)}, u32[]{:S(2)}) collective-permute-start(bf16[16,64,128]{2,1,0:T(8,128)(2,1)} %get-tuple-element.22), channel_id=1, source_target_pairs={{0,1},{1,0},{2,3},{3,2},{4,5},{5,4},{6,7},{7,6},{8,9},{9,8},{10,11... | collective-permute-start | bytes 786440 | tf_op jit(solution)/shard_map/ppermute | solution.py:522
  24.5 15.9 %collective-permute-start.9 = (bf16[12,64,128]{2,1,0:T(8,128)(2,1)}, bf16[12,64,128]{2,1,0:T(8,128)(2,1)S(1)}, u32[]{:S(2)}, u32[]{:S(2)}) collective-permute-start(bf16[12,64,128]{2,1,0:T(8,128)(2,1)} %get-tuple-element.20), channel_id=1, source_target_pairs={{0,1},{1,0},{2,3},{3,2},{4,5},{5,4},{6,7},{7,6},{8,9},{9,8},{10,11... | collective-permute-start | bytes 589832 | tf_op jit(solution)/shard_map/ppermute | solution.py:522
  30.5 11.5 %collective-permute-start.6 = (bf16[12,64,128]{2,1,0:T(8,128)(2,1)}, bf16[12,64,128]{2,1,0:T(8,128)(2,1)S(1)}, u32[]{:S(2)}, u32[]{:S(2)}) collective-permute-start(bf16[12,64,128]{2,1,0:T(8,128)(2,1)} %get-tuple-element.17.keep), channel_id=1, source_target_pairs={{0,12},{1,13},{2,14},{3,15},{4,0},{5,1},{6,2},{7,3},{8,4},{9,5},{1... | collective-permute-start | bytes 589832 | tf_op jit(solution)/shard_map/ppermute | solution.py:520
  35.7 8.4 %collective-permute-start.7 = (bf16[12,64,128]{2,1,0:T(8,128)(2,1)}, bf16[12,64,128]{2,1,0:T(8,128)(2,1)S(1)}, u32[]{:S(2)}, u32[]{:S(2)}) collective-permute-start(bf16[12,64,128]{2,1,0:T(8,128)(2,1)} %get-tuple-element.18), channel_id=1, source_target_pairs={{0,13},{1,12},{2,15},{3,14},{4,1},{5,0},{6,3},{7,2},{8,5},{9,4},{1... | collective-permute-start | bytes 589832 | tf_op jit(solution)/shard_map/ppermute | solution.py:520
  39.3 8.4 %collective-permute-start.5 = (bf16[12,64,128]{2,1,0:T(8,128)(2,1)}, bf16[12,64,128]{2,1,0:T(8,128)(2,1)S(1)}, u32[]{:S(2)}, u32[]{:S(2)}) collective-permute-start(bf16[12,64,128]{2,1,0:T(8,128)(2,1)} %get-tuple-element.18), channel_id=1, source_target_pairs={{0,1},{1,0},{2,3},{3,2},{4,5},{5,4},{6,7},{7,6},{8,9},{9,8},{10,11... | collective-permute-start | bytes 589832 | tf_op jit(solution)/shard_map/ppermute | solution.py:522
  39.3 1.0 %copy-start.1 = (bf16[16,64,128]{2,1,0:T(8,128)(2,1)S(1)}, bf16[16,64,128]{2,1,0:T(8,128)(2,1)}, u32[]{:S(2)}) copy-start(bf16[16,64,128]{2,1,0:T(8,128)(2,1)} %get-tuple-element.21.keep) | copy-start | bytes 786436
  40.4 25.0 %collective-permute-start.16 = (bf16[2,16,64,128]{3,2,1,0:T(8,128)(2,1)S(1)}, bf16[2,16,64,128]{3,2,1,0:T(8,128)(2,1)S(1)}, u32[]{:S(2)}, u32[]{:S(2)}) collective-permute-start(bf16[2,16,64,128]{3,2,1,0:T(8,128)(2,1)S(1)} %payload.7), channel_id=1, source_target_pairs={{0,2},{2,0},{4,6},{6,4},{8,10},{10,8},{12,14},{14,12},{1,3},{3,1},... | collective-permute-start | bytes 1572872 | tf_op jit(solution)/shard_map/ppermute | solution.py:536
  42.0 10.1 %collective-permute-start.2 = (bf16[12,64,128]{2,1,0:T(8,128)(2,1)}, bf16[12,64,128]{2,1,0:T(8,128)(2,1)S(1)}, u32[]{:S(2)}, u32[]{:S(2)}) collective-permute-start(bf16[12,64,128]{2,1,0:T(8,128)(2,1)} %get-tuple-element.15.keep), channel_id=1, source_target_pairs={{0,12},{1,13},{2,14},{3,15},{4,0},{5,1},{6,2},{7,3},{8,4},{9,5},{1... | collective-permute-start | bytes 589832 | tf_op jit(solution)/shard_map/ppermute | solution.py:520
  44.1 9.6 %collective-permute-start.3 = (bf16[12,64,128]{2,1,0:T(8,128)(2,1)}, bf16[12,64,128]{2,1,0:T(8,128)(2,1)S(1)}, u32[]{:S(2)}, u32[]{:S(2)}) collective-permute-start(bf16[12,64,128]{2,1,0:T(8,128)(2,1)} %get-tuple-element.16), channel_id=1, source_target_pairs={{0,13},{1,12},{2,15},{3,14},{4,1},{5,0},{6,3},{7,2},{8,5},{9,4},{1... | collective-permute-start | bytes 589832 | tf_op jit(solution)/shard_map/ppermute | solution.py:520
  47.7 6.5 %collective-permute-start.1 = (bf16[12,64,128]{2,1,0:T(8,128)(2,1)}, bf16[12,64,128]{2,1,0:T(8,128)(2,1)S(1)}, u32[]{:S(2)}, u32[]{:S(2)}) collective-permute-start(bf16[12,64,128]{2,1,0:T(8,128)(2,1)} %get-tuple-element.16), channel_id=1, source_target_pairs={{0,1},{1,0},{2,3},{3,2},{4,5},{5,4},{6,7},{7,6},{8,9},{9,8},{10,11... | collective-permute-start | bytes 589832 | tf_op jit(solution)/shard_map/ppermute | solution.py:522
  47.7 0.9 %copy-start.4 = (bf16[12,64,128]{2,1,0:T(8,128)(2,1)S(1)}, bf16[12,64,128]{2,1,0:T(8,128)(2,1)}, u32[]{:S(2)}) copy-start(bf16[12,64,128]{2,1,0:T(8,128)(2,1)} %get-tuple-element.19.keep) | copy-start | bytes 589828
  50.0 0.9 %copy-start.3 = (bf16[12,64,128]{2,1,0:T(8,128)(2,1)S(1)}, bf16[12,64,128]{2,1,0:T(8,128)(2,1)}, u32[]{:S(2)}) copy-start(bf16[12,64,128]{2,1,0:T(8,128)(2,1)} %get-tuple-element.17.keep) | copy-start | bytes 589828
  52.1 20.5 %collective-permute-start.12 = (bf16[2,12,64,128]{3,2,1,0:T(8,128)(2,1)}, bf16[2,12,64,128]{3,2,1,0:T(8,128)(2,1)S(1)}, u32[]{:S(2)}, u32[]{:S(2)}) collective-permute-start(bf16[2,12,64,128]{3,2,1,0:T(8,128)(2,1)} %payload.6), channel_id=1, source_target_pairs={{0,2},{2,0},{4,6},{6,4},{8,10},{10,8},{12,14},{14,12},{1,3},{3,1},... | collective-permute-start | bytes 1179656 | tf_op jit(solution)/shard_map/ppermute | solution.py:536
  53.7 25.9 %collective-permute-start.8 = (bf16[2,12,64,128]{3,2,1,0:T(8,128)(2,1)}, bf16[2,12,64,128]{3,2,1,0:T(8,128)(2,1)S(1)}, u32[]{:S(2)}, u32[]{:S(2)}) collective-permute-start(bf16[2,12,64,128]{3,2,1,0:T(8,128)(2,1)} %payload.5), channel_id=1, source_target_pairs={{0,2},{2,0},{4,6},{6,4},{8,10},{10,8},{12,14},{14,12},{1,3},{3,1},... | collective-permute-start | bytes 1179656 | tf_op jit(solution)/shard_map/ppermute | solution.py:536
  54.2 0.9 %copy-start.2 = (bf16[12,64,128]{2,1,0:T(8,128)(2,1)S(1)}, bf16[12,64,128]{2,1,0:T(8,128)(2,1)}, u32[]{:S(2)}) copy-start(bf16[12,64,128]{2,1,0:T(8,128)(2,1)} %get-tuple-element.15.keep) | copy-start | bytes 589828
  56.6 30.3 %collective-permute-start.4 = (bf16[2,12,64,128]{3,2,1,0:T(8,128)(2,1)}, bf16[2,12,64,128]{3,2,1,0:T(8,128)(2,1)S(1)}, u32[]{:S(2)}, u32[]{:S(2)}) collective-permute-start(bf16[2,12,64,128]{3,2,1,0:T(8,128)(2,1)} %payload.4), channel_id=1, source_target_pairs={{0,2},{2,0},{4,6},{6,4},{8,10},{10,8},{12,14},{14,12},{1,3},{3,1},... | collective-permute-start | bytes 1179656 | tf_op jit(solution)/shard_map/ppermute | solution.py:536
